TPU v7x, 32 devices: a whole 2x2x4 slice. The times are simulated.
32 devices in a mesh: groups: 2 (over x), ctx: 16 (over z, y, core).
Axes of the slice: x: 2, y: 2, z: 4, core: 2. Of those that a mesh axis runs over, the one named last changes fastest.
Arguments:
- queries: bfloat16 [8192, 3072], P(('groups', 'ctx')), parts along dimension 0, may hold values from -60 to 60
- key_states: bfloat16 [8192, 3072], P(('groups', 'ctx')), parts along dimension 0, may hold values from -6 to 6
- value_states: bfloat16 [8192, 3072], P(('groups', 'ctx')), parts along dimension 0, may hold values from -6 to 6
- stretch_lengths: int32 [32], P('groups'), parts along dimension 0, may hold values from 1 to 512, 4096 in all
- stretch_mask: int32 [32, 16], P('groups'), parts along dimension 0, may hold values from 0 to 1, as said below
Outputs:
- attended: bfloat16 [8192, 3072], P(('groups', 'ctx')), parts along dimension 0
There are 2 independent parts, one for each index of `groups`. A program takes and returns all parts, laid end to end along the dimension named above; each array names one. Nothing has to cross between parts.
Inputs may be any that keep to these rules, and one draw needn't show every extreme that they name: `stretch_lengths`: every stretch holds 1 to 512 tokens, at least one exactly 512; together 4096. stretch_mask[a, b] is 1 where b = a and 0 where b > a or b < a - 1.
All inputs are finite; a program needn't handle non-finite values.
Results may differ from a plain program's by a relative error of at most 0.0035.
Values may be sent and summed in bfloat16 or wider, within the bound.
No kernel may reach another device: no remote copies, remote signals or barrier semaphores. Data moves between devices by JAX's collectives and lax.ppermute only.
A program may use at most 192 MiB of HBM per device.

v0:
```python
import math

import jax
import jax.numpy as jnp
from jax import lax
from jax.experimental import pallas as pl
from jax.experimental.pallas import tpu as pltpu
from jax.sharding import PartitionSpec as P


HEAD = 128
MAXLEN = 512
WIN = 1
LEVEL = 4
SPLIT = (2, 2, 2)
OTHERS = tuple(range(1, LEVEL))
NEG = -1e30
TILE = 256
HBM = pl.BlockSpec(memory_space=pltpu.HBM)
VMEM = pl.BlockSpec(memory_space=pltpu.VMEM)
SMEM = pl.BlockSpec(memory_space=pltpu.SMEM)


def swap(value, bits):
    return lax.ppermute(value, "ctx", [(i, i ^ bits) for i in range(lax.axis_size("ctx"))])


def swap_levels(value, parity):
    count = lax.axis_size("ctx")
    pairs = []
    for low in range(parity * LEVEL, count - LEVEL, 2 * LEVEL):
        for i in range(low, low + LEVEL):
            pairs += [(i, i + LEVEL), (i + LEVEL, i)]
    return lax.ppermute(value, "ctx", pairs)


def run_copies(pairs, sems):
    copies = [pltpu.make_async_copy(a, b, sems.at[n]) for n, (a, b) in enumerate(pairs)]
    for c in copies:
        c.start()
    for c in copies:
        c.wait()


def cost(nbytes, flops=0):
    return pl.CostEstimate(flops=flops, bytes_accessed=nbytes, transcendentals=0)


def pack_columns(arrays, jobs):
    rows = arrays[0].shape[0]
    totals = [sum(span[3] for span in spans) for _, spans in jobs]

    def kernel(*refs):
        ins, outs, sems = refs[: len(arrays)], refs[len(arrays) : -1], refs[-1]
        j = lax.rem(lax.axis_index("ctx"), LEVEL)
        pairs = []
        for out, (d, spans) in zip(outs, jobs):
            to = 0
            for which, unit, offset, width in spans:
                c = pl.multiple_of((j ^ d) * unit + offset, 128)
                pairs.append((ins[which].at[:, pl.ds(c, width)], out.at[:, pl.ds(to, width)]))
                to += width
        run_copies(pairs, sems)

    return pl.pallas_call(
        kernel,
        out_shape=[jax.ShapeDtypeStruct((rows, total), arrays[0].dtype) for total in totals],
        in_specs=[HBM] * len(arrays),
        out_specs=[VMEM] * len(jobs),
        scratch_shapes=[pltpu.SemaphoreType.DMA((sum(len(spans) for _, spans in jobs),))],
        cost_estimate=cost(4 * rows * sum(totals)),
    )(*arrays)


def pack_z(own, swapped, ahead, offset, width):
    rows = own.shape[0]
    n_fwd = LEVEL - 1

    def kernel(o, *rest):
        outs, sems = rest[LEVEL - 1 : -1], rest[-1]
        pieces = [o.at[:, pl.ds(offset, 2 * width)]]
        pieces += [ref.at[:, pl.ds(0, 2 * width)] for ref in rest[: LEVEL - 1]]
        me = lax.axis_index("ctx")
        j = lax.rem(me, LEVEL)
        odd = lax.rem(me // LEVEL, 2)
        for parity in range(2):
            fwd, back = outs[parity], outs[1 - parity]

            @pl.when(odd == parity)
            def _():
                for d in range(1, LEVEL):
                    pltpu.make_async_copy(pieces[d], fwd.at[d - 1], sems.at[d - 1]).start()
                for b in range(ahead):
                    for d in range(LEVEL):
                        @pl.when((j ^ b) == d)
                        def _():
                            pltpu.make_async_copy(
                                pieces[d], back.at[b], sems.at[n_fwd + b]
                            ).start()
        for n in range(n_fwd + ahead):
            pltpu.make_async_copy(pieces[0], outs[0].at[0], sems.at[n]).wait()

    return pl.pallas_call(
        kernel,
        out_shape=[jax.ShapeDtypeStruct((n_fwd, rows, 2 * width), own.dtype)] * 2,
        in_specs=[HBM] * LEVEL,
        out_specs=[VMEM, VMEM],
        scratch_shapes=[pltpu.SemaphoreType.DMA((n_fwd + ahead,))],
        cost_estimate=cost(8 * rows * width * (n_fwd + ahead)),
        name="pack_z",
    )(own, *swapped)


def lookup_tables(lengths, mask, rows, key_blocks):
    stretches = lengths.shape[0]
    lanes = -(-stretches // HEAD) * HEAD
    key_rows, query_rows = key_blocks * rows, LEVEL * rows

    def kernel(len_ref, mask_ref, bias, onehot, ranges):
        base = (lax.axis_index("ctx") // LEVEL - 1) * query_rows
        lane = lax.broadcasted_iota(jnp.int32, (1, lanes), 1)
        for b in range(LEVEL):
            ranges[b, 0] = jnp.int32(0)
            ranges[b, 1] = jnp.int32(0)

        def scan(a, carry):
            start, before, own, lo, hi = carry
            length = len_ref[a]
            back = jnp.where(mask_ref[a, jnp.maximum(a - 1, 0)] > 0, before, 0)
            end = start + length
            here = lane == a
            for b in range(LEVEL):
                first = (LEVEL + b) * rows
                ranges[b, 0] = jnp.where(start <= first, start - back, ranges[b, 0])
                ranges[b, 1] = jnp.where(start < first + rows, end, ranges[b, 1])
            return (
                end,
                length,
                jnp.where(here, start, own),
                jnp.where(here, start - back, lo),
                jnp.where(here, end, hi),
            )

        zero = jnp.full((1, lanes), -(1 << 30), jnp.int32)
        _, _, own, lo, hi = lax.fori_loop(
            0, stretches, scan, (-base, jnp.int32(0), zero, zero, zero)
        )
        for b in range(LEVEL):
            start = jnp.maximum(ranges[b, 0], 0) // HEAD * HEAD
            tiles = (ranges[b, 1] - start + TILE - 1) // TILE
            ranges[b, 0] = jnp.minimum(start, key_rows - tiles * TILE)
            ranges[b, 1] = tiles

        @pl.loop(0, key_blocks)
        def _(i):
            at = pl.ds(pl.multiple_of(i * rows, rows), rows)
            pos = lax.broadcasted_iota(jnp.int32, (rows, lanes), 0) + i * rows
            inside = (pos >= lo) & (pos < hi)
            bias[at, :] = jnp.where(inside, 0.0, NEG).astype(bias.dtype)

        @pl.loop(0, LEVEL)
        def _(i):
            at = pl.ds(pl.multiple_of(i * rows, rows), rows)
            pos = lax.broadcasted_iota(jnp.int32, (rows, lanes), 0) + (LEVEL + i) * rows
            onehot[at, :] = jnp.where((pos >= own) & (pos < hi), 1.0, 0.0).astype(onehot.dtype)

    bf = jnp.bfloat16
    return pl.pallas_call(
        kernel,
        out_shape=[
            jax.ShapeDtypeStruct((key_rows, lanes), bf),
            jax.ShapeDtypeStruct((query_rows, lanes), bf),
            jax.ShapeDtypeStruct((LEVEL, 2), jnp.int32),
        ],
        in_specs=[SMEM, SMEM],
        out_specs=[VMEM, VMEM, SMEM],
        cost_estimate=cost(2 * (key_rows + query_rows) * lanes),
        name="lookup_tables",
    )(lengths, mask)


def attention(tables, queries, own, swapped, own_far, far, ahead, offset, width, slab):
    rows = queries.shape[0]
    heads = width // HEAD
    key_blocks = 2 * LEVEL + ahead
    key_rows = key_blocks * rows
    lanes = tables[0].shape[1]
    factor = math.log2(math.e) / math.sqrt(HEAD)
    n_copies = 2 + 2 * key_blocks + LEVEL

    def kernel(ranges, bias_hbm, onehot_hbm, q, *rest):
        level, rest = rest[:LEVEL], rest[LEVEL:]
        own_sides, sides, rest = rest[:2], rest[2:4], rest[4:]
        outs, scratch = rest[:LEVEL], rest[LEVEL:]
        ks, vs, vt, qs, os, acc, bias, onehot, sems, out_sems = scratch
        me = lax.axis_index("ctx")
        j = lax.rem(me, LEVEL)
        odd = lax.rem(me // LEVEL, 2)

        def kv(src, block, off=0):
            at = pl.ds(pl.multiple_of(block * rows, rows), rows)
            return [
                (src.at[:, pl.ds(off, width)], ks.at[at, :]),
                (src.at[:, pl.ds(off + width, width)], vs.at[at, :]),
            ]

        pairs = [(bias_hbm, bias), (onehot_hbm, onehot)]
        for d in range(LEVEL):
            pairs += kv(level[d], LEVEL + (j ^ d), 2 * offset if d == 0 else 0)
            at = pl.ds(pl.multiple_of((j ^ d) * rows, rows), rows)
            if d == 0:
                c = pl.multiple_of(j * slab + offset, HEAD)
                pairs.append((q.at[:, pl.ds(c, width)], qs.at[at, :]))
            else:
                pairs.append((level[d].at[:, pl.ds(2 * width, width)], qs.at[at, :]))
        near = len(pairs)

        def side_pairs(parity):
            behind, front = 1 - parity, parity
            out = kv(own_sides[behind], j, 2 * offset)
            for d in range(1, LEVEL):
                out += kv(sides[behind].at[d - 1], j ^ d)
            for b in range(ahead):
                out += kv(sides[front].at[b], 2 * LEVEL + b)
            return out

        copies = [pltpu.make_async_copy(a, b, sems.at[n]) for n, (a, b) in enumerate(pairs)]
        for c in copies:
            c.start()
        for parity in range(2):
            @pl.when(odd == parity)
            def _():
                for n, (a, b) in enumerate(side_pairs(parity)):
                    pltpu.make_async_copy(a, b, sems.at[near + n]).start()
        copies += [
            pltpu.make_async_copy(a, b, sems.at[near + n])
            for n, (a, b) in enumerate(side_pairs(0))
        ]
        for c in copies:
            c.wait()
        for h in range(heads):
            vt[h, HEAD:, :] = jnp.ones_like(vt[h, HEAD:, :])

        @pl.loop(0, key_rows // TILE)
        def _(i):
            at = pl.ds(pl.multiple_of(i * TILE, TILE), TILE)
            for h in range(heads):
                vt[h, :HEAD, at] = vs[at, h * HEAD : (h + 1) * HEAD].T

        @pl.loop(0, LEVEL)
        def _(b):
            at = pl.ds(pl.multiple_of(b * rows, rows), rows)
            start, tiles = ranges[b, 0], ranges[b, 1]
            for h in range(heads):
                acc[h] = jnp.zeros_like(acc[h])
            q_ext = [
                jnp.concatenate([qs[at, h * HEAD : (h + 1) * HEAD], onehot[at, :]], axis=1)
                for h in range(heads)
            ]

            def step(t, tops):
                k_at = pl.ds(pl.multiple_of(start + t * TILE, HEAD), TILE)
                scores = [
                    lax.dot_general(
                        jnp.concatenate(
                            [ks[k_at, h * HEAD : (h + 1) * HEAD], bias[k_at, :]], axis=1
                        ),
                        q_ext[h],
                        (((1,), (1,)), ((), ())),
                        preferred_element_type=jnp.float32,
                    )
                    for h in range(heads)
                ]
                new = []
                for h in range(heads):
                    s, top = scores[h], tops[h]
                    top_new = jnp.maximum(top, jnp.max(s, axis=0, keepdims=True))
                    p = jnp.exp2((s - top_new) * factor).astype(jnp.bfloat16)
                    alpha = jnp.exp2((top - top_new) * factor)
                    acc[h] = acc[h] * alpha + jnp.dot(
                        vt[h, :, k_at], p, preferred_element_type=jnp.float32
                    )
                    new.append(top_new)
                return tuple(new)

            low = jnp.full((1, rows), 2 * NEG, jnp.float32)
            lax.fori_loop(0, tiles, step, (low,) * heads)
            for h in range(heads):
                normed = acc[h, :HEAD, :] / acc[h, HEAD : HEAD + 1, :]
                os[at, h * HEAD : (h + 1) * HEAD] = normed.T.astype(jnp.bfloat16)

        run_copies(
            [
                (os.at[pl.ds(pl.multiple_of((j ^ d) * rows, rows), rows), :], outs[d])
                for d in range(LEVEL)
            ],
            out_sems,
        )

    bf = jnp.bfloat16
    bias, onehot, ranges = tables
    return pl.pallas_call(
        kernel,
        out_shape=[jax.ShapeDtypeStruct((rows, width), bf)] * LEVEL,
        in_specs=[SMEM] + [HBM] * (LEVEL + 7),
        out_specs=[HBM] * LEVEL,
        scratch_shapes=[
            pltpu.VMEM((key_rows, width), bf),
            pltpu.VMEM((key_rows, width), bf),
            pltpu.VMEM((heads, HEAD + 16, key_rows), bf),
            pltpu.VMEM((LEVEL * rows, width), bf),
            pltpu.VMEM((LEVEL * rows, width), bf),
            pltpu.VMEM((heads, HEAD + 16, rows), jnp.float32),
            pltpu.VMEM((key_rows, lanes), bf),
            pltpu.VMEM((LEVEL * rows, lanes), bf),
            pltpu.SemaphoreType.DMA((n_copies,)),
            pltpu.SemaphoreType.DMA((LEVEL,)),
        ],
        cost_estimate=cost(4 * key_rows * width, 8 * LEVEL * rows * 1024 * width),
        name="attention",
    )(ranges, bias, onehot, queries, own, *swapped, *own_far, *far)


def gather_out(pieces, rows, slab, dtype):
    def kernel(*refs):
        ins, out, sems = refs[:-2], refs[-2], refs[-1]
        j = lax.rem(lax.axis_index("ctx"), LEVEL)
        pairs, offset = [], 0
        for g, heads in enumerate(SPLIT):
            width = heads * HEAD
            for d in range(LEVEL):
                c = pl.multiple_of((j ^ d) * slab + offset, HEAD)
                pairs.append((ins[g * LEVEL + d], out.at[:, pl.ds(c, width)]))
            offset += width
        run_copies(pairs, sems)

    return pl.pallas_call(
        kernel,
        out_shape=jax.ShapeDtypeStruct((rows, LEVEL * slab), dtype),
        in_specs=[HBM] * len(pieces),
        out_specs=VMEM,
        scratch_shapes=[pltpu.SemaphoreType.DMA((len(pieces),))],
        cost_estimate=cost(4 * rows * LEVEL * slab),
        name="gather_out",
    )(*pieces)


def attend(queries, key_states, value_states, stretch_lengths, stretch_mask):
    rows, features = queries.shape
    slab = features // LEVEL
    ahead = (MAXLEN - 2) // rows + 1
    assert LEVEL * rows >= (WIN + 1) * MAXLEN - 1 and ahead < LEVEL
    assert sum(SPLIT) * HEAD == slab
    widths = [heads * HEAD for heads in SPLIT]
    offsets = [sum(widths[:g]) for g in range(len(widths))]
    groups = range(len(SPLIT))
    arrays = (key_states, value_states, queries)
    tables = lookup_tables(stretch_lengths, stretch_mask, rows, 2 * LEVEL + ahead)
    slabs = [[(i, slab, offsets[g], widths[g]) for i in range(3)] for g in groups]
    own_spans = [span for spans in slabs for span in spans[:2]]
    jobs = [(d, slabs[0]) for d in OTHERS] + [(0, own_spans)]
    *parts, own = pack_columns(arrays, jobs)
    jobs = [(d, slabs[g]) for g in groups[1:] for d in OTHERS]
    parts += pack_columns(arrays, jobs)
    swapped, far = [], []
    for g in groups:
        mine = parts[g * len(OTHERS) : (g + 1) * len(OTHERS)]
        swapped.append([swap(x, d) for x, d in zip(mine, OTHERS)])
    own_far = [swap_levels(own, p) for p in range(2)]
    for g in groups:
        sides = pack_z(own, swapped[g], ahead, 2 * offsets[g], widths[g])
        far.append([swap_levels(x, p) for p, x in enumerate(sides)])
    pieces = []
    for g in groups:
        outs = attention(
            tables, queries, own, swapped[g], own_far, far[g], ahead,
            offsets[g], widths[g], slab,
        )
        pieces += [outs[0]]
        pieces += [swap(outs[d], d) for d in OTHERS]
    return gather_out(pieces, rows, slab, queries.dtype)


def solution(mesh):
    rows = P(("groups", "ctx"), None)
    in_specs = (rows, rows, rows, P("groups"), P("groups", None))
    return jax.shard_map(attend, mesh=mesh, in_specs=in_specs, out_specs=rows, check_vma=False)
```

profile of v0, /device:TPU:19, one launch (start us, length us, event | category | flops | bytes accessed | tf_op | source)
XLA Modules:
  0.0 137.7 jit_solution(17505839391861491079)
XLA Ops:
  0.0 3.0 %shard_map.55 = (bf16[256,768]{1,0:T(8,128)(2,1)}, bf16[256,768]{1,0:T(8,128)(2,1)}, bf16[256,768]{1,0:T(8,128)(2,1)}, bf16[256,1536]{1,0:T(8,128)(2,1)}) custom-call(bf16[256,3072]{1,0:T(8,128)(2,1)} %refs_0_.3, bf16[256,3072]{1,0:T(8,128)(2,1)} %refs_1_.3, bf16[256,3072]{1,0:T(8,128)(2,1)} %q.5), custom_call_target="tpu_custom_call" | custom-call | bytes 3932160 | tf_op jit(solution)/shard_map/pallas_call | solution.py:65
  3.0 0.7 collective-permute-start
  3.8 1.2 collective-permute-start.1
  5.0 0.5 collective-permute-start.2
  5.5 3.3 %shard_map.56 = (bf16[256,768]{1,0:T(8,128)(2,1)}, bf16[256,768]{1,0:T(8,128)(2,1)}, bf16[256,768]{1,0:T(8,128)(2,1)}, bf16[256,768]{1,0:T(8,128)(2,1)}, bf16[25...) custom-call(bf16[256,3072]{1,0:T(8,128)(2,1)} %refs_0_.3, bf16[256,3072]{1,0:T(8,128)(2,1)} %refs_1_.3, bf16[256,3072]{1,0:T(8,128)(2,1)} %q.5), custom_call_target="tpu_custom_call" | custom-call | bytes 4718592 | tf_op jit(solution)/shard_map/pallas_call | solution.py:65
  8.8 0.2 collective-permute-start.10
  9.0 1.2 collective-permute-start.11
  10.2 0.6 collective-permute-start.18
  10.9 3.7 %collective-permute-done.1.rest_1_.rest_2_ = bf16[256,768]{1,0:T(8,128)(2,1)S(1)} collective-permute-done((bf16[256,768]{1,0:T(8,128)(2,1)}, bf16[256,768]{1,0:T(8,128)(2,1)S(1)}, u32[]{:S(2)}, u32[]{:S(2)}) %collective-permute-start.1) | collective-permute-done | bytes 393248 | tf_op jit(solution)/shard_map/ppermute | solution.py:25
  14.6 1.2 collective-permute-start.19
  15.8 8.1 %collective-permute-done.2.rest_2_.rest_3_ = bf16[256,768]{1,0:T(8,128)(2,1)} collective-permute-done((bf16[256,768]{1,0:T(8,128)(2,1)}, bf16[256,768]{1,0:T(8,128)(2,1)}, u32[]{:S(2)}, u32[]{:S(2)}) %collective-permute-start.2) | collective-permute-done | bytes 393248 | tf_op jit(solution)/shard_map/ppermute | solution.py:25
  23.9 2.1 %collective-permute-start.4 = (bf16[256,1536]{1,0:T(8,128)(2,1)S(1)}, bf16[256,1536]{1,0:T(8,128)(2,1)}, u32[]{:S(2)}, u32[]{:S(2)}) collective-permute-start(bf16[256,1536]{1,0:T(8,128)(2,1)S(1)} %copy-done), channel_id=1, source_target_pairs={{4,8},{8,4},{5,9},{9,5},{6,10},{10,6},{7,11},{11,7},{20,24},{24,20... | collective-permute-start | bytes 2359304 | tf_op jit(solution)/shard_map/ppermute | solution.py:34
  26.0 1.1 collective-permute-start.20
  27.1 2.5 %pack_z.3 = (bf16[3,256,512]{2,1,0:T(8,128)(2,1)}, bf16[3,256,512]{2,1,0:T(8,128)(2,1)}) custom-call(bf16[256,1536]{1,0:T(8,128)(2,1)} %get-tuple-element.39.o.rest_0_, bf16[256,768]{1,0:T(8,128)(2,1)} %copy-done.4, bf16[256,768]{1,0:T(8,128)(2,1)} %copy-done.6, bf16[256,768]{1,0:T(8,128)(2,1)} %collective-permute-done.2.rest_2_.rest_3_), custom_call_target="tpu_custom_call" | custom-call | bytes 2621440 | tf_op jit(solution)/shard_map/pack_z/pallas_call | solution.py:103
  29.6 1.9 %collective-permute-done.11.rest_1_.rest_2_ = bf16[256,768]{1,0:T(8,128)(2,1)S(1)} collective-permute-done((bf16[256,768]{1,0:T(8,128)(2,1)}, bf16[256,768]{1,0:T(8,128)(2,1)S(1)}, u32[]{:S(2)}, u32[]{:S(2)}) %collective-permute-start.11) | collective-permute-done | bytes 393248 | tf_op jit(solution)/shard_map/ppermute | solution.py:25
  31.5 1.2 collective-permute-start.3
  32.7 0.3 collective-permute-start.5
  33.0 6.9 %collective-permute-done.19.rest_1_.rest_2_ = bf16[256,768]{1,0:T(8,128)(2,1)} collective-permute-done((bf16[256,768]{1,0:T(8,128)(2,1)}, bf16[256,768]{1,0:T(8,128)(2,1)}, u32[]{:S(2)}, u32[]{:S(2)}) %collective-permute-start.19) | collective-permute-done | bytes 393248 | tf_op jit(solution)/shard_map/ppermute | solution.py:25
  39.9 2.6 %collective-permute-start.12 = (bf16[256,768]{1,0:T(8,128)(2,1)}, bf16[256,768]{1,0:T(8,128)(2,1)S(1)}, u32[]{:S(2)}, u32[]{:S(2)}) collective-permute-start(bf16[256,768]{1,0:T(8,128)(2,1)} %get-tuple-element.51), channel_id=1, source_target_pairs={{0,3},{1,2},{2,1},{3,0},{4,7},{5,6},{6,5},{7,4},{8,11},{9,10},{10,... | collective-permute-start | bytes 1179656 | tf_op jit(solution)/shard_map/ppermute | solution.py:25
  42.5 6.9 %collective-permute-done.20.rest_2_.rest_3_ = bf16[256,768]{1,0:T(8,128)(2,1)} collective-permute-done((bf16[256,768]{1,0:T(8,128)(2,1)}, bf16[256,768]{1,0:T(8,128)(2,1)}, u32[]{:S(2)}, u32[]{:S(2)}) %collective-permute-start.20) | collective-permute-done | bytes 393248 | tf_op jit(solution)/shard_map/ppermute | solution.py:25
  49.5 2.1 %collective-permute-start.6 = (bf16[3,256,512]{2,1,0:T(8,128)(2,1)}, bf16[3,256,512]{2,1,0:T(8,128)(2,1)}, u32[]{:S(2)}, u32[]{:S(2)}) collective-permute-start(bf16[3,256,512]{2,1,0:T(8,128)(2,1)} %get-tuple-element.44), channel_id=1, source_target_pairs={{4,8},{8,4},{5,9},{9,5},{6,10},{10,6},{7,11},{11,7},{20,24},{24,20... | collective-permute-start | bytes 2359304 | tf_op jit(solution)/shard_map/ppermute | solution.py:34
  51.5 2.5 %pack_z.5 = (bf16[3,256,512]{2,1,0:T(8,128)(2,1)}, bf16[3,256,512]{2,1,0:T(8,128)(2,1)}) custom-call(bf16[256,1536]{1,0:T(8,128)(2,1)} %get-tuple-element.39.o.rest_0_, bf16[256,768]{1,0:T(8,128)(2,1)} %copy-done.5, bf16[256,768]{1,0:T(8,128)(2,1)} %collective-permute-done.19.rest_1_.rest_2_, bf16[256,768]{1,0:T(8,128)(2,1)} %collective-permute-done.20.rest_2_.rest_3_), custom_call_target="tpu_custom_call" | custom-call | bytes 2621440 | tf_op jit(solution)/shard_map/pack_z/pallas_call | solution.py:103
  54.1 3.3 %collective-permute-done.12.rest_2_.rest_3_ = bf16[256,768]{1,0:T(8,128)(2,1)S(1)} collective-permute-done((bf16[256,768]{1,0:T(8,128)(2,1)}, bf16[256,768]{1,0:T(8,128)(2,1)S(1)}, u32[]{:S(2)}, u32[]{:S(2)}) %collective-permute-start.12) | collective-permute-done | bytes 393248 | tf_op jit(solution)/shard_map/ppermute | solution.py:25
  57.3 1.3 collective-permute-start.21
  58.6 1.9 %collective-permute-start.22 = (bf16[3,256,512]{2,1,0:T(8,128)(2,1)}, bf16[3,256,512]{2,1,0:T(8,128)(2,1)}, u32[]{:S(2)}, u32[]{:S(2)}) collective-permute-start(bf16[3,256,512]{2,1,0:T(8,128)(2,1)} %get-tuple-element.62), channel_id=1, source_target_pairs={{4,8},{8,4},{5,9},{9,5},{6,10},{10,6},{7,11},{11,7},{20,24},{24,20... | collective-permute-start | bytes 2359304 | tf_op jit(solution)/shard_map/ppermute | solution.py:34
  60.6 2.4 %pack_z.4 = (bf16[3,256,512]{2,1,0:T(8,128)(2,1)}, bf16[3,256,512]{2,1,0:T(8,128)(2,1)}) custom-call(bf16[256,1536]{1,0:T(8,128)(2,1)} %get-tuple-element.39.o.rest_0_, bf16[256,768]{1,0:T(8,128)(2,1)} %copy-done.2, bf16[256,768]{1,0:T(8,128)(2,1)} %copy-done.3, bf16[256,768]{1,0:T(8,128)(2,1)} %copy-done.7), custom_call_target="tpu_custom_call" | custom-call | bytes 2621440 | tf_op jit(solution)/shard_map/pack_z/pallas_call | solution.py:103
  63.0 0.1 collective-permute-start.13
  63.1 3.1 %collective-permute-done.5.rest_6_ = bf16[3,256,512]{2,1,0:T(8,128)(2,1)} collective-permute-done((bf16[3,256,512]{2,1,0:T(8,128)(2,1)}, bf16[3,256,512]{2,1,0:T(8,128)(2,1)}, u32[]{:S(2)}, u32[]{:S(2)}) %collective-permute-start.5) | collective-permute-done | bytes 786464 | tf_op jit(solution)/shard_map/ppermute | solution.py:34
  66.2 2.1 %collective-permute-start.14 = (bf16[3,256,512]{2,1,0:T(8,128)(2,1)}, bf16[3,256,512]{2,1,0:T(8,128)(2,1)S(1)}, u32[]{:S(2)}, u32[]{:S(2)}) collective-permute-start(bf16[3,256,512]{2,1,0:T(8,128)(2,1)} %get-tuple-element.53), channel_id=1, source_target_pairs={{4,8},{8,4},{5,9},{9,5},{6,10},{10,6},{7,11},{11,7},{20,24},{24,20... | collective-permute-start | bytes 2359304 | tf_op jit(solution)/shard_map/ppermute | solution.py:34
  68.3 2.5 %lookup_tables.1 = (bf16[2560,128]{1,0:T(8,128)(2,1)}, bf16[1024,128]{1,0:T(8,128)(2,1)}, s32[4,2]{1,0:T(4,128)}) custom-call(s32[16]{0:T(128)} %len_ref.1, s32[16,16]{1,0:T(8,128)} %mask_ref.1), custom_call_target="tpu_custom_call" | custom-call | bytes 917504 | tf_op jit(solution)/shard_map/lookup_tables/pallas_call | solution.py:168
  70.8 0.4 collective-permute-done.6.rest_7_
  71.2 14.7 %attention.3 = (bf16[256,256]{1,0:T(8,128)(2,1)}, bf16[256,256]{1,0:T(8,128)(2,1)}, bf16[256,256]{1,0:T(8,128)(2,1)}, bf16[256,256]{1,0:T(8,128)(2,1)}) custom-call(s32[4,2]{1,0:T(4,128)} %get-tuple-element.36.ranges, bf16[2560,128]{1,0:T(8,128)(2,1)} %get-tuple-element.37.bias_hbm, bf16[1024,128]{1,0:T(8,128)(2,1)} %get-tuple-element.38.onehot_hbm, ...), custom_call_target="tpu_custom_call" | custom-call | flops 2147483648 | bytes 2621440 | tf_op jit(solution)/shard_map/attention/pallas_call | solution.py:302
  85.9 4.0 %collective-permute-start.7 = (bf16[256,256]{1,0:T(8,128)(2,1)}, bf16[256,256]{1,0:T(8,128)(2,1)S(1)}, u32[]{:S(2)}, u32[]{:S(2)}) collective-permute-start(bf16[256,256]{1,0:T(8,128)(2,1)} %get-tuple-element.46), channel_id=1, source_target_pairs={{0,1},{1,0},{2,3},{3,2},{4,5},{5,4},{6,7},{7,6},{8,9},{9,8},{10,11... | collective-permute-start | bytes 393224 | tf_op jit(solution)/shard_map/ppermute | solution.py:25
  89.9 1.3 collective-permute-start.8
  91.2 0.5 collective-permute-start.9
  91.7 14.8 %attention.5 = (bf16[256,256]{1,0:T(8,128)(2,1)}, bf16[256,256]{1,0:T(8,128)(2,1)}, bf16[256,256]{1,0:T(8,128)(2,1)}, bf16[256,256]{1,0:T(8,128)(2,1)}) custom-call(s32[4,2]{1,0:T(4,128)} %get-tuple-element.36.ranges, bf16[2560,128]{1,0:T(8,128)(2,1)} %get-tuple-element.37.bias_hbm, bf16[1024,128]{1,0:T(8,128)(2,1)} %get-tuple-element.38.onehot_hbm, ...), custom_call_target="tpu_custom_call" | custom-call | flops 2147483648 | bytes 2621440 | tf_op jit(solution)/shard_map/attention/pallas_call | solution.py:302
  106.4 0.2 collective-permute-start.23
  106.6 1.3 collective-permute-start.24
  107.9 14.7 %attention.4 = (bf16[256,256]{1,0:T(8,128)(2,1)}, bf16[256,256]{1,0:T(8,128)(2,1)}, bf16[256,256]{1,0:T(8,128)(2,1)}, bf16[256,256]{1,0:T(8,128)(2,1)}) custom-call(s32[4,2]{1,0:T(4,128)} %get-tuple-element.36.ranges, bf16[2560,128]{1,0:T(8,128)(2,1)} %get-tuple-element.37.bias_hbm, bf16[1024,128]{1,0:T(8,128)(2,1)} %get-tuple-element.38.onehot_hbm, ...), custom_call_target="tpu_custom_call" | custom-call | flops 2147483648 | bytes 2621440 | tf_op jit(solution)/shard_map/attention/pallas_call | solution.py:302
  122.7 1.2 collective-permute-start.25
  123.9 0.2 collective-permute-start.15
  124.0 0.8 collective-permute-start.16
  124.9 1.2 collective-permute-start.17
  126.0 2.7 %collective-permute-done.25.refs_11_ = bf16[256,256]{1,0:T(8,128)(2,1)S(1)} collective-permute-done((bf16[256,256]{1,0:T(8,128)(2,1)S(1)}, bf16[256,256]{1,0:T(8,128)(2,1)S(1)}, u32[]{:S(2)}, u32[]{:S(2)}) %collective-permute-start.25) | collective-permute-done | bytes 131104 | tf_op jit(solution)/shard_map/ppermute | solution.py:25
  128.8 2.8 %collective-permute-done.16.refs_6_ = bf16[256,256]{1,0:T(8,128)(2,1)S(1)} collective-permute-done((bf16[256,256]{1,0:T(8,128)(2,1)}, bf16[256,256]{1,0:T(8,128)(2,1)S(1)}, u32[]{:S(2)}, u32[]{:S(2)}) %collective-permute-start.16) | collective-permute-done | bytes 131104 | tf_op jit(solution)/shard_map/ppermute | solution.py:25
  131.6 2.8 %collective-permute-done.17.refs_7_ = bf16[256,256]{1,0:T(8,128)(2,1)S(1)} collective-permute-done((bf16[256,256]{1,0:T(8,128)(2,1)}, bf16[256,256]{1,0:T(8,128)(2,1)S(1)}, u32[]{:S(2)}, u32[]{:S(2)}) %collective-permute-start.17) | collective-permute-done | bytes 131104 | tf_op jit(solution)/shard_map/ppermute | solution.py:25
  134.4 0.6 copy-done.16
  135.0 2.7 %gather_out.1 = bf16[256,3072]{1,0:T(8,128)(2,1)} custom-call(bf16[256,256]{1,0:T(8,128)(2,1)} %get-tuple-element.45.refs_0_, bf16[256,256]{1,0:T(8,128)(2,1)} %copy-done.8, bf16[256,256]{1,0:T(8,128)(2,1)} %copy-done.9, bf16[256,256]{1,0:T(8,128)(2,1)} %copy-done.10, bf16[256,256]{1,0:T(8,128)(2,1)} %get-tuple-element.54.refs_4_, ...), custom_call_target="tpu_custom_call" | custom-call | bytes 3145728 | tf_op jit(solution)/shard_map/gather_out/pallas_call | solution.py:337
  (56 shorter events, 0.1 us)
Async XLA Ops:
  3.0 7.2 %collective-permute-start = (bf16[256,768]{1,0:T(8,128)(2,1)}, bf16[256,768]{1,0:T(8,128)(2,1)S(1)}, u32[]{:S(2)}, u32[]{:S(2)}) collective-permute-start(bf16[256,768]{1,0:T(8,128)(2,1)} %get-tuple-element.40), channel_id=1, source_target_pairs={{0,1},{1,0},{2,3},{3,2},{4,5},{5,4},{6,7},{7,6},{8,9},{9,8},{10,11... | collective-permute-start | bytes 1179656 | tf_op jit(solution)/shard_map/ppermute | solution.py:25
  3.8 10.8 %collective-permute-start.1 = (bf16[256,768]{1,0:T(8,128)(2,1)}, bf16[256,768]{1,0:T(8,128)(2,1)S(1)}, u32[]{:S(2)}, u32[]{:S(2)}) collective-permute-start(bf16[256,768]{1,0:T(8,128)(2,1)} %get-tuple-element.41), channel_id=1, source_target_pairs={{0,2},{1,3},{2,0},{3,1},{4,6},{5,7},{6,4},{7,5},{8,10},{9,11},{10,... | collective-permute-start | bytes 1179656 | tf_op jit(solution)/shard_map/ppermute | solution.py:25
  5.0 18.9 %copy-start = (bf16[256,1536]{1,0:T(8,128)(2,1)S(1)}, bf16[256,1536]{1,0:T(8,128)(2,1)}, u32[]{:S(2)}) copy-start(bf16[256,1536]{1,0:T(8,128)(2,1)} %get-tuple-element.39.o.rest_0_) | copy-start | bytes 2359300
  5.0 18.9 %collective-permute-start.2 = (bf16[256,768]{1,0:T(8,128)(2,1)}, bf16[256,768]{1,0:T(8,128)(2,1)}, u32[]{:S(2)}, u32[]{:S(2)}) collective-permute-start(bf16[256,768]{1,0:T(8,128)(2,1)} %get-tuple-element.42), channel_id=1, source_target_pairs={{0,3},{1,2},{2,1},{3,0},{4,7},{5,6},{6,5},{7,4},{8,11},{9,10},{10,... | collective-permute-start | bytes 1179656 | tf_op jit(solution)/shard_map/ppermute | solution.py:25
  8.8 22.8 %copy-start.1 = (bf16[256,1536]{1,0:T(8,128)(2,1)S(1)}, bf16[256,1536]{1,0:T(8,128)(2,1)}, u32[]{:S(2)}) copy-start(bf16[256,1536]{1,0:T(8,128)(2,1)} %get-tuple-element.39.o.rest_0_) | copy-start | bytes 2359300
  8.8 17.2 %collective-permute-start.10 = (bf16[256,768]{1,0:T(8,128)(2,1)}, bf16[256,768]{1,0:T(8,128)(2,1)S(1)}, u32[]{:S(2)}, u32[]{:S(2)}) collective-permute-start(bf16[256,768]{1,0:T(8,128)(2,1)} %get-tuple-element.49), channel_id=1, source_target_pairs={{0,1},{1,0},{2,3},{3,2},{4,5},{5,4},{6,7},{7,6},{8,9},{9,8},{10,11... | collective-permute-start | bytes 1179656 | tf_op jit(solution)/shard_map/ppermute | solution.py:25
  9.0 22.5 %collective-permute-start.11 = (bf16[256,768]{1,0:T(8,128)(2,1)}, bf16[256,768]{1,0:T(8,128)(2,1)S(1)}, u32[]{:S(2)}, u32[]{:S(2)}) collective-permute-start(bf16[256,768]{1,0:T(8,128)(2,1)} %get-tuple-element.50), channel_id=1, source_target_pairs={{0,2},{1,3},{2,0},{3,1},{4,6},{5,7},{6,4},{7,5},{8,10},{9,11},{10,... | collective-permute-start | bytes 1179656 | tf_op jit(solution)/shard_map/ppermute | solution.py:25
  10.2 16.8 %copy-start.4 = (bf16[256,768]{1,0:T(8,128)(2,1)}, bf16[256,768]{1,0:T(8,128)(2,1)S(1)}, u32[]{:S(2)}) copy-start(bf16[256,768]{1,0:T(8,128)(2,1)S(1)} %collective-permute-done.rest_0_.rest_1_) | copy-start | bytes 1179652
  10.2 22.5 %collective-permute-start.18 = (bf16[256,768]{1,0:T(8,128)(2,1)}, bf16[256,768]{1,0:T(8,128)(2,1)S(1)}, u32[]{:S(2)}, u32[]{:S(2)}) collective-permute-start(bf16[256,768]{1,0:T(8,128)(2,1)} %get-tuple-element.58), channel_id=1, source_target_pairs={{0,1},{1,0},{2,3},{3,2},{4,5},{5,4},{6,7},{7,6},{8,9},{9,8},{10,11... | collective-permute-start | bytes 1179656 | tf_op jit(solution)/shard_map/ppermute | solution.py:25
  14.6 12.5 %copy-start.6 = (bf16[256,768]{1,0:T(8,128)(2,1)}, bf16[256,768]{1,0:T(8,128)(2,1)S(1)}, u32[]{:S(2)}) copy-start(bf16[256,768]{1,0:T(8,128)(2,1)S(1)} %collective-permute-done.1.rest_1_.rest_2_) | copy-start | bytes 1179652
  14.6 25.4 %collective-permute-start.19 = (bf16[256,768]{1,0:T(8,128)(2,1)}, bf16[256,768]{1,0:T(8,128)(2,1)}, u32[]{:S(2)}, u32[]{:S(2)}) collective-permute-start(bf16[256,768]{1,0:T(8,128)(2,1)} %get-tuple-element.59), channel_id=1, source_target_pairs={{0,2},{1,3},{2,0},{3,1},{4,6},{5,7},{6,4},{7,5},{8,10},{9,11},{10,... | collective-permute-start | bytes 1179656 | tf_op jit(solution)/shard_map/ppermute | solution.py:25
  23.9 34.8 %collective-permute-start.4 = (bf16[256,1536]{1,0:T(8,128)(2,1)S(1)}, bf16[256,1536]{1,0:T(8,128)(2,1)}, u32[]{:S(2)}, u32[]{:S(2)}) collective-permute-start(bf16[256,1536]{1,0:T(8,128)(2,1)S(1)} %copy-done), channel_id=1, source_target_pairs={{4,8},{8,4},{5,9},{9,5},{6,10},{10,6},{7,11},{11,7},{20,24},{24,20... | collective-permute-start | bytes 2359304 | tf_op jit(solution)/shard_map/ppermute | solution.py:34
  26.0 28.1 %copy-start.2 = (bf16[256,768]{1,0:T(8,128)(2,1)}, bf16[256,768]{1,0:T(8,128)(2,1)S(1)}, u32[]{:S(2)}) copy-start(bf16[256,768]{1,0:T(8,128)(2,1)S(1)} %collective-permute-done.10.rest_0_.rest_1_) | copy-start | bytes 1179652
  26.0 23.5 %collective-permute-start.20 = (bf16[256,768]{1,0:T(8,128)(2,1)}, bf16[256,768]{1,0:T(8,128)(2,1)}, u32[]{:S(2)}, u32[]{:S(2)}) collective-permute-start(bf16[256,768]{1,0:T(8,128)(2,1)} %get-tuple-element.60), channel_id=1, source_target_pairs={{0,3},{1,2},{2,1},{3,0},{4,7},{5,6},{6,5},{7,4},{8,11},{9,10},{10,... | collective-permute-start | bytes 1179656 | tf_op jit(solution)/shard_map/ppermute | solution.py:25
  31.5 29.0 %copy-start.3 = (bf16[256,768]{1,0:T(8,128)(2,1)}, bf16[256,768]{1,0:T(8,128)(2,1)S(1)}, u32[]{:S(2)}) copy-start(bf16[256,768]{1,0:T(8,128)(2,1)S(1)} %collective-permute-done.11.rest_1_.rest_2_) | copy-start | bytes 1179652
  31.5 31.5 %collective-permute-start.3 = (bf16[256,1536]{1,0:T(8,128)(2,1)S(1)}, bf16[256,1536]{1,0:T(8,128)(2,1)}, u32[]{:S(2)}, u32[]{:S(2)}) collective-permute-start(bf16[256,1536]{1,0:T(8,128)(2,1)S(1)} %copy-done.1), channel_id=1, source_target_pairs={{0,4},{4,0},{1,5},{5,1},{2,6},{6,2},{3,7},{7,3},{8,12},{12,8},{9,1... | collective-permute-start | bytes 2359304 | tf_op jit(solution)/shard_map/ppermute | solution.py:34
  32.7 18.8 %copy-start.5 = (bf16[256,768]{1,0:T(8,128)(2,1)}, bf16[256,768]{1,0:T(8,128)(2,1)S(1)}, u32[]{:S(2)}) copy-start(bf16[256,768]{1,0:T(8,128)(2,1)S(1)} %collective-permute-done.18.rest_0_.rest_1_) | copy-start | bytes 1179652
  32.7 33.5 %collective-permute-start.5 = (bf16[3,256,512]{2,1,0:T(8,128)(2,1)}, bf16[3,256,512]{2,1,0:T(8,128)(2,1)}, u32[]{:S(2)}, u32[]{:S(2)}) collective-permute-start(bf16[3,256,512]{2,1,0:T(8,128)(2,1)} %get-tuple-element.43), channel_id=1, source_target_pairs={{0,4},{4,0},{1,5},{5,1},{2,6},{6,2},{3,7},{7,3},{8,12},{12,8},{9,1... | collective-permute-start | bytes 2359304 | tf_op jit(solution)/shard_map/ppermute | solution.py:34
  39.9 17.4 %collective-permute-start.12 = (bf16[256,768]{1,0:T(8,128)(2,1)}, bf16[256,768]{1,0:T(8,128)(2,1)S(1)}, u32[]{:S(2)}, u32[]{:S(2)}) collective-permute-start(bf16[256,768]{1,0:T(8,128)(2,1)} %get-tuple-element.51), channel_id=1, source_target_pairs={{0,3},{1,2},{2,1},{3,0},{4,7},{5,6},{6,5},{7,4},{8,11},{9,10},{10,... | collective-permute-start | bytes 1179656 | tf_op jit(solution)/shard_map/ppermute | solution.py:25
  49.5 21.8 %collective-permute-start.6 = (bf16[3,256,512]{2,1,0:T(8,128)(2,1)}, bf16[3,256,512]{2,1,0:T(8,128)(2,1)}, u32[]{:S(2)}, u32[]{:S(2)}) collective-permute-start(bf16[3,256,512]{2,1,0:T(8,128)(2,1)} %get-tuple-element.44), channel_id=1, source_target_pairs={{4,8},{8,4},{5,9},{9,5},{6,10},{10,6},{7,11},{11,7},{20,24},{24,20... | collective-permute-start | bytes 2359304 | tf_op jit(solution)/shard_map/ppermute | solution.py:34
  57.3 3.2 %copy-start.7 = (bf16[256,768]{1,0:T(8,128)(2,1)}, bf16[256,768]{1,0:T(8,128)(2,1)S(1)}, u32[]{:S(2)}) copy-start(bf16[256,768]{1,0:T(8,128)(2,1)S(1)} %collective-permute-done.12.rest_2_.rest_3_) | copy-start | bytes 1179652
  57.3 32.6 %collective-permute-start.21 = (bf16[3,256,512]{2,1,0:T(8,128)(2,1)}, bf16[3,256,512]{2,1,0:T(8,128)(2,1)S(1)}, u32[]{:S(2)}, u32[]{:S(2)}) collective-permute-start(bf16[3,256,512]{2,1,0:T(8,128)(2,1)} %get-tuple-element.61), channel_id=1, source_target_pairs={{0,4},{4,0},{1,5},{5,1},{2,6},{6,2},{3,7},{7,3},{8,12},{12,8},{9,1... | collective-permute-start | bytes 2359304 | tf_op jit(solution)/shard_map/ppermute | solution.py:34
  58.6 32.5 %collective-permute-start.22 = (bf16[3,256,512]{2,1,0:T(8,128)(2,1)}, bf16[3,256,512]{2,1,0:T(8,128)(2,1)}, u32[]{:S(2)}, u32[]{:S(2)}) collective-permute-start(bf16[3,256,512]{2,1,0:T(8,128)(2,1)} %get-tuple-element.62), channel_id=1, source_target_pairs={{4,8},{8,4},{5,9},{9,5},{6,10},{10,6},{7,11},{11,7},{20,24},{24,20... | collective-permute-start | bytes 2359304 | tf_op jit(solution)/shard_map/ppermute | solution.py:34
  63.0 43.4 %collective-permute-start.13 = (bf16[3,256,512]{2,1,0:T(8,128)(2,1)}, bf16[3,256,512]{2,1,0:T(8,128)(2,1)S(1)}, u32[]{:S(2)}, u32[]{:S(2)}) collective-permute-start(bf16[3,256,512]{2,1,0:T(8,128)(2,1)} %get-tuple-element.52), channel_id=1, source_target_pairs={{0,4},{4,0},{1,5},{5,1},{2,6},{6,2},{3,7},{7,3},{8,12},{12,8},{9,1... | collective-permute-start | bytes 2359304 | tf_op jit(solution)/shard_map/ppermute | solution.py:34
  66.2 40.4 %collective-permute-start.14 = (bf16[3,256,512]{2,1,0:T(8,128)(2,1)}, bf16[3,256,512]{2,1,0:T(8,128)(2,1)S(1)}, u32[]{:S(2)}, u32[]{:S(2)}) collective-permute-start(bf16[3,256,512]{2,1,0:T(8,128)(2,1)} %get-tuple-element.53), channel_id=1, source_target_pairs={{4,8},{8,4},{5,9},{9,5},{6,10},{10,6},{7,11},{11,7},{20,24},{24,20... | collective-permute-start | bytes 2359304 | tf_op jit(solution)/shard_map/ppermute | solution.py:34
  85.9 36.7 %collective-permute-start.7 = (bf16[256,256]{1,0:T(8,128)(2,1)}, bf16[256,256]{1,0:T(8,128)(2,1)S(1)}, u32[]{:S(2)}, u32[]{:S(2)}) collective-permute-start(bf16[256,256]{1,0:T(8,128)(2,1)} %get-tuple-element.46), channel_id=1, source_target_pairs={{0,1},{1,0},{2,3},{3,2},{4,5},{5,4},{6,7},{7,6},{8,9},{9,8},{10,11... | collective-permute-start | bytes 393224 | tf_op jit(solution)/shard_map/ppermute | solution.py:25
  89.9 1.7 %copy-start.19 = (bf16[3,256,512]{2,1,0:T(8,128)(2,1)}, bf16[3,256,512]{2,1,0:T(8,128)(2,1)S(1)}, u32[]{:S(2)}) copy-start(bf16[3,256,512]{2,1,0:T(8,128)(2,1)S(1)} %collective-permute-done.21.rest_6_) | copy-start | bytes 2359300
  89.9 33.9 %collective-permute-start.8 = (bf16[256,256]{1,0:T(8,128)(2,1)}, bf16[256,256]{1,0:T(8,128)(2,1)S(1)}, u32[]{:S(2)}, u32[]{:S(2)}) collective-permute-start(bf16[256,256]{1,0:T(8,128)(2,1)} %get-tuple-element.47), channel_id=1, source_target_pairs={{0,2},{1,3},{2,0},{3,1},{4,6},{5,7},{6,4},{7,5},{8,10},{9,11},{10,... | collective-permute-start | bytes 393224 | tf_op jit(solution)/shard_map/ppermute | solution.py:25
  91.2 32.8 %collective-permute-start.9 = (bf16[256,256]{1,0:T(8,128)(2,1)}, bf16[256,256]{1,0:T(8,128)(2,1)S(1)}, u32[]{:S(2)}, u32[]{:S(2)}) collective-permute-start(bf16[256,256]{1,0:T(8,128)(2,1)} %get-tuple-element.48), channel_id=1, source_target_pairs={{0,3},{1,2},{2,1},{3,0},{4,7},{5,6},{6,5},{7,4},{8,11},{9,10},{10,... | collective-permute-start | bytes 393224 | tf_op jit(solution)/shard_map/ppermute | solution.py:25
  106.4 1.5 %copy-start.17 = (bf16[3,256,512]{2,1,0:T(8,128)(2,1)}, bf16[3,256,512]{2,1,0:T(8,128)(2,1)S(1)}, u32[]{:S(2)}) copy-start(bf16[3,256,512]{2,1,0:T(8,128)(2,1)S(1)} %collective-permute-done.13.rest_6_) | copy-start | bytes 2359300
  106.4 18.4 %collective-permute-start.23 = (bf16[256,256]{1,0:T(8,128)(2,1)}, bf16[256,256]{1,0:T(8,128)(2,1)S(1)}, u32[]{:S(2)}, u32[]{:S(2)}) collective-permute-start(bf16[256,256]{1,0:T(8,128)(2,1)} %get-tuple-element.64), channel_id=1, source_target_pairs={{0,1},{1,0},{2,3},{3,2},{4,5},{5,4},{6,7},{7,6},{8,9},{9,8},{10,11... | collective-permute-start | bytes 393224 | tf_op jit(solution)/shard_map/ppermute | solution.py:25
  106.6 1.3 copy-start.18
  106.6 16.0 %copy-start.20 = (bf16[256,256]{1,0:T(8,128)(2,1)S(1)}, bf16[256,256]{1,0:T(8,128)(2,1)}, u32[]{:S(2)}) copy-start(bf16[256,256]{1,0:T(8,128)(2,1)} %get-tuple-element.66) | copy-start | bytes 393220
  106.6 19.4 %collective-permute-start.24 = (bf16[256,256]{1,0:T(8,128)(2,1)}, bf16[256,256]{1,0:T(8,128)(2,1)S(1)}, u32[]{:S(2)}, u32[]{:S(2)}) collective-permute-start(bf16[256,256]{1,0:T(8,128)(2,1)} %get-tuple-element.65), channel_id=1, source_target_pairs={{0,2},{1,3},{2,0},{3,1},{4,6},{5,7},{6,4},{7,5},{8,10},{9,11},{10,... | collective-permute-start | bytes 393224 | tf_op jit(solution)/shard_map/ppermute | solution.py:25
  122.7 11.7 %copy-start.8 = (bf16[256,256]{1,0:T(8,128)(2,1)}, bf16[256,256]{1,0:T(8,128)(2,1)S(1)}, u32[]{:S(2)}) copy-start(bf16[256,256]{1,0:T(8,128)(2,1)S(1)} %collective-permute-done.7.refs_1_) | copy-start | bytes 393220
  122.7 6.1 %collective-permute-start.25 = (bf16[256,256]{1,0:T(8,128)(2,1)S(1)}, bf16[256,256]{1,0:T(8,128)(2,1)S(1)}, u32[]{:S(2)}, u32[]{:S(2)}) collective-permute-start(bf16[256,256]{1,0:T(8,128)(2,1)S(1)} %copy-done.20), channel_id=1, source_target_pairs={{0,3},{1,2},{2,1},{3,0},{4,7},{5,6},{6,5},{7,4},{8,11},{9,10},{10,... | collective-permute-start | bytes 393224 | tf_op jit(solution)/shard_map/ppermute | solution.py:25
  123.9 10.5 %copy-start.9 = (bf16[256,256]{1,0:T(8,128)(2,1)}, bf16[256,256]{1,0:T(8,128)(2,1)S(1)}, u32[]{:S(2)}) copy-start(bf16[256,256]{1,0:T(8,128)(2,1)S(1)} %collective-permute-done.8.refs_2_) | copy-start | bytes 393220
  123.9 4.9 %collective-permute-start.15 = (bf16[256,256]{1,0:T(8,128)(2,1)}, bf16[256,256]{1,0:T(8,128)(2,1)S(1)}, u32[]{:S(2)}, u32[]{:S(2)}) collective-permute-start(bf16[256,256]{1,0:T(8,128)(2,1)} %get-tuple-element.55), channel_id=1, source_target_pairs={{0,1},{1,0},{2,3},{3,2},{4,5},{5,4},{6,7},{7,6},{8,9},{9,8},{10,11... | collective-permute-start | bytes 393224 | tf_op jit(solution)/shard_map/ppermute | solution.py:25
  124.0 10.4 %copy-start.10 = (bf16[256,256]{1,0:T(8,128)(2,1)}, bf16[256,256]{1,0:T(8,128)(2,1)S(1)}, u32[]{:S(2)}) copy-start(bf16[256,256]{1,0:T(8,128)(2,1)S(1)} %collective-permute-done.9.refs_3_) | copy-start | bytes 393220
  124.0 7.5 %collective-permute-start.16 = (bf16[256,256]{1,0:T(8,128)(2,1)}, bf16[256,256]{1,0:T(8,128)(2,1)S(1)}, u32[]{:S(2)}, u32[]{:S(2)}) collective-permute-start(bf16[256,256]{1,0:T(8,128)(2,1)} %get-tuple-element.56), channel_id=1, source_target_pairs={{0,2},{1,3},{2,0},{3,1},{4,6},{5,7},{6,4},{7,5},{8,10},{9,11},{10,... | collective-permute-start | bytes 393224 | tf_op jit(solution)/shard_map/ppermute | solution.py:25
  124.9 9.5 %copy-start.11 = (bf16[256,256]{1,0:T(8,128)(2,1)}, bf16[256,256]{1,0:T(8,128)(2,1)S(1)}, u32[]{:S(2)}) copy-start(bf16[256,256]{1,0:T(8,128)(2,1)S(1)} %collective-permute-done.23.refs_9_) | copy-start | bytes 393220
  124.9 9.5 %collective-permute-start.17 = (bf16[256,256]{1,0:T(8,128)(2,1)}, bf16[256,256]{1,0:T(8,128)(2,1)S(1)}, u32[]{:S(2)}, u32[]{:S(2)}) collective-permute-start(bf16[256,256]{1,0:T(8,128)(2,1)} %get-tuple-element.57), channel_id=1, source_target_pairs={{0,3},{1,2},{2,1},{3,0},{4,7},{5,6},{6,5},{7,4},{8,11},{9,10},{10,... | collective-permute-start | bytes 393224 | tf_op jit(solution)/shard_map/ppermute | solution.py:25
  126.0 8.4 %copy-start.12 = (bf16[256,256]{1,0:T(8,128)(2,1)}, bf16[256,256]{1,0:T(8,128)(2,1)S(1)}, u32[]{:S(2)}) copy-start(bf16[256,256]{1,0:T(8,128)(2,1)S(1)} %collective-permute-done.24.refs_10_) | copy-start | bytes 393220
  128.8 5.7 %copy-start.13 = (bf16[256,256]{1,0:T(8,128)(2,1)}, bf16[256,256]{1,0:T(8,128)(2,1)S(1)}, u32[]{:S(2)}) copy-start(bf16[256,256]{1,0:T(8,128)(2,1)S(1)} %collective-permute-done.25.refs_11_) | copy-start | bytes 393220
  128.8 5.7 %copy-start.14 = (bf16[256,256]{1,0:T(8,128)(2,1)}, bf16[256,256]{1,0:T(8,128)(2,1)S(1)}, u32[]{:S(2)}) copy-start(bf16[256,256]{1,0:T(8,128)(2,1)S(1)} %collective-permute-done.15.refs_5_) | copy-start | bytes 393220
  131.6 2.9 %copy-start.15 = (bf16[256,256]{1,0:T(8,128)(2,1)}, bf16[256,256]{1,0:T(8,128)(2,1)S(1)}, u32[]{:S(2)}) copy-start(bf16[256,256]{1,0:T(8,128)(2,1)S(1)} %collective-permute-done.16.refs_6_) | copy-start | bytes 393220
  134.4 0.6 copy-start.16
where the time goes:
time: 138 us
  Pallas kernels  63.1 us (46%)
  waiting for transfers between devices  42.7 us (31%)
  starting transfers between devices  30.9 us (22%)
    pallas_call x3, Pallas kernels, attention(): pl.pallas_call(kernel, out_shape=[jax.ShapeDtypeStruct((rows, width), bf)...  44.2 us
    ppermute x18, waiting for transfers between devices, swap(): lax.ppermute(value, 'ctx', [(i, i ^ bits) for i in range(lax.axis_size('c...  39.2 us
    ppermute x18, starting transfers between devices, swap(): lax.ppermute(value, 'ctx', [(i, i ^ bits) for i in range(lax.axis_size('c...  20 us
    ppermute x8, starting transfers between devices, swap_levels(): return lax.ppermute(value, 'ctx', pairs)  10.9 us
    pallas_call x3, Pallas kernels, pack_z(): pl.pallas_call(kernel, out_shape=[jax.ShapeDtypeStruct((n_fwd, rows, 2 *...  7.49 us
    pallas_call x2, Pallas kernels, pack_columns(): pl.pallas_call(kernel, out_shape=[jax.ShapeDtypeStruct((rows, total), arr...  6.29 us
    ppermute x8, waiting for transfers between devices, swap_levels(): return lax.ppermute(value, 'ctx', pairs)  3.53 us
  transfers between devices with their start and end apart: 26, of which 11 were waited for; matrix products, arithmetic and copies ran while one was open for 0% of the time, Pallas kernels for 42%

commit v1 on v0

--- a/solution.py
+++ b/solution.py
@@ -16,7 +16,8 @@
 OTHERS = tuple(range(1, LEVEL))
 NEG = -1e30
 TILE = 256
-HBM = pl.BlockSpec(memory_space=pltpu.HBM)
+SIZES = (2, 3, 4, 5, 6, 8)
+HBM = pl.BlockSpec(memory_space=pl.ANY)
 VMEM = pl.BlockSpec(memory_space=pltpu.VMEM)
 SMEM = pl.BlockSpec(memory_space=pltpu.SMEM)
 
@@ -147,7 +148,9 @@
         )
         for b in range(LEVEL):
             start = jnp.maximum(ranges[b, 0], 0) // HEAD * HEAD
-            tiles = (ranges[b, 1] - start + TILE - 1) // TILE
+            tiles = jnp.int32(SIZES[-1])
+            for size in SIZES[-2::-1]:
+                tiles = jnp.where(ranges[b, 1] - start <= size * TILE, size, tiles)
             ranges[b, 0] = jnp.minimum(start, key_rows - tiles * TILE)
             ranges[b, 1] = tiles
 
@@ -192,7 +195,7 @@
         level, rest = rest[:LEVEL], rest[LEVEL:]
         own_sides, sides, rest = rest[:2], rest[2:4], rest[4:]
         outs, scratch = rest[:LEVEL], rest[LEVEL:]
-        ks, vs, vt, qs, os, acc, bias, onehot, sems, out_sems = scratch
+        ks, vs, vt, qs, os, bias, onehot, sems, out_sems = scratch
         me = lax.axis_index("ctx")
         j = lax.rem(me, LEVEL)
         odd = lax.rem(me // LEVEL, 2)
@@ -250,44 +253,30 @@
         @pl.loop(0, LEVEL)
         def _(b):
             at = pl.ds(pl.multiple_of(b * rows, rows), rows)
-            start, tiles = ranges[b, 0], ranges[b, 1]
-            for h in range(heads):
-                acc[h] = jnp.zeros_like(acc[h])
-            q_ext = [
-                jnp.concatenate([qs[at, h * HEAD : (h + 1) * HEAD], onehot[at, :]], axis=1)
-                for h in range(heads)
-            ]
-
-            def step(t, tops):
-                k_at = pl.ds(pl.multiple_of(start + t * TILE, HEAD), TILE)
-                scores = [
-                    lax.dot_general(
-                        jnp.concatenate(
-                            [ks[k_at, h * HEAD : (h + 1) * HEAD], bias[k_at, :]], axis=1
-                        ),
-                        q_ext[h],
-                        (((1,), (1,)), ((), ())),
-                        preferred_element_type=jnp.float32,
-                    )
-                    for h in range(heads)
-                ]
-                new = []
-                for h in range(heads):
-                    s, top = scores[h], tops[h]
-                    top_new = jnp.maximum(top, jnp.max(s, axis=0, keepdims=True))
-                    p = jnp.exp2((s - top_new) * factor).astype(jnp.bfloat16)
-                    alpha = jnp.exp2((top - top_new) * factor)
-                    acc[h] = acc[h] * alpha + jnp.dot(
-                        vt[h, :, k_at], p, preferred_element_type=jnp.float32
-                    )
-                    new.append(top_new)
-                return tuple(new)
-
-            low = jnp.full((1, rows), 2 * NEG, jnp.float32)
-            lax.fori_loop(0, tiles, step, (low,) * heads)
-            for h in range(heads):
-                normed = acc[h, :HEAD, :] / acc[h, HEAD : HEAD + 1, :]
-                os[at, h * HEAD : (h + 1) * HEAD] = normed.T.astype(jnp.bfloat16)
+            start = pl.multiple_of(ranges[b, 0], HEAD)
+            for size in SIZES:
+                @pl.when(ranges[b, 1] == size)
+                def _():
+                    k_at = pl.ds(start, size * TILE)
+                    scores = [
+                        lax.dot_general(
+                            jnp.concatenate(
+                                [ks[k_at, h * HEAD : (h + 1) * HEAD], bias[k_at, :]], axis=1
+                            ),
+                            jnp.concatenate(
+                                [qs[at, h * HEAD : (h + 1) * HEAD], onehot[at, :]], axis=1
+                            ),
+                            (((1,), (1,)), ((), ())),
+                            preferred_element_type=jnp.float32,
+                        )
+                        for h in range(heads)
+                    ]
+                    for h, s in enumerate(scores):
+                        top = jnp.max(s, axis=0, keepdims=True)
+                        p = jnp.exp2((s - top) * factor).astype(jnp.bfloat16)
+                        both = jnp.dot(vt[h, :, k_at], p, preferred_element_type=jnp.float32)
+                        normed = both[:HEAD] / both[HEAD : HEAD + 1]
+                        os[at, h * HEAD : (h + 1) * HEAD] = normed.T.astype(jnp.bfloat16)
 
         run_copies(
             [
@@ -310,7 +299,6 @@
             pltpu.VMEM((heads, HEAD + 16, key_rows), bf),
             pltpu.VMEM((LEVEL * rows, width), bf),
             pltpu.VMEM((LEVEL * rows, width), bf),
-            pltpu.VMEM((heads, HEAD + 16, rows), jnp.float32),
             pltpu.VMEM((key_rows, lanes), bf),
             pltpu.VMEM((LEVEL * rows, lanes), bf),
             pltpu.SemaphoreType.DMA((n_copies,)),
@@ -351,6 +339,7 @@
     ahead = (MAXLEN - 2) // rows + 1
     assert LEVEL * rows >= (WIN + 1) * MAXLEN - 1 and ahead < LEVEL
     assert sum(SPLIT) * HEAD == slab
+    assert (WIN + 2) * MAXLEN + rows + HEAD <= SIZES[-1] * TILE + 4
     widths = [heads * HEAD for heads in SPLIT]
     offsets = [sum(widths[:g]) for g in range(len(widths))]
     groups = range(len(SPLIT))

time: 138 us -> 132 us (0.957)
  Pallas kernels: 63.1 us -> 49.7 us
  waiting for transfers between devices: 42.7 us -> 46.9 us
  starting transfers between devices: 30.9 us -> 33.3 us
    pallas_call x3, Pallas kernels: 44.2 us -> 30.8 us  [attention(): pl.pallas_call(kernel, out_shape=[jax.ShapeDtypeStruct((rows, width), bf)...]
    ppermute x8, waiting for transfers between devices: 3.53 us -> 7.66 us  [swap_levels(): return lax.ppermute(value, 'ctx', pairs)]
    ppermute x18, starting transfers between devices: 20 us -> 22.4 us  [swap(): lax.ppermute(value, 'ctx', [(i, i ^ bits) for i in range(lax.axis_size('c...]
  transfers between devices with their start and end apart: 26 -> 26, of which waited for: 11 -> 14; matrix products, arithmetic and copies ran while one was open for 0% -> 0% of each run, Pallas kernels for 42% -> 34%
where the time goes in v1:
time: 132 us; the launch traced here: 131 us
  Pallas kernels  49.7 us (38%)
  waiting for transfers between devices  46.9 us (36%)
  starting transfers between devices  33.3 us (25%)
    ppermute x18, waiting for transfers between devices, swap(): lax.ppermute(value, 'ctx', [(i, i ^ bits) for i in range(lax.axis_size('c...  39.2 us
    pallas_call x3, Pallas kernels, attention(): pl.pallas_call(kernel, out_shape=[jax.ShapeDtypeStruct((rows, width), bf)...  30.8 us
    ppermute x18, starting transfers between devices, swap(): lax.ppermute(value, 'ctx', [(i, i ^ bits) for i in range(lax.axis_size('c...  22.4 us
    ppermute x8, starting transfers between devices, swap_levels(): return lax.ppermute(value, 'ctx', pairs)  10.9 us
    ppermute x8, waiting for transfers between devices, swap_levels(): return lax.ppermute(value, 'ctx', pairs)  7.66 us
    pallas_call x3, Pallas kernels, pack_z(): pl.pallas_call(kernel, out_shape=[jax.ShapeDtypeStruct((n_fwd, rows, 2 *...  7.46 us
    pallas_call x2, Pallas kernels, pack_columns(): pl.pallas_call(kernel, out_shape=[jax.ShapeDtypeStruct((rows, total), arr...  6.29 us
    pallas_call x1, Pallas kernels, gather_out(): pl.pallas_call(kernel, out_shape=jax.ShapeDtypeStruct((rows, LEVEL * slab...  2.68 us
  transfers between devices with their start and end apart: 26, of which 14 were waited for; matrix products, arithmetic and copies ran while one was open for 0% of the time, Pallas kernels for 34%

profile of v1, /device:TPU:19, one launch (start us, length us, event | category | flops | bytes accessed | tf_op | source)
XLA Modules:
  0.0 131.1 jit_solution(9171611070451169719)
XLA Ops:
  0.0 3.0 %shard_map.55 = (bf16[256,768]{1,0:T(8,128)(2,1)}, bf16[256,768]{1,0:T(8,128)(2,1)}, bf16[256,768]{1,0:T(8,128)(2,1)}, bf16[256,1536]{1,0:T(8,128)(2,1)}) custom-call(bf16[256,3072]{1,0:T(8,128)(2,1)} %refs_0_.3, bf16[256,3072]{1,0:T(8,128)(2,1)} %refs_1_.3, bf16[256,3072]{1,0:T(8,128)(2,1)} %q.5), custom_call_target="tpu_custom_call" | custom-call | bytes 3932160 | tf_op jit(solution)/shard_map/pallas_call | solution.py:66
  3.0 0.7 collective-permute-start
  3.8 1.2 collective-permute-start.1
  5.0 0.5 collective-permute-start.2
  5.5 3.3 %shard_map.56 = (bf16[256,768]{1,0:T(8,128)(2,1)}, bf16[256,768]{1,0:T(8,128)(2,1)}, bf16[256,768]{1,0:T(8,128)(2,1)}, bf16[256,768]{1,0:T(8,128)(2,1)}, bf16[25...) custom-call(bf16[256,3072]{1,0:T(8,128)(2,1)} %refs_0_.3, bf16[256,3072]{1,0:T(8,128)(2,1)} %refs_1_.3, bf16[256,3072]{1,0:T(8,128)(2,1)} %q.5), custom_call_target="tpu_custom_call" | custom-call | bytes 4718592 | tf_op jit(solution)/shard_map/pallas_call | solution.py:66
  9.0 1.2 collective-permute-start.11
  10.2 0.6 collective-permute-start.18
  10.9 3.7 %collective-permute-done.1.rest_1_.rest_2_ = bf16[256,768]{1,0:T(8,128)(2,1)S(1)} collective-permute-done((bf16[256,768]{1,0:T(8,128)(2,1)}, bf16[256,768]{1,0:T(8,128)(2,1)S(1)}, u32[]{:S(2)}, u32[]{:S(2)}) %collective-permute-start.1) | collective-permute-done | bytes 393248 | tf_op jit(solution)/shard_map/ppermute | solution.py:26
  14.6 1.2 collective-permute-start.19
  15.8 8.1 %collective-permute-done.2.rest_2_.rest_3_ = bf16[256,768]{1,0:T(8,128)(2,1)} collective-permute-done((bf16[256,768]{1,0:T(8,128)(2,1)}, bf16[256,768]{1,0:T(8,128)(2,1)}, u32[]{:S(2)}, u32[]{:S(2)}) %collective-permute-start.2) | collective-permute-done | bytes 393248 | tf_op jit(solution)/shard_map/ppermute | solution.py:26
  23.9 2.1 %collective-permute-start.4 = (bf16[256,1536]{1,0:T(8,128)(2,1)S(1)}, bf16[256,1536]{1,0:T(8,128)(2,1)}, u32[]{:S(2)}, u32[]{:S(2)}) collective-permute-start(bf16[256,1536]{1,0:T(8,128)(2,1)S(1)} %copy-done), channel_id=1, source_target_pairs={{4,8},{8,4},{5,9},{9,5},{6,10},{10,6},{7,11},{11,7},{20,24},{24,20... | collective-permute-start | bytes 2359304 | tf_op jit(solution)/shard_map/ppermute | solution.py:35
  26.0 1.1 collective-permute-start.20
  27.1 2.5 %pack_z.3 = (bf16[3,256,512]{2,1,0:T(8,128)(2,1)}, bf16[3,256,512]{2,1,0:T(8,128)(2,1)}) custom-call(bf16[256,1536]{1,0:T(8,128)(2,1)} %get-tuple-element.39.o.rest_0_, bf16[256,768]{1,0:T(8,128)(2,1)} %copy-done.4, bf16[256,768]{1,0:T(8,128)(2,1)} %copy-done.6, bf16[256,768]{1,0:T(8,128)(2,1)} %collective-permute-done.2.rest_2_.rest_3_), custom_call_target="tpu_custom_call" | custom-call | bytes 2621440 | tf_op jit(solution)/shard_map/pack_z/pallas_call | solution.py:104
  29.6 2.0 %collective-permute-done.11.rest_1_.rest_2_ = bf16[256,768]{1,0:T(8,128)(2,1)S(1)} collective-permute-done((bf16[256,768]{1,0:T(8,128)(2,1)}, bf16[256,768]{1,0:T(8,128)(2,1)S(1)}, u32[]{:S(2)}, u32[]{:S(2)}) %collective-permute-start.11) | collective-permute-done | bytes 393248 | tf_op jit(solution)/shard_map/ppermute | solution.py:26
  31.5 1.2 collective-permute-start.3
  32.7 0.3 collective-permute-start.5
  33.0 6.9 %collective-permute-done.19.rest_1_.rest_2_ = bf16[256,768]{1,0:T(8,128)(2,1)} collective-permute-done((bf16[256,768]{1,0:T(8,128)(2,1)}, bf16[256,768]{1,0:T(8,128)(2,1)}, u32[]{:S(2)}, u32[]{:S(2)}) %collective-permute-start.19) | collective-permute-done | bytes 393248 | tf_op jit(solution)/shard_map/ppermute | solution.py:26
  39.9 2.6 %collective-permute-start.12 = (bf16[256,768]{1,0:T(8,128)(2,1)}, bf16[256,768]{1,0:T(8,128)(2,1)S(1)}, u32[]{:S(2)}, u32[]{:S(2)}) collective-permute-start(bf16[256,768]{1,0:T(8,128)(2,1)} %get-tuple-element.51), channel_id=1, source_target_pairs={{0,3},{1,2},{2,1},{3,0},{4,7},{5,6},{6,5},{7,4},{8,11},{9,10},{10,... | collective-permute-start | bytes 1179656 | tf_op jit(solution)/shard_map/ppermute | solution.py:26
  42.5 6.9 %collective-permute-done.20.rest_2_.rest_3_ = bf16[256,768]{1,0:T(8,128)(2,1)} collective-permute-done((bf16[256,768]{1,0:T(8,128)(2,1)}, bf16[256,768]{1,0:T(8,128)(2,1)}, u32[]{:S(2)}, u32[]{:S(2)}) %collective-permute-start.20) | collective-permute-done | bytes 393248 | tf_op jit(solution)/shard_map/ppermute | solution.py:26
  49.5 2.1 %collective-permute-start.6 = (bf16[3,256,512]{2,1,0:T(8,128)(2,1)}, bf16[3,256,512]{2,1,0:T(8,128)(2,1)}, u32[]{:S(2)}, u32[]{:S(2)}) collective-permute-start(bf16[3,256,512]{2,1,0:T(8,128)(2,1)} %get-tuple-element.44), channel_id=1, source_target_pairs={{4,8},{8,4},{5,9},{9,5},{6,10},{10,6},{7,11},{11,7},{20,24},{24,20... | collective-permute-start | bytes 2359304 | tf_op jit(solution)/shard_map/ppermute | solution.py:35
  51.5 2.5 %pack_z.5 = (bf16[3,256,512]{2,1,0:T(8,128)(2,1)}, bf16[3,256,512]{2,1,0:T(8,128)(2,1)}) custom-call(bf16[256,1536]{1,0:T(8,128)(2,1)} %get-tuple-element.39.o.rest_0_, bf16[256,768]{1,0:T(8,128)(2,1)} %copy-done.5, bf16[256,768]{1,0:T(8,128)(2,1)} %collective-permute-done.19.rest_1_.rest_2_, bf16[256,768]{1,0:T(8,128)(2,1)} %collective-permute-done.20.rest_2_.rest_3_), custom_call_target="tpu_custom_call" | custom-call | bytes 2621440 | tf_op jit(solution)/shard_map/pack_z/pallas_call | solution.py:104
  54.1 3.3 %collective-permute-done.12.rest_2_.rest_3_ = bf16[256,768]{1,0:T(8,128)(2,1)S(1)} collective-permute-done((bf16[256,768]{1,0:T(8,128)(2,1)}, bf16[256,768]{1,0:T(8,128)(2,1)S(1)}, u32[]{:S(2)}, u32[]{:S(2)}) %collective-permute-start.12) | collective-permute-done | bytes 393248 | tf_op jit(solution)/shard_map/ppermute | solution.py:26
  57.3 1.3 collective-permute-start.21
  58.6 1.9 %collective-permute-start.22 = (bf16[3,256,512]{2,1,0:T(8,128)(2,1)}, bf16[3,256,512]{2,1,0:T(8,128)(2,1)}, u32[]{:S(2)}, u32[]{:S(2)}) collective-permute-start(bf16[3,256,512]{2,1,0:T(8,128)(2,1)} %get-tuple-element.62), channel_id=1, source_target_pairs={{4,8},{8,4},{5,9},{9,5},{6,10},{10,6},{7,11},{11,7},{20,24},{24,20... | collective-permute-start | bytes 2359304 | tf_op jit(solution)/shard_map/ppermute | solution.py:35
  60.6 2.4 %pack_z.4 = (bf16[3,256,512]{2,1,0:T(8,128)(2,1)}, bf16[3,256,512]{2,1,0:T(8,128)(2,1)}) custom-call(bf16[256,1536]{1,0:T(8,128)(2,1)} %get-tuple-element.39.o.rest_0_, bf16[256,768]{1,0:T(8,128)(2,1)} %copy-done.2, bf16[256,768]{1,0:T(8,128)(2,1)} %copy-done.3, bf16[256,768]{1,0:T(8,128)(2,1)} %copy-done.7), custom_call_target="tpu_custom_call" | custom-call | bytes 2621440 | tf_op jit(solution)/shard_map/pack_z/pallas_call | solution.py:104
  63.1 3.1 %collective-permute-done.5.rest_6_ = bf16[3,256,512]{2,1,0:T(8,128)(2,1)} collective-permute-done((bf16[3,256,512]{2,1,0:T(8,128)(2,1)}, bf16[3,256,512]{2,1,0:T(8,128)(2,1)}, u32[]{:S(2)}, u32[]{:S(2)}) %collective-permute-start.5) | collective-permute-done | bytes 786464 | tf_op jit(solution)/shard_map/ppermute | solution.py:35
  66.2 2.1 %collective-permute-start.14 = (bf16[3,256,512]{2,1,0:T(8,128)(2,1)}, bf16[3,256,512]{2,1,0:T(8,128)(2,1)S(1)}, u32[]{:S(2)}, u32[]{:S(2)}) collective-permute-start(bf16[3,256,512]{2,1,0:T(8,128)(2,1)} %get-tuple-element.53), channel_id=1, source_target_pairs={{4,8},{8,4},{5,9},{9,5},{6,10},{10,6},{7,11},{11,7},{20,24},{24,20... | collective-permute-start | bytes 2359304 | tf_op jit(solution)/shard_map/ppermute | solution.py:35
  68.3 2.5 %lookup_tables.1 = (bf16[2560,128]{1,0:T(8,128)(2,1)}, bf16[1024,128]{1,0:T(8,128)(2,1)}, s32[4,2]{1,0:T(4,128)}) custom-call(s32[16]{0:T(128)} %len_ref.1, s32[16,16]{1,0:T(8,128)} %mask_ref.1), custom_call_target="tpu_custom_call" | custom-call | bytes 917504 | tf_op jit(solution)/shard_map/lookup_tables/pallas_call | solution.py:171
  70.8 0.4 collective-permute-done.6.rest_7_
  71.2 10.2 %attention.3 = (bf16[256,256]{1,0:T(8,128)(2,1)}, bf16[256,256]{1,0:T(8,128)(2,1)}, bf16[256,256]{1,0:T(8,128)(2,1)}, bf16[256,256]{1,0:T(8,128)(2,1)}) custom-call(s32[4,2]{1,0:T(4,128)} %get-tuple-element.36.ranges, bf16[2560,128]{1,0:T(8,128)(2,1)} %get-tuple-element.37.bias_hbm, bf16[1024,128]{1,0:T(8,128)(2,1)} %get-tuple-element.38.onehot_hbm, ...), custom_call_target="tpu_custom_call" | custom-call | flops 2147483648 | bytes 2621440 | tf_op jit(solution)/shard_map/attention/pallas_call | solution.py:291
  81.4 4.0 %collective-permute-start.7 = (bf16[256,256]{1,0:T(8,128)(2,1)}, bf16[256,256]{1,0:T(8,128)(2,1)S(1)}, u32[]{:S(2)}, u32[]{:S(2)}) collective-permute-start(bf16[256,256]{1,0:T(8,128)(2,1)} %get-tuple-element.46), channel_id=1, source_target_pairs={{0,1},{1,0},{2,3},{3,2},{4,5},{5,4},{6,7},{7,6},{8,9},{9,8},{10,11... | collective-permute-start | bytes 393224 | tf_op jit(solution)/shard_map/ppermute | solution.py:26
  85.4 1.2 collective-permute-start.8
  86.6 1.3 %collective-permute-done.22.rest_7_ = bf16[3,256,512]{2,1,0:T(8,128)(2,1)} collective-permute-done((bf16[3,256,512]{2,1,0:T(8,128)(2,1)}, bf16[3,256,512]{2,1,0:T(8,128)(2,1)}, u32[]{:S(2)}, u32[]{:S(2)}) %collective-permute-start.22) | collective-permute-done | bytes 786464 | tf_op jit(solution)/shard_map/ppermute | solution.py:35
  88.0 1.2 collective-permute-start.9
  89.1 10.4 %attention.5 = (bf16[256,256]{1,0:T(8,128)(2,1)}, bf16[256,256]{1,0:T(8,128)(2,1)}, bf16[256,256]{1,0:T(8,128)(2,1)}, bf16[256,256]{1,0:T(8,128)(2,1)}) custom-call(s32[4,2]{1,0:T(4,128)} %get-tuple-element.36.ranges, bf16[2560,128]{1,0:T(8,128)(2,1)} %get-tuple-element.37.bias_hbm, bf16[1024,128]{1,0:T(8,128)(2,1)} %get-tuple-element.38.onehot_hbm, ...), custom_call_target="tpu_custom_call" | custom-call | flops 2147483648 | bytes 2621440 | tf_op jit(solution)/shard_map/attention/pallas_call | solution.py:291
  99.6 0.3 collective-permute-done.13.rest_6_
  99.8 2.2 %collective-permute-start.23 = (bf16[256,256]{1,0:T(8,128)(2,1)}, bf16[256,256]{1,0:T(8,128)(2,1)S(1)}, u32[]{:S(2)}, u32[]{:S(2)}) collective-permute-start(bf16[256,256]{1,0:T(8,128)(2,1)} %get-tuple-element.64), channel_id=1, source_target_pairs={{0,1},{1,0},{2,3},{3,2},{4,5},{5,4},{6,7},{7,6},{8,9},{9,8},{10,11... | collective-permute-start | bytes 393224 | tf_op jit(solution)/shard_map/ppermute | solution.py:26
  102.0 2.6 %collective-permute-done.14.rest_7_ = bf16[3,256,512]{2,1,0:T(8,128)(2,1)S(1)} collective-permute-done((bf16[3,256,512]{2,1,0:T(8,128)(2,1)}, bf16[3,256,512]{2,1,0:T(8,128)(2,1)S(1)}, u32[]{:S(2)}, u32[]{:S(2)}) %collective-permute-start.14) | collective-permute-done | bytes 786464 | tf_op jit(solution)/shard_map/ppermute | solution.py:35
  104.6 1.0 collective-permute-start.24
  105.6 10.2 %attention.4 = (bf16[256,256]{1,0:T(8,128)(2,1)}, bf16[256,256]{1,0:T(8,128)(2,1)}, bf16[256,256]{1,0:T(8,128)(2,1)}, bf16[256,256]{1,0:T(8,128)(2,1)}) custom-call(s32[4,2]{1,0:T(4,128)} %get-tuple-element.36.ranges, bf16[2560,128]{1,0:T(8,128)(2,1)} %get-tuple-element.37.bias_hbm, bf16[1024,128]{1,0:T(8,128)(2,1)} %get-tuple-element.38.onehot_hbm, ...), custom_call_target="tpu_custom_call" | custom-call | flops 2147483648 | bytes 2621440 | tf_op jit(solution)/shard_map/attention/pallas_call | solution.py:291
  115.9 1.2 collective-permute-start.25
  117.2 0.9 collective-permute-start.16
  118.0 1.2 collective-permute-start.17
  119.2 2.8 %collective-permute-done.25.refs_11_ = bf16[256,256]{1,0:T(8,128)(2,1)S(1)} collective-permute-done((bf16[256,256]{1,0:T(8,128)(2,1)S(1)}, bf16[256,256]{1,0:T(8,128)(2,1)S(1)}, u32[]{:S(2)}, u32[]{:S(2)}) %collective-permute-start.25) | collective-permute-done | bytes 131104 | tf_op jit(solution)/shard_map/ppermute | solution.py:26
  122.0 2.8 %collective-permute-done.16.refs_6_ = bf16[256,256]{1,0:T(8,128)(2,1)S(1)} collective-permute-done((bf16[256,256]{1,0:T(8,128)(2,1)}, bf16[256,256]{1,0:T(8,128)(2,1)S(1)}, u32[]{:S(2)}, u32[]{:S(2)}) %collective-permute-start.16) | collective-permute-done | bytes 131104 | tf_op jit(solution)/shard_map/ppermute | solution.py:26
  124.8 2.8 %collective-permute-done.17.refs_7_ = bf16[256,256]{1,0:T(8,128)(2,1)S(1)} collective-permute-done((bf16[256,256]{1,0:T(8,128)(2,1)}, bf16[256,256]{1,0:T(8,128)(2,1)S(1)}, u32[]{:S(2)}, u32[]{:S(2)}) %collective-permute-start.17) | collective-permute-done | bytes 131104 | tf_op jit(solution)/shard_map/ppermute | solution.py:26
  127.6 0.6 copy-done.16
  128.2 2.7 %gather_out.1 = bf16[256,3072]{1,0:T(8,128)(2,1)} custom-call(bf16[256,256]{1,0:T(8,128)(2,1)} %get-tuple-element.45.refs_0_, bf16[256,256]{1,0:T(8,128)(2,1)} %copy-done.8, bf16[256,256]{1,0:T(8,128)(2,1)} %copy-done.9, bf16[256,256]{1,0:T(8,128)(2,1)} %copy-done.10, bf16[256,256]{1,0:T(8,128)(2,1)} %get-tuple-element.54.refs_4_, ...), custom_call_target="tpu_custom_call" | custom-call | bytes 3145728 | tf_op jit(solution)/shard_map/gather_out/pallas_call | solution.py:325
  (56 shorter events, 0.5 us)
Async XLA Ops:
  3.0 7.2 %collective-permute-start = (bf16[256,768]{1,0:T(8,128)(2,1)}, bf16[256,768]{1,0:T(8,128)(2,1)S(1)}, u32[]{:S(2)}, u32[]{:S(2)}) collective-permute-start(bf16[256,768]{1,0:T(8,128)(2,1)} %get-tuple-element.40), channel_id=1, source_target_pairs={{0,1},{1,0},{2,3},{3,2},{4,5},{5,4},{6,7},{7,6},{8,9},{9,8},{10,11... | collective-permute-start | bytes 1179656 | tf_op jit(solution)/shard_map/ppermute | solution.py:26
  3.8 10.8 %collective-permute-start.1 = (bf16[256,768]{1,0:T(8,128)(2,1)}, bf16[256,768]{1,0:T(8,128)(2,1)S(1)}, u32[]{:S(2)}, u32[]{:S(2)}) collective-permute-start(bf16[256,768]{1,0:T(8,128)(2,1)} %get-tuple-element.41), channel_id=1, source_target_pairs={{0,2},{1,3},{2,0},{3,1},{4,6},{5,7},{6,4},{7,5},{8,10},{9,11},{10,... | collective-permute-start | bytes 1179656 | tf_op jit(solution)/shard_map/ppermute | solution.py:26
  5.0 18.9 %copy-start = (bf16[256,1536]{1,0:T(8,128)(2,1)S(1)}, bf16[256,1536]{1,0:T(8,128)(2,1)}, u32[]{:S(2)}) copy-start(bf16[256,1536]{1,0:T(8,128)(2,1)} %get-tuple-element.39.o.rest_0_) | copy-start | bytes 2359300
  5.0 18.9 %collective-permute-start.2 = (bf16[256,768]{1,0:T(8,128)(2,1)}, bf16[256,768]{1,0:T(8,128)(2,1)}, u32[]{:S(2)}, u32[]{:S(2)}) collective-permute-start(bf16[256,768]{1,0:T(8,128)(2,1)} %get-tuple-element.42), channel_id=1, source_target_pairs={{0,3},{1,2},{2,1},{3,0},{4,7},{5,6},{6,5},{7,4},{8,11},{9,10},{10,... | collective-permute-start | bytes 1179656 | tf_op jit(solution)/shard_map/ppermute | solution.py:26
  8.8 22.8 %copy-start.1 = (bf16[256,1536]{1,0:T(8,128)(2,1)S(1)}, bf16[256,1536]{1,0:T(8,128)(2,1)}, u32[]{:S(2)}) copy-start(bf16[256,1536]{1,0:T(8,128)(2,1)} %get-tuple-element.39.o.rest_0_) | copy-start | bytes 2359300
  8.8 17.2 %collective-permute-start.10 = (bf16[256,768]{1,0:T(8,128)(2,1)}, bf16[256,768]{1,0:T(8,128)(2,1)S(1)}, u32[]{:S(2)}, u32[]{:S(2)}) collective-permute-start(bf16[256,768]{1,0:T(8,128)(2,1)} %get-tuple-element.49), channel_id=1, source_target_pairs={{0,1},{1,0},{2,3},{3,2},{4,5},{5,4},{6,7},{7,6},{8,9},{9,8},{10,11... | collective-permute-start | bytes 1179656 | tf_op jit(solution)/shard_map/ppermute | solution.py:26
  9.0 22.5 %collective-permute-start.11 = (bf16[256,768]{1,0:T(8,128)(2,1)}, bf16[256,768]{1,0:T(8,128)(2,1)S(1)}, u32[]{:S(2)}, u32[]{:S(2)}) collective-permute-start(bf16[256,768]{1,0:T(8,128)(2,1)} %get-tuple-element.50), channel_id=1, source_target_pairs={{0,2},{1,3},{2,0},{3,1},{4,6},{5,7},{6,4},{7,5},{8,10},{9,11},{10,... | collective-permute-start | bytes 1179656 | tf_op jit(solution)/shard_map/ppermute | solution.py:26
  10.2 16.8 %copy-start.4 = (bf16[256,768]{1,0:T(8,128)(2,1)}, bf16[256,768]{1,0:T(8,128)(2,1)S(1)}, u32[]{:S(2)}) copy-start(bf16[256,768]{1,0:T(8,128)(2,1)S(1)} %collective-permute-done.rest_0_.rest_1_) | copy-start | bytes 1179652
  10.2 22.5 %collective-permute-start.18 = (bf16[256,768]{1,0:T(8,128)(2,1)}, bf16[256,768]{1,0:T(8,128)(2,1)S(1)}, u32[]{:S(2)}, u32[]{:S(2)}) collective-permute-start(bf16[256,768]{1,0:T(8,128)(2,1)} %get-tuple-element.58), channel_id=1, source_target_pairs={{0,1},{1,0},{2,3},{3,2},{4,5},{5,4},{6,7},{7,6},{8,9},{9,8},{10,11... | collective-permute-start | bytes 1179656 | tf_op jit(solution)/shard_map/ppermute | solution.py:26
  14.6 12.5 %copy-start.6 = (bf16[256,768]{1,0:T(8,128)(2,1)}, bf16[256,768]{1,0:T(8,128)(2,1)S(1)}, u32[]{:S(2)}) copy-start(bf16[256,768]{1,0:T(8,128)(2,1)S(1)} %collective-permute-done.1.rest_1_.rest_2_) | copy-start | bytes 1179652
  14.6 25.4 %collective-permute-start.19 = (bf16[256,768]{1,0:T(8,128)(2,1)}, bf16[256,768]{1,0:T(8,128)(2,1)}, u32[]{:S(2)}, u32[]{:S(2)}) collective-permute-start(bf16[256,768]{1,0:T(8,128)(2,1)} %get-tuple-element.59), channel_id=1, source_target_pairs={{0,2},{1,3},{2,0},{3,1},{4,6},{5,7},{6,4},{7,5},{8,10},{9,11},{10,... | collective-permute-start | bytes 1179656 | tf_op jit(solution)/shard_map/ppermute | solution.py:26
  23.9 34.8 %collective-permute-start.4 = (bf16[256,1536]{1,0:T(8,128)(2,1)S(1)}, bf16[256,1536]{1,0:T(8,128)(2,1)}, u32[]{:S(2)}, u32[]{:S(2)}) collective-permute-start(bf16[256,1536]{1,0:T(8,128)(2,1)S(1)} %copy-done), channel_id=1, source_target_pairs={{4,8},{8,4},{5,9},{9,5},{6,10},{10,6},{7,11},{11,7},{20,24},{24,20... | collective-permute-start | bytes 2359304 | tf_op jit(solution)/shard_map/ppermute | solution.py:35
  26.0 28.1 %copy-start.2 = (bf16[256,768]{1,0:T(8,128)(2,1)}, bf16[256,768]{1,0:T(8,128)(2,1)S(1)}, u32[]{:S(2)}) copy-start(bf16[256,768]{1,0:T(8,128)(2,1)S(1)} %collective-permute-done.10.rest_0_.rest_1_) | copy-start | bytes 1179652
  26.0 23.5 %collective-permute-start.20 = (bf16[256,768]{1,0:T(8,128)(2,1)}, bf16[256,768]{1,0:T(8,128)(2,1)}, u32[]{:S(2)}, u32[]{:S(2)}) collective-permute-start(bf16[256,768]{1,0:T(8,128)(2,1)} %get-tuple-element.60), channel_id=1, source_target_pairs={{0,3},{1,2},{2,1},{3,0},{4,7},{5,6},{6,5},{7,4},{8,11},{9,10},{10,... | collective-permute-start | bytes 1179656 | tf_op jit(solution)/shard_map/ppermute | solution.py:26
  31.5 29.0 %copy-start.3 = (bf16[256,768]{1,0:T(8,128)(2,1)}, bf16[256,768]{1,0:T(8,128)(2,1)S(1)}, u32[]{:S(2)}) copy-start(bf16[256,768]{1,0:T(8,128)(2,1)S(1)} %collective-permute-done.11.rest_1_.rest_2_) | copy-start | bytes 1179652
  31.5 31.5 %collective-permute-start.3 = (bf16[256,1536]{1,0:T(8,128)(2,1)S(1)}, bf16[256,1536]{1,0:T(8,128)(2,1)}, u32[]{:S(2)}, u32[]{:S(2)}) collective-permute-start(bf16[256,1536]{1,0:T(8,128)(2,1)S(1)} %copy-done.1), channel_id=1, source_target_pairs={{0,4},{4,0},{1,5},{5,1},{2,6},{6,2},{3,7},{7,3},{8,12},{12,8},{9,1... | collective-permute-start | bytes 2359304 | tf_op jit(solution)/shard_map/ppermute | solution.py:35
  32.7 18.8 %copy-start.5 = (bf16[256,768]{1,0:T(8,128)(2,1)}, bf16[256,768]{1,0:T(8,128)(2,1)S(1)}, u32[]{:S(2)}) copy-start(bf16[256,768]{1,0:T(8,128)(2,1)S(1)} %collective-permute-done.18.rest_0_.rest_1_) | copy-start | bytes 1179652
  32.7 33.5 %collective-permute-start.5 = (bf16[3,256,512]{2,1,0:T(8,128)(2,1)}, bf16[3,256,512]{2,1,0:T(8,128)(2,1)}, u32[]{:S(2)}, u32[]{:S(2)}) collective-permute-start(bf16[3,256,512]{2,1,0:T(8,128)(2,1)} %get-tuple-element.43), channel_id=1, source_target_pairs={{0,4},{4,0},{1,5},{5,1},{2,6},{6,2},{3,7},{7,3},{8,12},{12,8},{9,1... | collective-permute-start | bytes 2359304 | tf_op jit(solution)/shard_map/ppermute | solution.py:35
  39.9 17.4 %collective-permute-start.12 = (bf16[256,768]{1,0:T(8,128)(2,1)}, bf16[256,768]{1,0:T(8,128)(2,1)S(1)}, u32[]{:S(2)}, u32[]{:S(2)}) collective-permute-start(bf16[256,768]{1,0:T(8,128)(2,1)} %get-tuple-element.51), channel_id=1, source_target_pairs={{0,3},{1,2},{2,1},{3,0},{4,7},{5,6},{6,5},{7,4},{8,11},{9,10},{10,... | collective-permute-start | bytes 1179656 | tf_op jit(solution)/shard_map/ppermute | solution.py:26
  49.5 21.8 %collective-permute-start.6 = (bf16[3,256,512]{2,1,0:T(8,128)(2,1)}, bf16[3,256,512]{2,1,0:T(8,128)(2,1)}, u32[]{:S(2)}, u32[]{:S(2)}) collective-permute-start(bf16[3,256,512]{2,1,0:T(8,128)(2,1)} %get-tuple-element.44), channel_id=1, source_target_pairs={{4,8},{8,4},{5,9},{9,5},{6,10},{10,6},{7,11},{11,7},{20,24},{24,20... | collective-permute-start | bytes 2359304 | tf_op jit(solution)/shard_map/ppermute | solution.py:35
  57.3 3.2 %copy-start.7 = (bf16[256,768]{1,0:T(8,128)(2,1)}, bf16[256,768]{1,0:T(8,128)(2,1)S(1)}, u32[]{:S(2)}) copy-start(bf16[256,768]{1,0:T(8,128)(2,1)S(1)} %collective-permute-done.12.rest_2_.rest_3_) | copy-start | bytes 1179652
  57.3 28.0 %collective-permute-start.21 = (bf16[3,256,512]{2,1,0:T(8,128)(2,1)}, bf16[3,256,512]{2,1,0:T(8,128)(2,1)S(1)}, u32[]{:S(2)}, u32[]{:S(2)}) collective-permute-start(bf16[3,256,512]{2,1,0:T(8,128)(2,1)} %get-tuple-element.61), channel_id=1, source_target_pairs={{0,4},{4,0},{1,5},{5,1},{2,6},{6,2},{3,7},{7,3},{8,12},{12,8},{9,1... | collective-permute-start | bytes 2359304 | tf_op jit(solution)/shard_map/ppermute | solution.py:35
  58.6 29.3 %collective-permute-start.22 = (bf16[3,256,512]{2,1,0:T(8,128)(2,1)}, bf16[3,256,512]{2,1,0:T(8,128)(2,1)}, u32[]{:S(2)}, u32[]{:S(2)}) collective-permute-start(bf16[3,256,512]{2,1,0:T(8,128)(2,1)} %get-tuple-element.62), channel_id=1, source_target_pairs={{4,8},{8,4},{5,9},{9,5},{6,10},{10,6},{7,11},{11,7},{20,24},{24,20... | collective-permute-start | bytes 2359304 | tf_op jit(solution)/shard_map/ppermute | solution.py:35
  63.0 36.8 %collective-permute-start.13 = (bf16[3,256,512]{2,1,0:T(8,128)(2,1)}, bf16[3,256,512]{2,1,0:T(8,128)(2,1)S(1)}, u32[]{:S(2)}, u32[]{:S(2)}) collective-permute-start(bf16[3,256,512]{2,1,0:T(8,128)(2,1)} %get-tuple-element.52), channel_id=1, source_target_pairs={{0,4},{4,0},{1,5},{5,1},{2,6},{6,2},{3,7},{7,3},{8,12},{12,8},{9,1... | collective-permute-start | bytes 2359304 | tf_op jit(solution)/shard_map/ppermute | solution.py:35
  66.2 38.4 %collective-permute-start.14 = (bf16[3,256,512]{2,1,0:T(8,128)(2,1)}, bf16[3,256,512]{2,1,0:T(8,128)(2,1)S(1)}, u32[]{:S(2)}, u32[]{:S(2)}) collective-permute-start(bf16[3,256,512]{2,1,0:T(8,128)(2,1)} %get-tuple-element.53), channel_id=1, source_target_pairs={{4,8},{8,4},{5,9},{9,5},{6,10},{10,6},{7,11},{11,7},{20,24},{24,20... | collective-permute-start | bytes 2359304 | tf_op jit(solution)/shard_map/ppermute | solution.py:35
  81.4 34.4 %collective-permute-start.7 = (bf16[256,256]{1,0:T(8,128)(2,1)}, bf16[256,256]{1,0:T(8,128)(2,1)S(1)}, u32[]{:S(2)}, u32[]{:S(2)}) collective-permute-start(bf16[256,256]{1,0:T(8,128)(2,1)} %get-tuple-element.46), channel_id=1, source_target_pairs={{0,1},{1,0},{2,3},{3,2},{4,5},{5,4},{6,7},{7,6},{8,9},{9,8},{10,11... | collective-permute-start | bytes 393224 | tf_op jit(solution)/shard_map/ppermute | solution.py:26
  85.4 3.7 %copy-start.19 = (bf16[3,256,512]{2,1,0:T(8,128)(2,1)}, bf16[3,256,512]{2,1,0:T(8,128)(2,1)S(1)}, u32[]{:S(2)}) copy-start(bf16[3,256,512]{2,1,0:T(8,128)(2,1)S(1)} %collective-permute-done.21.rest_6_) | copy-start | bytes 2359300
  85.4 31.7 %collective-permute-start.8 = (bf16[256,256]{1,0:T(8,128)(2,1)}, bf16[256,256]{1,0:T(8,128)(2,1)S(1)}, u32[]{:S(2)}, u32[]{:S(2)}) collective-permute-start(bf16[256,256]{1,0:T(8,128)(2,1)} %get-tuple-element.47), channel_id=1, source_target_pairs={{0,2},{1,3},{2,0},{3,1},{4,6},{5,7},{6,4},{7,5},{8,10},{9,11},{10,... | collective-permute-start | bytes 393224 | tf_op jit(solution)/shard_map/ppermute | solution.py:26
  88.0 29.2 %collective-permute-start.9 = (bf16[256,256]{1,0:T(8,128)(2,1)}, bf16[256,256]{1,0:T(8,128)(2,1)S(1)}, u32[]{:S(2)}, u32[]{:S(2)}) collective-permute-start(bf16[256,256]{1,0:T(8,128)(2,1)} %get-tuple-element.48), channel_id=1, source_target_pairs={{0,3},{1,2},{2,1},{3,0},{4,7},{5,6},{6,5},{7,4},{8,11},{9,10},{10,... | collective-permute-start | bytes 393224 | tf_op jit(solution)/shard_map/ppermute | solution.py:26
  99.8 5.8 %copy-start.17 = (bf16[3,256,512]{2,1,0:T(8,128)(2,1)}, bf16[3,256,512]{2,1,0:T(8,128)(2,1)S(1)}, u32[]{:S(2)}) copy-start(bf16[3,256,512]{2,1,0:T(8,128)(2,1)S(1)} %collective-permute-done.13.rest_6_) | copy-start | bytes 2359300
  99.8 18.2 %collective-permute-start.23 = (bf16[256,256]{1,0:T(8,128)(2,1)}, bf16[256,256]{1,0:T(8,128)(2,1)S(1)}, u32[]{:S(2)}, u32[]{:S(2)}) collective-permute-start(bf16[256,256]{1,0:T(8,128)(2,1)} %get-tuple-element.64), channel_id=1, source_target_pairs={{0,1},{1,0},{2,3},{3,2},{4,5},{5,4},{6,7},{7,6},{8,9},{9,8},{10,11... | collective-permute-start | bytes 393224 | tf_op jit(solution)/shard_map/ppermute | solution.py:26
  104.6 1.0 copy-start.18
  104.6 11.2 %copy-start.20 = (bf16[256,256]{1,0:T(8,128)(2,1)S(1)}, bf16[256,256]{1,0:T(8,128)(2,1)}, u32[]{:S(2)}) copy-start(bf16[256,256]{1,0:T(8,128)(2,1)} %get-tuple-element.66) | copy-start | bytes 393220
  104.6 14.6 %collective-permute-start.24 = (bf16[256,256]{1,0:T(8,128)(2,1)}, bf16[256,256]{1,0:T(8,128)(2,1)S(1)}, u32[]{:S(2)}, u32[]{:S(2)}) collective-permute-start(bf16[256,256]{1,0:T(8,128)(2,1)} %get-tuple-element.65), channel_id=1, source_target_pairs={{0,2},{1,3},{2,0},{3,1},{4,6},{5,7},{6,4},{7,5},{8,10},{9,11},{10,... | collective-permute-start | bytes 393224 | tf_op jit(solution)/shard_map/ppermute | solution.py:26
  115.8 11.7 %copy-start.8 = (bf16[256,256]{1,0:T(8,128)(2,1)}, bf16[256,256]{1,0:T(8,128)(2,1)S(1)}, u32[]{:S(2)}) copy-start(bf16[256,256]{1,0:T(8,128)(2,1)S(1)} %collective-permute-done.7.refs_1_) | copy-start | bytes 393220
  115.9 6.1 %collective-permute-start.25 = (bf16[256,256]{1,0:T(8,128)(2,1)S(1)}, bf16[256,256]{1,0:T(8,128)(2,1)S(1)}, u32[]{:S(2)}, u32[]{:S(2)}) collective-permute-start(bf16[256,256]{1,0:T(8,128)(2,1)S(1)} %copy-done.20), channel_id=1, source_target_pairs={{0,3},{1,2},{2,1},{3,0},{4,7},{5,6},{6,5},{7,4},{8,11},{9,10},{10,... | collective-permute-start | bytes 393224 | tf_op jit(solution)/shard_map/ppermute | solution.py:26
  117.0 10.5 %copy-start.9 = (bf16[256,256]{1,0:T(8,128)(2,1)}, bf16[256,256]{1,0:T(8,128)(2,1)S(1)}, u32[]{:S(2)}) copy-start(bf16[256,256]{1,0:T(8,128)(2,1)S(1)} %collective-permute-done.8.refs_2_) | copy-start | bytes 393220
  117.0 4.9 %collective-permute-start.15 = (bf16[256,256]{1,0:T(8,128)(2,1)}, bf16[256,256]{1,0:T(8,128)(2,1)S(1)}, u32[]{:S(2)}, u32[]{:S(2)}) collective-permute-start(bf16[256,256]{1,0:T(8,128)(2,1)} %get-tuple-element.55), channel_id=1, source_target_pairs={{0,1},{1,0},{2,3},{3,2},{4,5},{5,4},{6,7},{7,6},{8,9},{9,8},{10,11... | collective-permute-start | bytes 393224 | tf_op jit(solution)/shard_map/ppermute | solution.py:26
  117.2 10.4 %copy-start.10 = (bf16[256,256]{1,0:T(8,128)(2,1)}, bf16[256,256]{1,0:T(8,128)(2,1)S(1)}, u32[]{:S(2)}) copy-start(bf16[256,256]{1,0:T(8,128)(2,1)S(1)} %collective-permute-done.9.refs_3_) | copy-start | bytes 393220
  117.2 7.6 %collective-permute-start.16 = (bf16[256,256]{1,0:T(8,128)(2,1)}, bf16[256,256]{1,0:T(8,128)(2,1)S(1)}, u32[]{:S(2)}, u32[]{:S(2)}) collective-permute-start(bf16[256,256]{1,0:T(8,128)(2,1)} %get-tuple-element.56), channel_id=1, source_target_pairs={{0,2},{1,3},{2,0},{3,1},{4,6},{5,7},{6,4},{7,5},{8,10},{9,11},{10,... | collective-permute-start | bytes 393224 | tf_op jit(solution)/shard_map/ppermute | solution.py:26
  118.0 9.6 %copy-start.11 = (bf16[256,256]{1,0:T(8,128)(2,1)}, bf16[256,256]{1,0:T(8,128)(2,1)S(1)}, u32[]{:S(2)}) copy-start(bf16[256,256]{1,0:T(8,128)(2,1)S(1)} %collective-permute-done.23.refs_9_) | copy-start | bytes 393220
  118.0 9.5 %collective-permute-start.17 = (bf16[256,256]{1,0:T(8,128)(2,1)}, bf16[256,256]{1,0:T(8,128)(2,1)S(1)}, u32[]{:S(2)}, u32[]{:S(2)}) collective-permute-start(bf16[256,256]{1,0:T(8,128)(2,1)} %get-tuple-element.57), channel_id=1, source_target_pairs={{0,3},{1,2},{2,1},{3,0},{4,7},{5,6},{6,5},{7,4},{8,11},{9,10},{10,... | collective-permute-start | bytes 393224 | tf_op jit(solution)/shard_map/ppermute | solution.py:26
  119.2 8.4 %copy-start.12 = (bf16[256,256]{1,0:T(8,128)(2,1)}, bf16[256,256]{1,0:T(8,128)(2,1)S(1)}, u32[]{:S(2)}) copy-start(bf16[256,256]{1,0:T(8,128)(2,1)S(1)} %collective-permute-done.24.refs_10_) | copy-start | bytes 393220
  122.0 5.7 %copy-start.13 = (bf16[256,256]{1,0:T(8,128)(2,1)}, bf16[256,256]{1,0:T(8,128)(2,1)S(1)}, u32[]{:S(2)}) copy-start(bf16[256,256]{1,0:T(8,128)(2,1)S(1)} %collective-permute-done.25.refs_11_) | copy-start | bytes 393220
  122.0 5.7 %copy-start.14 = (bf16[256,256]{1,0:T(8,128)(2,1)}, bf16[256,256]{1,0:T(8,128)(2,1)S(1)}, u32[]{:S(2)}) copy-start(bf16[256,256]{1,0:T(8,128)(2,1)S(1)} %collective-permute-done.15.refs_5_) | copy-start | bytes 393220
  124.8 2.9 %copy-start.15 = (bf16[256,256]{1,0:T(8,128)(2,1)}, bf16[256,256]{1,0:T(8,128)(2,1)S(1)}, u32[]{:S(2)}) copy-start(bf16[256,256]{1,0:T(8,128)(2,1)S(1)} %collective-permute-done.16.refs_6_) | copy-start | bytes 393220
  127.6 0.6 copy-start.16

commit v2 on v1

--- a/solution.py
+++ b/solution.py
@@ -28,11 +28,11 @@
 
 def swap_levels(value, parity):
     count = lax.axis_size("ctx")
-    pairs = []
+    pairs = {i: i ^ 1 for i in range(count)}
     for low in range(parity * LEVEL, count - LEVEL, 2 * LEVEL):
         for i in range(low, low + LEVEL):
-            pairs += [(i, i + LEVEL), (i + LEVEL, i)]
-    return lax.ppermute(value, "ctx", pairs)
+            pairs[i], pairs[i + LEVEL] = i + LEVEL, i
+    return lax.ppermute(value, "ctx", sorted(pairs.items()))
 
 
 def run_copies(pairs, sems):
@@ -153,6 +153,12 @@
                 tiles = jnp.where(ranges[b, 1] - start <= size * TILE, size, tiles)
             ranges[b, 0] = jnp.minimum(start, key_rows - tiles * TILE)
             ranges[b, 1] = tiles
+        low, high = jnp.int32(key_rows), jnp.int32(0)
+        for b in range(LEVEL):
+            low = jnp.minimum(low, ranges[b, 0])
+            high = jnp.maximum(high, ranges[b, 0] + ranges[b, 1] * TILE)
+        ranges[LEVEL, 0] = low // rows
+        ranges[LEVEL, 1] = (high + rows - 1) // rows
 
         @pl.loop(0, key_blocks)
         def _(i):
@@ -173,7 +179,7 @@
         out_shape=[
             jax.ShapeDtypeStruct((key_rows, lanes), bf),
             jax.ShapeDtypeStruct((query_rows, lanes), bf),
-            jax.ShapeDtypeStruct((LEVEL, 2), jnp.int32),
+            jax.ShapeDtypeStruct((LEVEL + 1, 2), jnp.int32),
         ],
         in_specs=[SMEM, SMEM],
         out_specs=[VMEM, VMEM, SMEM],
@@ -182,17 +188,20 @@
     )(lengths, mask)
 
 
-def attention(tables, queries, own, swapped, own_far, far, ahead, offset, width, slab):
+def attention(
+    tables, queries, own, swapped, q_swapped, own_far, far, ahead, offset, width, q_offset, slab
+):
     rows = queries.shape[0]
     heads = width // HEAD
     key_blocks = 2 * LEVEL + ahead
     key_rows = key_blocks * rows
     lanes = tables[0].shape[1]
     factor = math.log2(math.e) / math.sqrt(HEAD)
-    n_copies = 2 + 2 * key_blocks + LEVEL
+    n_copies = 2 * key_blocks + 2 + LEVEL
 
     def kernel(ranges, bias_hbm, onehot_hbm, q, *rest):
         level, rest = rest[:LEVEL], rest[LEVEL:]
+        asked, rest = rest[: LEVEL - 1], rest[LEVEL - 1 :]
         own_sides, sides, rest = rest[:2], rest[2:4], rest[4:]
         outs, scratch = rest[:LEVEL], rest[LEVEL:]
         ks, vs, vt, qs, os, bias, onehot, sems, out_sems = scratch
@@ -202,23 +211,30 @@
 
         def kv(src, block, off=0):
             at = pl.ds(pl.multiple_of(block * rows, rows), rows)
-            return [
-                (src.at[:, pl.ds(off, width)], ks.at[at, :]),
-                (src.at[:, pl.ds(off + width, width)], vs.at[at, :]),
-            ]
-
-        pairs = [(bias_hbm, bias), (onehot_hbm, onehot)]
+            value = pltpu.make_async_copy(
+                src.at[:, pl.ds(off + width, width)], vs.at[at, :], sems.at[block]
+            )
+            key = pltpu.make_async_copy(
+                src.at[:, pl.ds(off, width)], ks.at[at, :], sems.at[key_blocks + block]
+            )
+            return [value, key]
+
+        def level_copies():
+            copies = []
+            for d in range(LEVEL):
+                copies += kv(level[d], LEVEL + (j ^ d), 2 * offset if d == 0 else 0)
+            return copies
+
+        rest_pairs = [(bias_hbm, bias), (onehot_hbm, onehot)]
         for d in range(LEVEL):
-            pairs += kv(level[d], LEVEL + (j ^ d), 2 * offset if d == 0 else 0)
             at = pl.ds(pl.multiple_of((j ^ d) * rows, rows), rows)
             if d == 0:
                 c = pl.multiple_of(j * slab + offset, HEAD)
-                pairs.append((q.at[:, pl.ds(c, width)], qs.at[at, :]))
+                rest_pairs.append((q.at[:, pl.ds(c, width)], qs.at[at, :]))
             else:
-                pairs.append((level[d].at[:, pl.ds(2 * width, width)], qs.at[at, :]))
-        near = len(pairs)
-
-        def side_pairs(parity):
+                rest_pairs.append((asked[d - 1].at[:, pl.ds(q_offset, width)], qs.at[at, :]))
+
+        def side_copies(parity):
             behind, front = 1 - parity, parity
             out = kv(own_sides[behind], j, 2 * offset)
             for d in range(1, LEVEL):
@@ -227,28 +243,41 @@
                 out += kv(sides[front].at[b], 2 * LEVEL + b)
             return out
 
-        copies = [pltpu.make_async_copy(a, b, sems.at[n]) for n, (a, b) in enumerate(pairs)]
-        for c in copies:
+        near = level_copies()
+        rest = [
+            pltpu.make_async_copy(a, b, sems.at[2 * key_blocks + n])
+            for n, (a, b) in enumerate(rest_pairs)
+        ]
+        for part in range(2):
+            for c in near[part::2]:
+                c.start()
+            for parity in range(2):
+                @pl.when(odd == parity)
+                def _():
+                    for c in side_copies(parity)[part::2]:
+                        c.start()
+        for c in rest:
             c.start()
-        for parity in range(2):
-            @pl.when(odd == parity)
-            def _():
-                for n, (a, b) in enumerate(side_pairs(parity)):
-                    pltpu.make_async_copy(a, b, sems.at[near + n]).start()
-        copies += [
-            pltpu.make_async_copy(a, b, sems.at[near + n])
-            for n, (a, b) in enumerate(side_pairs(0))
-        ]
-        for c in copies:
-            c.wait()
         for h in range(heads):
             vt[h, HEAD:, :] = jnp.ones_like(vt[h, HEAD:, :])
 
-        @pl.loop(0, key_rows // TILE)
+        @pl.loop(0, key_blocks)
         def _(i):
-            at = pl.ds(pl.multiple_of(i * TILE, TILE), TILE)
-            for h in range(heads):
-                vt[h, :HEAD, at] = vs[at, h * HEAD : (h + 1) * HEAD].T
+            at = pl.ds(pl.multiple_of(i * rows, rows), rows)
+            pltpu.make_async_copy(ks.at[at, :], vs.at[at, :], sems.at[i]).wait()
+
+            @pl.when((i >= ranges[LEVEL, 0]) & (i < ranges[LEVEL, 1]))
+            def _():
+                for h in range(heads):
+                    vt[h, :HEAD, at] = vs[at, h * HEAD : (h + 1) * HEAD].T
+
+        @pl.loop(0, key_blocks)
+        def _(i):
+            at = pl.ds(pl.multiple_of(i * rows, rows), rows)
+            pltpu.make_async_copy(vs.at[at, :], ks.at[at, :], sems.at[key_blocks + i]).wait()
+
+        for c in rest:
+            c.wait()
 
         @pl.loop(0, LEVEL)
         def _(b):
@@ -291,7 +320,7 @@
     return pl.pallas_call(
         kernel,
         out_shape=[jax.ShapeDtypeStruct((rows, width), bf)] * LEVEL,
-        in_specs=[SMEM] + [HBM] * (LEVEL + 7),
+        in_specs=[SMEM] + [HBM] * (2 * LEVEL + 6),
         out_specs=[HBM] * LEVEL,
         scratch_shapes=[
             pltpu.VMEM((key_rows, width), bf),
@@ -306,7 +335,7 @@
         ],
         cost_estimate=cost(4 * key_rows * width, 8 * LEVEL * rows * 1024 * width),
         name="attention",
-    )(ranges, bias, onehot, queries, own, *swapped, *own_far, *far)
+    )(ranges, bias, onehot, queries, own, *swapped, *q_swapped, *own_far, *far)
 
 
 def gather_out(pieces, rows, slab, dtype):
@@ -345,15 +374,21 @@
     groups = range(len(SPLIT))
     arrays = (key_states, value_states, queries)
     tables = lookup_tables(stretch_lengths, stretch_mask, rows, 2 * LEVEL + ahead)
-    slabs = [[(i, slab, offsets[g], widths[g]) for i in range(3)] for g in groups]
-    own_spans = [span for spans in slabs for span in spans[:2]]
-    jobs = [(d, slabs[0]) for d in OTHERS] + [(0, own_spans)]
+
+    def spans(kinds, g):
+        return [(i, slab, offsets[g], widths[g]) for i in kinds]
+
+    messages = [spans((0, 1), 0)]
+    messages += [spans((0, 1), g) + spans((2,), g - 1) for g in groups[1:]]
+    messages += [spans((2,), groups[-1])]
+    own_spans = [span for g in groups for span in spans((0, 1), g)]
+    jobs = [(d, messages[0]) for d in OTHERS] + [(0, own_spans)]
     *parts, own = pack_columns(arrays, jobs)
-    jobs = [(d, slabs[g]) for g in groups[1:] for d in OTHERS]
+    jobs = [(d, message) for message in messages[1:] for d in OTHERS]
     parts += pack_columns(arrays, jobs)
     swapped, far = [], []
-    for g in groups:
-        mine = parts[g * len(OTHERS) : (g + 1) * len(OTHERS)]
+    for m in range(len(messages)):
+        mine = parts[m * len(OTHERS) : (m + 1) * len(OTHERS)]
         swapped.append([swap(x, d) for x, d in zip(mine, OTHERS)])
     own_far = [swap_levels(own, p) for p in range(2)]
     for g in groups:
@@ -362,8 +397,8 @@
     pieces = []
     for g in groups:
         outs = attention(
-            tables, queries, own, swapped[g], own_far, far[g], ahead,
-            offsets[g], widths[g], slab,
+            tables, queries, own, swapped[g], swapped[g + 1], own_far, far[g], ahead,
+            offsets[g], widths[g], 2 * widths[g + 1] if g < groups[-1] else 0, slab,
         )
         pieces += [outs[0]]
         pieces += [swap(outs[d], d) for d in OTHERS]

time: 132 us -> 129 us (0.977)
  the two profiles are of different devices: /device:TPU:19 before, /device:TPU:14 now
where the time goes in v2:
time: 129 us; the launch traced here: 128 us
  waiting for transfers between devices  58.9 us (46%)
  Pallas kernels  44.7 us (35%)
  starting transfers between devices  21.2 us (16%)
  local copies, waits for them, and re-layouts  2.27 us (2%)
    ppermute x21, waiting for transfers between devices, swap(): lax.ppermute(value, 'ctx', [(i, i ^ bits) for i in range(lax.axis_size('c...  42.9 us
    pallas_call x3, Pallas kernels, attention(): pl.pallas_call(kernel, out_shape=[jax.ShapeDtypeStruct((rows, width), bf)...  25.6 us
    ppermute x8, waiting for transfers between devices, swap_levels(): return lax.ppermute(value, 'ctx', sorted(pairs.items()))  15.9 us
    ppermute x21, starting transfers between devices, swap(): lax.ppermute(value, 'ctx', [(i, i ^ bits) for i in range(lax.axis_size('c...  11.2 us
    ppermute x8, starting transfers between devices, swap_levels(): return lax.ppermute(value, 'ctx', sorted(pairs.items()))  9.98 us
    pallas_call x3, Pallas kernels, pack_z(): pl.pallas_call(kernel, out_shape=[jax.ShapeDtypeStruct((n_fwd, rows, 2 *...  7.56 us
    pallas_call x2, Pallas kernels, pack_columns(): pl.pallas_call(kernel, out_shape=[jax.ShapeDtypeStruct((rows, total), arr...  6.37 us
    pallas_call x1, Pallas kernels, gather_out(): pl.pallas_call(kernel, out_shape=jax.ShapeDtypeStruct((rows, LEVEL * slab...  2.68 us
  transfers between devices with their start and end apart: 29, of which 14 were waited for; matrix products, arithmetic and copies ran while one was open for 0% of the time, Pallas kernels for 31%

profile of v2, /device:TPU:14, one launch (start us, length us, event | category | flops | bytes accessed | tf_op | source)
XLA Modules:
  0.0 127.6 jit_solution(14318639138244937770)
XLA Ops:
  0.0 2.7 %shard_map.55 = (bf16[256,512]{1,0:T(8,128)(2,1)}, bf16[256,512]{1,0:T(8,128)(2,1)}, bf16[256,512]{1,0:T(8,128)(2,1)}, bf16[256,1536]{1,0:T(8,128)(2,1)}) custom-call(bf16[256,3072]{1,0:T(8,128)(2,1)} %refs_0_.3, bf16[256,3072]{1,0:T(8,128)(2,1)} %refs_1_.3, bf16[256,3072]{1,0:T(8,128)(2,1)} %q.5), custom_call_target="tpu_custom_call" | custom-call | bytes 3145728 | tf_op jit(solution)/shard_map/pallas_call | solution.py:66
  2.8 3.7 %shard_map.56 = (bf16[256,768]{1,0:T(8,128)(2,1)}, bf16[256,768]{1,0:T(8,128)(2,1)}, bf16[256,768]{1,0:T(8,128)(2,1)}, bf16[256,768]{1,0:T(8,128)(2,1)}, bf16[25...) custom-call(bf16[256,3072]{1,0:T(8,128)(2,1)} %refs_0_.3, ...), custom_call_target="tpu_custom_call" | custom-call | bytes 5505024 | tf_op jit(solution)/shard_map/pallas_call | solution.py:66
  6.5 0.5 collective-permute-start.21
  7.0 0.5 collective-permute-start.22
  7.5 1.5 %collective-permute-start.1 = (bf16[256,512]{1,0:T(8,128)(2,1)}, bf16[256,512]{1,0:T(8,128)(2,1)S(1)}, u32[]{:S(2)}, u32[]{:S(2)}) collective-permute-start(bf16[256,512]{1,0:T(8,128)(2,1)} %get-tuple-element.44), channel_id=1, source_target_pairs={{0,2},{1,3},{2,0},{3,1},{4,6},{5,7},{6,4},{7,5},{8,10},{9,11},{10,... | collective-permute-start | bytes 786440 | tf_op jit(solution)/shard_map/ppermute | solution.py:26
  9.0 0.6 collective-permute-start.3
  9.6 3.9 %collective-permute-done.22.rest_5_ = bf16[256,256]{1,0:T(8,128)(2,1)S(1)} collective-permute-done((bf16[256,256]{1,0:T(8,128)(2,1)}, bf16[256,256]{1,0:T(8,128)(2,1)S(1)}, u32[]{:S(2)}, u32[]{:S(2)}) %collective-permute-start.22) | collective-permute-done | bytes 131104 | tf_op jit(solution)/shard_map/ppermute | solution.py:26
  13.6 0.5 collective-permute-start.4
  14.1 5.1 %collective-permute-done.1.rest_1_.rest_2_ = bf16[256,512]{1,0:T(8,128)(2,1)S(1)} collective-permute-done((bf16[256,512]{1,0:T(8,128)(2,1)}, bf16[256,512]{1,0:T(8,128)(2,1)S(1)}, u32[]{:S(2)}, u32[]{:S(2)}) %collective-permute-start.1) | collective-permute-done | bytes 262176 | tf_op jit(solution)/shard_map/ppermute | solution.py:26
  19.2 0.5 collective-permute-start.14
  19.7 3.3 %collective-permute-done.2.rest_2_.rest_3_ = bf16[256,512]{1,0:T(8,128)(2,1)S(1)} collective-permute-done((bf16[256,512]{1,0:T(8,128)(2,1)}, bf16[256,512]{1,0:T(8,128)(2,1)S(1)}, u32[]{:S(2)}, u32[]{:S(2)}) %collective-permute-start.2) | collective-permute-done | bytes 262176 | tf_op jit(solution)/shard_map/ppermute | solution.py:26
  23.0 0.7 copy-done.8
  23.7 1.6 %collective-permute-start.7 = (bf16[256,1536]{1,0:T(8,128)(2,1)S(1)}, bf16[256,1536]{1,0:T(8,128)(2,1)S(1)}, u32[]{:S(2)}, u32[]{:S(2)}) collective-permute-start(bf16[256,1536]{1,0:T(8,128)(2,1)S(1)} %copy-done), channel_id=1, source_target_pairs={{0,1},{1,0},{2,3},{3,2},{4,8},{5,9},{6,10},{7,11},{8,4},{9,5},{10,... | collective-permute-start | bytes 2359304 | tf_op jit(solution)/shard_map/ppermute | solution.py:35
  25.3 1.4 %collective-permute-start.15 = (bf16[256,768]{1,0:T(8,128)(2,1)}, bf16[256,768]{1,0:T(8,128)(2,1)}, u32[]{:S(2)}, u32[]{:S(2)}) collective-permute-start(bf16[256,768]{1,0:T(8,128)(2,1)} %get-tuple-element.57), channel_id=1, source_target_pairs={{0,3},{1,2},{2,1},{3,0},{4,7},{5,6},{6,5},{7,4},{8,11},{9,10},{10,... | collective-permute-start | bytes 1179656 | tf_op jit(solution)/shard_map/ppermute | solution.py:26
  26.8 2.6 %pack_z.3 = (bf16[3,256,512]{2,1,0:T(8,128)(2,1)}, bf16[3,256,512]{2,1,0:T(8,128)(2,1)}) custom-call(bf16[256,1536]{1,0:T(8,128)(2,1)} %get-tuple-element.42.o.rest_0_, bf16[256,512]{1,0:T(8,128)(2,1)} %copy-done.6, bf16[256,512]{1,0:T(8,128)(2,1)} %copy-done.7, bf16[256,512]{1,0:T(8,128)(2,1)} %copy-done.8), custom_call_target="tpu_custom_call" | custom-call | bytes 2621440 | tf_op jit(solution)/shard_map/pack_z/pallas_call | solution.py:104
  29.3 4.0 %collective-permute-done.4.rest_5_.rest_1_.rest_2_ = bf16[256,768]{1,0:T(8,128)(2,1)} collective-permute-done((bf16[256,768]{1,0:T(8,128)(2,1)}, bf16[256,768]{1,0:T(8,128)(2,1)}, u32[]{:S(2)}, u32[]{:S(2)}) %collective-permute-start.4) | collective-permute-done | bytes 393248 | tf_op jit(solution)/shard_map/ppermute | solution.py:26
  33.3 0.5 collective-permute-start.6
  33.8 1.6 %collective-permute-start.8 = (bf16[3,256,512]{2,1,0:T(8,128)(2,1)}, bf16[3,256,512]{2,1,0:T(8,128)(2,1)}, u32[]{:S(2)}, u32[]{:S(2)}) collective-permute-start(bf16[3,256,512]{2,1,0:T(8,128)(2,1)} %get-tuple-element.49), channel_id=1, source_target_pairs={{0,4},{1,5},{2,6},{3,7},{4,0},{5,1},{6,2},{7,3},{8,12},{9,13},{10,... | collective-permute-start | bytes 2359304 | tf_op jit(solution)/shard_map/ppermute | solution.py:35
  35.4 6.4 %collective-permute-done.14.rest_5_.rest_1_.rest_2_ = bf16[256,768]{1,0:T(8,128)(2,1)} collective-permute-done((bf16[256,768]{1,0:T(8,128)(2,1)}, bf16[256,768]{1,0:T(8,128)(2,1)}, u32[]{:S(2)}, u32[]{:S(2)}) %collective-permute-start.14) | collective-permute-done | bytes 393248 | tf_op jit(solution)/shard_map/ppermute | solution.py:26
  41.8 6.7 %collective-permute-done.15.rest_6_.rest_2_.rest_3_ = bf16[256,768]{1,0:T(8,128)(2,1)} collective-permute-done((bf16[256,768]{1,0:T(8,128)(2,1)}, bf16[256,768]{1,0:T(8,128)(2,1)}, u32[]{:S(2)}, u32[]{:S(2)}) %collective-permute-start.15) | collective-permute-done | bytes 393248 | tf_op jit(solution)/shard_map/ppermute | solution.py:26
  48.4 1.6 %collective-permute-start.9 = (bf16[3,256,512]{2,1,0:T(8,128)(2,1)}, bf16[3,256,512]{2,1,0:T(8,128)(2,1)}, u32[]{:S(2)}, u32[]{:S(2)}) collective-permute-start(bf16[3,256,512]{2,1,0:T(8,128)(2,1)} %get-tuple-element.50), channel_id=1, source_target_pairs={{0,1},{1,0},{2,3},{3,2},{4,8},{5,9},{6,10},{7,11},{8,4},{9,5},{10,... | collective-permute-start | bytes 2359304 | tf_op jit(solution)/shard_map/ppermute | solution.py:35
  50.0 2.5 %pack_z.5 = (bf16[3,256,512]{2,1,0:T(8,128)(2,1)}, bf16[3,256,512]{2,1,0:T(8,128)(2,1)}) custom-call(bf16[256,1536]{1,0:T(8,128)(2,1)} %get-tuple-element.42.o.rest_0_, bf16[256,768]{1,0:T(8,128)(2,1)} %copy-done.4, bf16[256,768]{1,0:T(8,128)(2,1)} %collective-permute-done.14.rest_5_.rest_1_.rest_2_, ...), custom_call_target="tpu_custom_call" | custom-call | bytes 2621440 | tf_op jit(solution)/shard_map/pack_z/pallas_call | solution.py:104
  52.5 4.3 %collective-permute-done.5.rest_6_.rest_2_.rest_3_ = bf16[256,768]{1,0:T(8,128)(2,1)} collective-permute-done((bf16[256,768]{1,0:T(8,128)(2,1)}, bf16[256,768]{1,0:T(8,128)(2,1)}, u32[]{:S(2)}, u32[]{:S(2)}) %collective-permute-start.5) | collective-permute-done | bytes 393248 | tf_op jit(solution)/shard_map/ppermute | solution.py:26
  56.8 0.4 collective-permute-start.24
  57.3 2.7 %collective-permute-start.25 = (bf16[3,256,512]{2,1,0:T(8,128)(2,1)}, bf16[3,256,512]{2,1,0:T(8,128)(2,1)S(1)}, u32[]{:S(2)}, u32[]{:S(2)}) collective-permute-start(bf16[3,256,512]{2,1,0:T(8,128)(2,1)} %get-tuple-element.68), channel_id=1, source_target_pairs={{0,1},{1,0},{2,3},{3,2},{4,8},{5,9},{6,10},{7,11},{8,4},{9,5},{10,... | collective-permute-start | bytes 2359304 | tf_op jit(solution)/shard_map/ppermute | solution.py:35
  60.0 2.5 %pack_z.4 = (bf16[3,256,512]{2,1,0:T(8,128)(2,1)}, bf16[3,256,512]{2,1,0:T(8,128)(2,1)}) custom-call(bf16[256,1536]{1,0:T(8,128)(2,1)} %get-tuple-element.42.o.rest_0_, bf16[256,768]{1,0:T(8,128)(2,1)} %copy-done.5, bf16[256,768]{1,0:T(8,128)(2,1)} %collective-permute-done.4.rest_5_.rest_1_.rest_2_, ...), custom_call_target="tpu_custom_call" | custom-call | bytes 2621440 | tf_op jit(solution)/shard_map/pack_z/pallas_call | solution.py:104
  62.6 8.1 %collective-permute-done.8.rest_9_ = bf16[3,256,512]{2,1,0:T(8,128)(2,1)} collective-permute-done((bf16[3,256,512]{2,1,0:T(8,128)(2,1)}, bf16[3,256,512]{2,1,0:T(8,128)(2,1)}, u32[]{:S(2)}, u32[]{:S(2)}) %collective-permute-start.8) | collective-permute-done | bytes 786464 | tf_op jit(solution)/shard_map/ppermute | solution.py:35
  70.7 1.6 %collective-permute-start.17 = (bf16[3,256,512]{2,1,0:T(8,128)(2,1)}, bf16[3,256,512]{2,1,0:T(8,128)(2,1)}, u32[]{:S(2)}, u32[]{:S(2)}) collective-permute-start(bf16[3,256,512]{2,1,0:T(8,128)(2,1)} %get-tuple-element.59), channel_id=1, source_target_pairs={{0,1},{1,0},{2,3},{3,2},{4,8},{5,9},{6,10},{7,11},{8,4},{9,5},{10,... | collective-permute-start | bytes 2359304 | tf_op jit(solution)/shard_map/ppermute | solution.py:35
  72.3 2.5 %lookup_tables.1 = (bf16[2560,128]{1,0:T(8,128)(2,1)}, bf16[1024,128]{1,0:T(8,128)(2,1)}, s32[5,2]{1,0:T(8,128)}) custom-call(s32[16]{0:T(128)} %len_ref.1, s32[16,16]{1,0:T(8,128)} %mask_ref.1), custom_call_target="tpu_custom_call" | custom-call | bytes 917504 | tf_op jit(solution)/shard_map/lookup_tables/pallas_call | solution.py:177
  74.8 0.1 collective-permute-start.23
  74.9 8.5 %attention.3 = (bf16[256,256]{1,0:T(8,128)(2,1)}, bf16[256,256]{1,0:T(8,128)(2,1)}, bf16[256,256]{1,0:T(8,128)(2,1)}, bf16[256,256]{1,0:T(8,128)(2,1)}) custom-call(s32[5,2]{1,0:T(8,128)} %get-tuple-element.39.ranges, bf16[2560,128]{1,0:T(8,128)(2,1)} %get-tuple-element.40.bias_hbm, bf16[1024,128]{1,0:T(8,128)(2,1)} %get-tuple-element.41.onehot_hbm, ...), custom_call_target="tpu_custom_call" | custom-call | flops 2147483648 | bytes 2621440 | tf_op jit(solution)/shard_map/attention/pallas_call | solution.py:320
  83.5 0.7 collective-permute-start.10
  84.1 3.4 %collective-permute-done.24.rest_9_ = bf16[3,256,512]{2,1,0:T(8,128)(2,1)} collective-permute-done((bf16[3,256,512]{2,1,0:T(8,128)(2,1)}, bf16[3,256,512]{2,1,0:T(8,128)(2,1)}, u32[]{:S(2)}, u32[]{:S(2)}) %collective-permute-start.24) | collective-permute-done | bytes 786464 | tf_op jit(solution)/shard_map/ppermute | solution.py:35
  87.6 0.5 collective-permute-start.11
  88.1 0.9 copy-done.9
  89.0 8.5 %attention.5 = (bf16[256,256]{1,0:T(8,128)(2,1)}, bf16[256,256]{1,0:T(8,128)(2,1)}, bf16[256,256]{1,0:T(8,128)(2,1)}, bf16[256,256]{1,0:T(8,128)(2,1)}) custom-call(s32[5,2]{1,0:T(8,128)} %get-tuple-element.39.ranges, bf16[2560,128]{1,0:T(8,128)(2,1)} %get-tuple-element.40.bias_hbm, bf16[1024,128]{1,0:T(8,128)(2,1)} %get-tuple-element.41.onehot_hbm, ...), custom_call_target="tpu_custom_call" | custom-call | flops 2147483648 | bytes 2621440 | tf_op jit(solution)/shard_map/attention/pallas_call | solution.py:320
  97.5 4.2 %collective-permute-done.16.rest_9_ = bf16[3,256,512]{2,1,0:T(8,128)(2,1)S(1)} collective-permute-done((bf16[3,256,512]{2,1,0:T(8,128)(2,1)}, bf16[3,256,512]{2,1,0:T(8,128)(2,1)S(1)}, u32[]{:S(2)}, u32[]{:S(2)}) %collective-permute-start.16) | collective-permute-done | bytes 786464 | tf_op jit(solution)/shard_map/ppermute | solution.py:35
  101.7 0.2 collective-permute-done.17.rest_10_
  101.9 2.1 %collective-permute-start.27 = (bf16[256,256]{1,0:T(8,128)(2,1)}, bf16[256,256]{1,0:T(8,128)(2,1)S(1)}, u32[]{:S(2)}, u32[]{:S(2)}) collective-permute-start(bf16[256,256]{1,0:T(8,128)(2,1)} %get-tuple-element.71), channel_id=1, source_target_pairs={{0,2},{1,3},{2,0},{3,1},{4,6},{5,7},{6,4},{7,5},{8,10},{9,11},{10,... | collective-permute-start | bytes 393224 | tf_op jit(solution)/shard_map/ppermute | solution.py:26
  104.1 8.5 %attention.4 = (bf16[256,256]{1,0:T(8,128)(2,1)}, bf16[256,256]{1,0:T(8,128)(2,1)}, bf16[256,256]{1,0:T(8,128)(2,1)}, bf16[256,256]{1,0:T(8,128)(2,1)}) custom-call(s32[5,2]{1,0:T(8,128)} %get-tuple-element.39.ranges, bf16[2560,128]{1,0:T(8,128)(2,1)} %get-tuple-element.40.bias_hbm, bf16[1024,128]{1,0:T(8,128)(2,1)} %get-tuple-element.41.onehot_hbm, ...), custom_call_target="tpu_custom_call" | custom-call | flops 2147483648 | bytes 2621440 | tf_op jit(solution)/shard_map/attention/pallas_call | solution.py:320
  112.6 0.1 collective-permute-start.28
  112.7 0.2 collective-permute-start.18
  113.0 1.9 %collective-permute-start.19 = (bf16[256,256]{1,0:T(8,128)(2,1)}, bf16[256,256]{1,0:T(8,128)(2,1)S(1)}, u32[]{:S(2)}, u32[]{:S(2)}) collective-permute-start(bf16[256,256]{1,0:T(8,128)(2,1)} %get-tuple-element.62), channel_id=1, source_target_pairs={{0,2},{1,3},{2,0},{3,1},{4,6},{5,7},{6,4},{7,5},{8,10},{9,11},{10,... | collective-permute-start | bytes 393224 | tf_op jit(solution)/shard_map/ppermute | solution.py:26
  114.9 3.6 %collective-permute-done.28.refs_11_ = bf16[256,256]{1,0:T(8,128)(2,1)S(1)} collective-permute-done((bf16[256,256]{1,0:T(8,128)(2,1)S(1)}, bf16[256,256]{1,0:T(8,128)(2,1)S(1)}, u32[]{:S(2)}, u32[]{:S(2)}) %collective-permute-start.28) | collective-permute-done | bytes 131104 | tf_op jit(solution)/shard_map/ppermute | solution.py:26
  118.5 2.8 %collective-permute-done.19.refs_6_ = bf16[256,256]{1,0:T(8,128)(2,1)S(1)} collective-permute-done((bf16[256,256]{1,0:T(8,128)(2,1)}, bf16[256,256]{1,0:T(8,128)(2,1)S(1)}, u32[]{:S(2)}, u32[]{:S(2)}) %collective-permute-start.19) | collective-permute-done | bytes 131104 | tf_op jit(solution)/shard_map/ppermute | solution.py:26
  121.3 2.8 %collective-permute-done.20.refs_7_ = bf16[256,256]{1,0:T(8,128)(2,1)S(1)} collective-permute-done((bf16[256,256]{1,0:T(8,128)(2,1)}, bf16[256,256]{1,0:T(8,128)(2,1)S(1)}, u32[]{:S(2)}, u32[]{:S(2)}) %collective-permute-start.20) | collective-permute-done | bytes 131104 | tf_op jit(solution)/shard_map/ppermute | solution.py:26
  124.1 0.6 copy-done.22
  124.7 2.7 %gather_out.1 = bf16[256,3072]{1,0:T(8,128)(2,1)} custom-call(bf16[256,256]{1,0:T(8,128)(2,1)} %get-tuple-element.51.refs_0_, bf16[256,256]{1,0:T(8,128)(2,1)} %copy-done.14, bf16[256,256]{1,0:T(8,128)(2,1)} %copy-done.15, bf16[256,256]{1,0:T(8,128)(2,1)} %copy-done.16, bf16[256,256]{1,0:T(8,128)(2,1)} %get-tuple-element.60.refs_4_, ...), custom_call_target="tpu_custom_call" | custom-call | bytes 3145728 | tf_op jit(solution)/shard_map/gather_out/pallas_call | solution.py:354
  (70 shorter events, 0.3 us)
Async XLA Ops:
  2.7 21.0 %copy-start = (bf16[256,1536]{1,0:T(8,128)(2,1)S(1)}, bf16[256,1536]{1,0:T(8,128)(2,1)}, u32[]{:S(2)}) copy-start(bf16[256,1536]{1,0:T(8,128)(2,1)} %get-tuple-element.42.o.rest_0_) | copy-start | bytes 2359300
  2.7 11.3 %collective-permute-start = (bf16[256,512]{1,0:T(8,128)(2,1)}, bf16[256,512]{1,0:T(8,128)(2,1)S(1)}, u32[]{:S(2)}, u32[]{:S(2)}) collective-permute-start(bf16[256,512]{1,0:T(8,128)(2,1)} %get-tuple-element.43), channel_id=1, source_target_pairs={{0,1},{1,0},{2,3},{3,2},{4,5},{5,4},{6,7},{7,6},{8,9},{9,8},{10,11... | collective-permute-start | bytes 786440 | tf_op jit(solution)/shard_map/ppermute | solution.py:26
  6.5 26.9 %copy-start.1 = (bf16[256,1536]{1,0:T(8,128)(2,1)S(1)}, bf16[256,1536]{1,0:T(8,128)(2,1)}, u32[]{:S(2)}) copy-start(bf16[256,1536]{1,0:T(8,128)(2,1)} %get-tuple-element.42.o.rest_0_) | copy-start | bytes 2359300
  6.5 2.5 %collective-permute-start.21 = (bf16[256,256]{1,0:T(8,128)(2,1)}, bf16[256,256]{1,0:T(8,128)(2,1)S(1)}, u32[]{:S(2)}, u32[]{:S(2)}) collective-permute-start(bf16[256,256]{1,0:T(8,128)(2,1)} %get-tuple-element.64), channel_id=1, source_target_pairs={{0,1},{1,0},{2,3},{3,2},{4,5},{5,4},{6,7},{7,6},{8,9},{9,8},{10,11... | collective-permute-start | bytes 393224 | tf_op jit(solution)/shard_map/ppermute | solution.py:26
  7.0 6.6 %collective-permute-start.22 = (bf16[256,256]{1,0:T(8,128)(2,1)}, bf16[256,256]{1,0:T(8,128)(2,1)S(1)}, u32[]{:S(2)}, u32[]{:S(2)}) collective-permute-start(bf16[256,256]{1,0:T(8,128)(2,1)} %get-tuple-element.65), channel_id=1, source_target_pairs={{0,2},{1,3},{2,0},{3,1},{4,6},{5,7},{6,4},{7,5},{8,10},{9,11},{10,... | collective-permute-start | bytes 393224 | tf_op jit(solution)/shard_map/ppermute | solution.py:26
  7.5 11.7 %collective-permute-start.1 = (bf16[256,512]{1,0:T(8,128)(2,1)}, bf16[256,512]{1,0:T(8,128)(2,1)S(1)}, u32[]{:S(2)}, u32[]{:S(2)}) collective-permute-start(bf16[256,512]{1,0:T(8,128)(2,1)} %get-tuple-element.44), channel_id=1, source_target_pairs={{0,2},{1,3},{2,0},{3,1},{4,6},{5,7},{6,4},{7,5},{8,10},{9,11},{10,... | collective-permute-start | bytes 786440 | tf_op jit(solution)/shard_map/ppermute | solution.py:26
  9.0 14.0 %collective-permute-start.2 = (bf16[256,512]{1,0:T(8,128)(2,1)}, bf16[256,512]{1,0:T(8,128)(2,1)S(1)}, u32[]{:S(2)}, u32[]{:S(2)}) collective-permute-start(bf16[256,512]{1,0:T(8,128)(2,1)} %get-tuple-element.45), channel_id=1, source_target_pairs={{0,3},{1,2},{2,1},{3,0},{4,7},{5,6},{6,5},{7,4},{8,11},{9,10},{10,... | collective-permute-start | bytes 786440 | tf_op jit(solution)/shard_map/ppermute | solution.py:26
  9.0 14.0 %copy-start.11 = (bf16[256,256]{1,0:T(8,128)(2,1)}, bf16[256,256]{1,0:T(8,128)(2,1)S(1)}, u32[]{:S(2)}) copy-start(bf16[256,256]{1,0:T(8,128)(2,1)S(1)} %collective-permute-done.21.rest_4_) | copy-start | bytes 393220
  9.0 16.3 %collective-permute-start.3 = (bf16[256,768]{1,0:T(8,128)(2,1)}, bf16[256,768]{1,0:T(8,128)(2,1)S(1)}, u32[]{:S(2)}, u32[]{:S(2)}) collective-permute-start(bf16[256,768]{1,0:T(8,128)(2,1)} %get-tuple-element.46), channel_id=1, source_target_pairs={{0,1},{1,0},{2,3},{3,2},{4,5},{5,4},{6,7},{7,6},{8,9},{9,8},{10,11... | collective-permute-start | bytes 1179656 | tf_op jit(solution)/shard_map/ppermute | solution.py:26
  13.6 9.5 %copy-start.12 = (bf16[256,256]{1,0:T(8,128)(2,1)}, bf16[256,256]{1,0:T(8,128)(2,1)S(1)}, u32[]{:S(2)}) copy-start(bf16[256,256]{1,0:T(8,128)(2,1)S(1)} %collective-permute-done.22.rest_5_) | copy-start | bytes 393220
  13.6 19.8 %collective-permute-start.4 = (bf16[256,768]{1,0:T(8,128)(2,1)}, bf16[256,768]{1,0:T(8,128)(2,1)}, u32[]{:S(2)}, u32[]{:S(2)}) collective-permute-start(bf16[256,768]{1,0:T(8,128)(2,1)} %get-tuple-element.47), channel_id=1, source_target_pairs={{0,2},{1,3},{2,0},{3,1},{4,6},{5,7},{6,4},{7,5},{8,10},{9,11},{10,... | collective-permute-start | bytes 1179656 | tf_op jit(solution)/shard_map/ppermute | solution.py:26
  14.1 12.7 %copy-start.6 = (bf16[256,512]{1,0:T(8,128)(2,1)}, bf16[256,512]{1,0:T(8,128)(2,1)S(1)}, u32[]{:S(2)}) copy-start(bf16[256,512]{1,0:T(8,128)(2,1)S(1)} %collective-permute-done.rest_0_.rest_1_) | copy-start | bytes 786436
  14.1 19.7 %collective-permute-start.13 = (bf16[256,768]{1,0:T(8,128)(2,1)}, bf16[256,768]{1,0:T(8,128)(2,1)S(1)}, u32[]{:S(2)}, u32[]{:S(2)}) collective-permute-start(bf16[256,768]{1,0:T(8,128)(2,1)} %get-tuple-element.55), channel_id=1, source_target_pairs={{0,1},{1,0},{2,3},{3,2},{4,5},{5,4},{6,7},{7,6},{8,9},{9,8},{10,11... | collective-permute-start | bytes 1179656 | tf_op jit(solution)/shard_map/ppermute | solution.py:26
  19.2 22.6 %collective-permute-start.14 = (bf16[256,768]{1,0:T(8,128)(2,1)}, bf16[256,768]{1,0:T(8,128)(2,1)}, u32[]{:S(2)}, u32[]{:S(2)}) collective-permute-start(bf16[256,768]{1,0:T(8,128)(2,1)} %get-tuple-element.56), channel_id=1, source_target_pairs={{0,2},{1,3},{2,0},{3,1},{4,6},{5,7},{6,4},{7,5},{8,10},{9,11},{10,... | collective-permute-start | bytes 1179656 | tf_op jit(solution)/shard_map/ppermute | solution.py:26
  23.7 33.5 %collective-permute-start.7 = (bf16[256,1536]{1,0:T(8,128)(2,1)S(1)}, bf16[256,1536]{1,0:T(8,128)(2,1)S(1)}, u32[]{:S(2)}, u32[]{:S(2)}) collective-permute-start(bf16[256,1536]{1,0:T(8,128)(2,1)S(1)} %copy-done), channel_id=1, source_target_pairs={{0,1},{1,0},{2,3},{3,2},{4,8},{5,9},{6,10},{7,11},{8,4},{9,5},{10,... | collective-permute-start | bytes 2359304 | tf_op jit(solution)/shard_map/ppermute | solution.py:35
  25.3 4.0 %copy-start.5 = (bf16[256,768]{1,0:T(8,128)(2,1)}, bf16[256,768]{1,0:T(8,128)(2,1)S(1)}, u32[]{:S(2)}) copy-start(bf16[256,768]{1,0:T(8,128)(2,1)S(1)} %collective-permute-done.3.rest_4_.rest_0_.rest_1_) | copy-start | bytes 1179652
  25.3 23.1 %collective-permute-start.15 = (bf16[256,768]{1,0:T(8,128)(2,1)}, bf16[256,768]{1,0:T(8,128)(2,1)}, u32[]{:S(2)}, u32[]{:S(2)}) collective-permute-start(bf16[256,768]{1,0:T(8,128)(2,1)} %get-tuple-element.57), channel_id=1, source_target_pairs={{0,3},{1,2},{2,1},{3,0},{4,7},{5,6},{6,5},{7,4},{8,11},{9,10},{10,... | collective-permute-start | bytes 1179656 | tf_op jit(solution)/shard_map/ppermute | solution.py:26
  33.3 29.2 %collective-permute-start.6 = (bf16[256,1536]{1,0:T(8,128)(2,1)S(1)}, bf16[256,1536]{1,0:T(8,128)(2,1)S(1)}, u32[]{:S(2)}, u32[]{:S(2)}) collective-permute-start(bf16[256,1536]{1,0:T(8,128)(2,1)S(1)} %copy-done.1), channel_id=1, source_target_pairs={{0,4},{1,5},{2,6},{3,7},{4,0},{5,1},{6,2},{7,3},{8,12},{9,13},{10,... | collective-permute-start | bytes 2359304 | tf_op jit(solution)/shard_map/ppermute | solution.py:35
  33.8 16.2 %copy-start.4 = (bf16[256,768]{1,0:T(8,128)(2,1)}, bf16[256,768]{1,0:T(8,128)(2,1)S(1)}, u32[]{:S(2)}) copy-start(bf16[256,768]{1,0:T(8,128)(2,1)S(1)} %collective-permute-done.13.rest_4_.rest_0_.rest_1_) | copy-start | bytes 1179652
  33.8 36.9 %collective-permute-start.8 = (bf16[3,256,512]{2,1,0:T(8,128)(2,1)}, bf16[3,256,512]{2,1,0:T(8,128)(2,1)}, u32[]{:S(2)}, u32[]{:S(2)}) collective-permute-start(bf16[3,256,512]{2,1,0:T(8,128)(2,1)} %get-tuple-element.49), channel_id=1, source_target_pairs={{0,4},{1,5},{2,6},{3,7},{4,0},{5,1},{6,2},{7,3},{8,12},{9,13},{10,... | collective-permute-start | bytes 2359304 | tf_op jit(solution)/shard_map/ppermute | solution.py:35
  41.8 15.1 %collective-permute-start.5 = (bf16[256,768]{1,0:T(8,128)(2,1)}, bf16[256,768]{1,0:T(8,128)(2,1)}, u32[]{:S(2)}, u32[]{:S(2)}) collective-permute-start(bf16[256,768]{1,0:T(8,128)(2,1)} %get-tuple-element.48), channel_id=1, source_target_pairs={{0,3},{1,2},{2,1},{3,0},{4,7},{5,6},{6,5},{7,4},{8,11},{9,10},{10,... | collective-permute-start | bytes 1179656 | tf_op jit(solution)/shard_map/ppermute | solution.py:26
  48.4 26.4 %collective-permute-start.9 = (bf16[3,256,512]{2,1,0:T(8,128)(2,1)}, bf16[3,256,512]{2,1,0:T(8,128)(2,1)}, u32[]{:S(2)}, u32[]{:S(2)}) collective-permute-start(bf16[3,256,512]{2,1,0:T(8,128)(2,1)} %get-tuple-element.50), channel_id=1, source_target_pairs={{0,1},{1,0},{2,3},{3,2},{4,8},{5,9},{6,10},{7,11},{8,4},{9,5},{10,... | collective-permute-start | bytes 2359304 | tf_op jit(solution)/shard_map/ppermute | solution.py:35
  52.5 22.3 %copy-start.23 = (bf16[256,256]{1,0:T(8,128)(2,1)S(1)}, bf16[256,256]{1,0:T(8,128)(2,1)}, u32[]{:S(2)}) copy-start(bf16[256,256]{1,0:T(8,128)(2,1)} %get-tuple-element.66) | copy-start | bytes 393220
  56.8 30.7 %collective-permute-start.24 = (bf16[3,256,512]{2,1,0:T(8,128)(2,1)}, bf16[3,256,512]{2,1,0:T(8,128)(2,1)}, u32[]{:S(2)}, u32[]{:S(2)}) collective-permute-start(bf16[3,256,512]{2,1,0:T(8,128)(2,1)} %get-tuple-element.67), channel_id=1, source_target_pairs={{0,4},{1,5},{2,6},{3,7},{4,0},{5,1},{6,2},{7,3},{8,12},{9,13},{10,... | collective-permute-start | bytes 2359304 | tf_op jit(solution)/shard_map/ppermute | solution.py:35
  57.3 17.6 %copy-start.2 = (bf16[256,1536]{1,0:T(8,128)(2,1)}, bf16[256,1536]{1,0:T(8,128)(2,1)S(1)}, u32[]{:S(2)}) copy-start(bf16[256,1536]{1,0:T(8,128)(2,1)S(1)} %collective-permute-done.7.rest_8_) | copy-start | bytes 2359300
  57.3 30.8 %collective-permute-start.25 = (bf16[3,256,512]{2,1,0:T(8,128)(2,1)}, bf16[3,256,512]{2,1,0:T(8,128)(2,1)S(1)}, u32[]{:S(2)}, u32[]{:S(2)}) collective-permute-start(bf16[3,256,512]{2,1,0:T(8,128)(2,1)} %get-tuple-element.68), channel_id=1, source_target_pairs={{0,1},{1,0},{2,3},{3,2},{4,8},{5,9},{6,10},{7,11},{8,4},{9,5},{10,... | collective-permute-start | bytes 2359304 | tf_op jit(solution)/shard_map/ppermute | solution.py:35
  62.5 12.4 %copy-start.3 = (bf16[256,1536]{1,0:T(8,128)(2,1)}, bf16[256,1536]{1,0:T(8,128)(2,1)S(1)}, u32[]{:S(2)}) copy-start(bf16[256,1536]{1,0:T(8,128)(2,1)S(1)} %collective-permute-done.6.rest_7_) | copy-start | bytes 2359300
  62.5 39.2 %collective-permute-start.16 = (bf16[3,256,512]{2,1,0:T(8,128)(2,1)}, bf16[3,256,512]{2,1,0:T(8,128)(2,1)S(1)}, u32[]{:S(2)}, u32[]{:S(2)}) collective-permute-start(bf16[3,256,512]{2,1,0:T(8,128)(2,1)} %get-tuple-element.58), channel_id=1, source_target_pairs={{0,4},{1,5},{2,6},{3,7},{4,0},{5,1},{6,2},{7,3},{8,12},{9,13},{10,... | collective-permute-start | bytes 2359304 | tf_op jit(solution)/shard_map/ppermute | solution.py:35
  70.7 31.2 %collective-permute-start.17 = (bf16[3,256,512]{2,1,0:T(8,128)(2,1)}, bf16[3,256,512]{2,1,0:T(8,128)(2,1)}, u32[]{:S(2)}, u32[]{:S(2)}) collective-permute-start(bf16[3,256,512]{2,1,0:T(8,128)(2,1)} %get-tuple-element.59), channel_id=1, source_target_pairs={{0,1},{1,0},{2,3},{3,2},{4,8},{5,9},{6,10},{7,11},{8,4},{9,5},{10,... | collective-permute-start | bytes 2359304 | tf_op jit(solution)/shard_map/ppermute | solution.py:35
  74.8 8.6 %collective-permute-start.23 = (bf16[256,256]{1,0:T(8,128)(2,1)S(1)}, bf16[256,256]{1,0:T(8,128)(2,1)S(1)}, u32[]{:S(2)}, u32[]{:S(2)}) collective-permute-start(bf16[256,256]{1,0:T(8,128)(2,1)S(1)} %copy-done.23), channel_id=1, source_target_pairs={{0,3},{1,2},{2,1},{3,0},{4,7},{5,6},{6,5},{7,4},{8,11},{9,10},{10,... | collective-permute-start | bytes 393224 | tf_op jit(solution)/shard_map/ppermute | solution.py:26
  83.5 4.6 %copy-start.13 = (bf16[256,256]{1,0:T(8,128)(2,1)}, bf16[256,256]{1,0:T(8,128)(2,1)S(1)}, u32[]{:S(2)}) copy-start(bf16[256,256]{1,0:T(8,128)(2,1)S(1)} %collective-permute-done.23.rest_6_) | copy-start | bytes 393220
  83.5 29.1 %collective-permute-start.10 = (bf16[256,256]{1,0:T(8,128)(2,1)}, bf16[256,256]{1,0:T(8,128)(2,1)S(1)}, u32[]{:S(2)}, u32[]{:S(2)}) collective-permute-start(bf16[256,256]{1,0:T(8,128)(2,1)} %get-tuple-element.52), channel_id=1, source_target_pairs={{0,1},{1,0},{2,3},{3,2},{4,5},{5,4},{6,7},{7,6},{8,9},{9,8},{10,11... | collective-permute-start | bytes 393224 | tf_op jit(solution)/shard_map/ppermute | solution.py:26
  87.6 25.1 %collective-permute-start.11 = (bf16[256,256]{1,0:T(8,128)(2,1)}, bf16[256,256]{1,0:T(8,128)(2,1)S(1)}, u32[]{:S(2)}, u32[]{:S(2)}) collective-permute-start(bf16[256,256]{1,0:T(8,128)(2,1)} %get-tuple-element.53), channel_id=1, source_target_pairs={{0,2},{1,3},{2,0},{3,1},{4,6},{5,7},{6,4},{7,5},{8,10},{9,11},{10,... | collective-permute-start | bytes 393224 | tf_op jit(solution)/shard_map/ppermute | solution.py:26
  88.1 24.9 %collective-permute-start.12 = (bf16[256,256]{1,0:T(8,128)(2,1)}, bf16[256,256]{1,0:T(8,128)(2,1)S(1)}, u32[]{:S(2)}, u32[]{:S(2)}) collective-permute-start(bf16[256,256]{1,0:T(8,128)(2,1)} %get-tuple-element.54), channel_id=1, source_target_pairs={{0,3},{1,2},{2,1},{3,0},{4,7},{5,6},{6,5},{7,4},{8,11},{9,10},{10,... | collective-permute-start | bytes 393224 | tf_op jit(solution)/shard_map/ppermute | solution.py:26
  101.7 13.2 %collective-permute-start.26 = (bf16[256,256]{1,0:T(8,128)(2,1)}, bf16[256,256]{1,0:T(8,128)(2,1)S(1)}, u32[]{:S(2)}, u32[]{:S(2)}) collective-permute-start(bf16[256,256]{1,0:T(8,128)(2,1)} %get-tuple-element.70), channel_id=1, source_target_pairs={{0,1},{1,0},{2,3},{3,2},{4,5},{5,4},{6,7},{7,6},{8,9},{9,8},{10,11... | collective-permute-start | bytes 393224 | tf_op jit(solution)/shard_map/ppermute | solution.py:26
  101.9 10.7 %copy-start.24 = (bf16[256,256]{1,0:T(8,128)(2,1)S(1)}, bf16[256,256]{1,0:T(8,128)(2,1)}, u32[]{:S(2)}) copy-start(bf16[256,256]{1,0:T(8,128)(2,1)} %get-tuple-element.72) | copy-start | bytes 393220
  101.9 12.9 %collective-permute-start.27 = (bf16[256,256]{1,0:T(8,128)(2,1)}, bf16[256,256]{1,0:T(8,128)(2,1)S(1)}, u32[]{:S(2)}, u32[]{:S(2)}) collective-permute-start(bf16[256,256]{1,0:T(8,128)(2,1)} %get-tuple-element.71), channel_id=1, source_target_pairs={{0,2},{1,3},{2,0},{3,1},{4,6},{5,7},{6,4},{7,5},{8,10},{9,11},{10,... | collective-permute-start | bytes 393224 | tf_op jit(solution)/shard_map/ppermute | solution.py:26
  112.6 11.5 %copy-start.14 = (bf16[256,256]{1,0:T(8,128)(2,1)}, bf16[256,256]{1,0:T(8,128)(2,1)S(1)}, u32[]{:S(2)}) copy-start(bf16[256,256]{1,0:T(8,128)(2,1)S(1)} %collective-permute-done.10.refs_1_) | copy-start | bytes 393220
  112.6 5.8 %collective-permute-start.28 = (bf16[256,256]{1,0:T(8,128)(2,1)S(1)}, bf16[256,256]{1,0:T(8,128)(2,1)S(1)}, u32[]{:S(2)}, u32[]{:S(2)}) collective-permute-start(bf16[256,256]{1,0:T(8,128)(2,1)S(1)} %copy-done.24), channel_id=1, source_target_pairs={{0,3},{1,2},{2,1},{3,0},{4,7},{5,6},{6,5},{7,4},{8,11},{9,10},{10,... | collective-permute-start | bytes 393224 | tf_op jit(solution)/shard_map/ppermute | solution.py:26
  112.7 11.4 %copy-start.15 = (bf16[256,256]{1,0:T(8,128)(2,1)}, bf16[256,256]{1,0:T(8,128)(2,1)S(1)}, u32[]{:S(2)}) copy-start(bf16[256,256]{1,0:T(8,128)(2,1)S(1)} %collective-permute-done.11.refs_2_) | copy-start | bytes 393220
  112.7 5.7 %collective-permute-start.18 = (bf16[256,256]{1,0:T(8,128)(2,1)}, bf16[256,256]{1,0:T(8,128)(2,1)S(1)}, u32[]{:S(2)}, u32[]{:S(2)}) collective-permute-start(bf16[256,256]{1,0:T(8,128)(2,1)} %get-tuple-element.61), channel_id=1, source_target_pairs={{0,1},{1,0},{2,3},{3,2},{4,5},{5,4},{6,7},{7,6},{8,9},{9,8},{10,11... | collective-permute-start | bytes 393224 | tf_op jit(solution)/shard_map/ppermute | solution.py:26
  113.0 11.1 %copy-start.16 = (bf16[256,256]{1,0:T(8,128)(2,1)}, bf16[256,256]{1,0:T(8,128)(2,1)S(1)}, u32[]{:S(2)}) copy-start(bf16[256,256]{1,0:T(8,128)(2,1)S(1)} %collective-permute-done.12.refs_3_) | copy-start | bytes 393220
  113.0 8.3 %collective-permute-start.19 = (bf16[256,256]{1,0:T(8,128)(2,1)}, bf16[256,256]{1,0:T(8,128)(2,1)S(1)}, u32[]{:S(2)}, u32[]{:S(2)}) collective-permute-start(bf16[256,256]{1,0:T(8,128)(2,1)} %get-tuple-element.62), channel_id=1, source_target_pairs={{0,2},{1,3},{2,0},{3,1},{4,6},{5,7},{6,4},{7,5},{8,10},{9,11},{10,... | collective-permute-start | bytes 393224 | tf_op jit(solution)/shard_map/ppermute | solution.py:26
  114.8 9.3 %copy-start.17 = (bf16[256,256]{1,0:T(8,128)(2,1)}, bf16[256,256]{1,0:T(8,128)(2,1)S(1)}, u32[]{:S(2)}) copy-start(bf16[256,256]{1,0:T(8,128)(2,1)S(1)} %collective-permute-done.26.refs_9_) | copy-start | bytes 393220
  114.8 9.2 %collective-permute-start.20 = (bf16[256,256]{1,0:T(8,128)(2,1)}, bf16[256,256]{1,0:T(8,128)(2,1)S(1)}, u32[]{:S(2)}, u32[]{:S(2)}) collective-permute-start(bf16[256,256]{1,0:T(8,128)(2,1)} %get-tuple-element.63), channel_id=1, source_target_pairs={{0,3},{1,2},{2,1},{3,0},{4,7},{5,6},{6,5},{7,4},{8,11},{9,10},{10,... | collective-permute-start | bytes 393224 | tf_op jit(solution)/shard_map/ppermute | solution.py:26
  114.9 9.2 %copy-start.18 = (bf16[256,256]{1,0:T(8,128)(2,1)}, bf16[256,256]{1,0:T(8,128)(2,1)S(1)}, u32[]{:S(2)}) copy-start(bf16[256,256]{1,0:T(8,128)(2,1)S(1)} %collective-permute-done.27.refs_10_) | copy-start | bytes 393220
  118.5 5.7 %copy-start.19 = (bf16[256,256]{1,0:T(8,128)(2,1)}, bf16[256,256]{1,0:T(8,128)(2,1)S(1)}, u32[]{:S(2)}) copy-start(bf16[256,256]{1,0:T(8,128)(2,1)S(1)} %collective-permute-done.28.refs_11_) | copy-start | bytes 393220
  118.5 5.7 %copy-start.20 = (bf16[256,256]{1,0:T(8,128)(2,1)}, bf16[256,256]{1,0:T(8,128)(2,1)S(1)}, u32[]{:S(2)}) copy-start(bf16[256,256]{1,0:T(8,128)(2,1)S(1)} %collective-permute-done.18.refs_5_) | copy-start | bytes 393220
  (6 other events, 11.3 us)

commit v3 on v2

--- a/solution.py
+++ b/solution.py
@@ -17,7 +17,7 @@
 NEG = -1e30
 TILE = 256
 SIZES = (2, 3, 4, 5, 6, 8)
-HBM = pl.BlockSpec(memory_space=pl.ANY)
+ANY = pl.BlockSpec(memory_space=pl.ANY)
 VMEM = pl.BlockSpec(memory_space=pltpu.VMEM)
 SMEM = pl.BlockSpec(memory_space=pltpu.SMEM)
 
@@ -47,7 +47,11 @@
     return pl.CostEstimate(flops=flops, bytes_accessed=nbytes, transcendentals=0)
 
 
-def pack_columns(arrays, jobs):
+def vmem(mebibytes):
+    return pltpu.CompilerParams(vmem_limit_bytes=mebibytes << 20)
+
+
+def pack_columns(arrays, jobs, limit):
     rows = arrays[0].shape[0]
     totals = [sum(span[3] for span in spans) for _, spans in jobs]
 
@@ -66,10 +70,11 @@
     return pl.pallas_call(
         kernel,
         out_shape=[jax.ShapeDtypeStruct((rows, total), arrays[0].dtype) for total in totals],
-        in_specs=[HBM] * len(arrays),
+        in_specs=[ANY] * len(arrays),
         out_specs=[VMEM] * len(jobs),
         scratch_shapes=[pltpu.SemaphoreType.DMA((sum(len(spans) for _, spans in jobs),))],
         cost_estimate=cost(4 * rows * sum(totals)),
+        compiler_params=vmem(limit),
     )(*arrays)
 
 
@@ -104,10 +109,11 @@
     return pl.pallas_call(
         kernel,
         out_shape=[jax.ShapeDtypeStruct((n_fwd, rows, 2 * width), own.dtype)] * 2,
-        in_specs=[HBM] * LEVEL,
+        in_specs=[ANY] * LEVEL,
         out_specs=[VMEM, VMEM],
         scratch_shapes=[pltpu.SemaphoreType.DMA((n_fwd + ahead,))],
         cost_estimate=cost(8 * rows * width * (n_fwd + ahead)),
+        compiler_params=vmem(8),
         name="pack_z",
     )(own, *swapped)
 
@@ -184,6 +190,7 @@
         in_specs=[SMEM, SMEM],
         out_specs=[VMEM, VMEM, SMEM],
         cost_estimate=cost(2 * (key_rows + query_rows) * lanes),
+        compiler_params=vmem(8),
         name="lookup_tables",
     )(lengths, mask)
 
@@ -320,8 +327,8 @@
     return pl.pallas_call(
         kernel,
         out_shape=[jax.ShapeDtypeStruct((rows, width), bf)] * LEVEL,
-        in_specs=[SMEM] + [HBM] * (2 * LEVEL + 6),
-        out_specs=[HBM] * LEVEL,
+        in_specs=[SMEM] + [ANY] * (2 * LEVEL + 6),
+        out_specs=[ANY] * LEVEL,
         scratch_shapes=[
             pltpu.VMEM((key_rows, width), bf),
             pltpu.VMEM((key_rows, width), bf),
@@ -334,6 +341,7 @@
             pltpu.SemaphoreType.DMA((LEVEL,)),
         ],
         cost_estimate=cost(4 * key_rows * width, 8 * LEVEL * rows * 1024 * width),
+        compiler_params=vmem(24),
         name="attention",
     )(ranges, bias, onehot, queries, own, *swapped, *q_swapped, *own_far, *far)
 
@@ -354,10 +362,11 @@
     return pl.pallas_call(
         kernel,
         out_shape=jax.ShapeDtypeStruct((rows, LEVEL * slab), dtype),
-        in_specs=[HBM] * len(pieces),
+        in_specs=[ANY] * len(pieces),
         out_specs=VMEM,
         scratch_shapes=[pltpu.SemaphoreType.DMA((len(pieces),))],
         cost_estimate=cost(4 * rows * LEVEL * slab),
+        compiler_params=vmem(8),
         name="gather_out",
     )(*pieces)
 
@@ -382,10 +391,11 @@
     messages += [spans((0, 1), g) + spans((2,), g - 1) for g in groups[1:]]
     messages += [spans((2,), groups[-1])]
     own_spans = [span for g in groups for span in spans((0, 1), g)]
-    jobs = [(d, messages[0]) for d in OTHERS] + [(0, own_spans)]
-    *parts, own = pack_columns(arrays, jobs)
+    (own,) = pack_columns(arrays[:2], [(0, own_spans)], 60)
+    jobs = [(d, messages[0]) for d in OTHERS]
+    parts = pack_columns(arrays[:2], jobs, 60)
     jobs = [(d, message) for message in messages[1:] for d in OTHERS]
-    parts += pack_columns(arrays, jobs)
+    parts += pack_columns(arrays, jobs, 12)
     swapped, far = [], []
     for m in range(len(messages)):
         mine = parts[m * len(OTHERS) : (m + 1) * len(OTHERS)]

time: 129 us -> 125 us (0.969)
  Pallas kernels: 44.7 us -> 33.6 us
  waiting for transfers between devices: 58.9 us -> 62.3 us
  local copies, waits for them, and re-layouts: 2.27 us -> 4.63 us
    pallas_call x3, Pallas kernels: 7.56 us -> 0.53 us  [pack_z(): pl.pallas_call(kernel, out_shape=[jax.ShapeDtypeStruct((n_fwd, rows, 2 *...]
    ppermute x8, waiting for transfers between devices: 15.9 us -> 19.6 us  [swap_levels(): return lax.ppermute(value, 'ctx', sorted(pairs.items()))]
    unnamed x50 -> x30, local copies, waits for them, and re-layouts: 2.27 us -> 4.63 us
    ppermute x21, starting transfers between devices: 11.2 us -> 13.5 us  [swap(): lax.ppermute(value, 'ctx', [(i, i ^ bits) for i in range(lax.axis_size('c...]
    pallas_call x3, Pallas kernels: 25.6 us -> 23.3 us  [attention(): pl.pallas_call(kernel, out_shape=[jax.ShapeDtypeStruct((rows, width), bf)...]
    ppermute x8, starting transfers between devices: 9.98 us -> 8.55 us  [swap_levels(): return lax.ppermute(value, 'ctx', sorted(pairs.items()))]
    pallas_call x2 -> x3, Pallas kernels: 6.37 us -> 6.21 us  [pack_columns(): pl.pallas_call(kernel, out_shape=[jax.ShapeDtypeStruct((rows, total), arr...]
  transfers between devices with their start and end apart: 29 -> 29, of which waited for: 14 -> 13; matrix products, arithmetic and copies ran while one was open for 0% -> 0% of each run, Pallas kernels for 31% -> 24%
where the time goes in v3:
time: 125 us; the launch traced here: 123 us
  waiting for transfers between devices  62.3 us (50%)
  Pallas kernels  33.6 us (27%)
  starting transfers between devices  22.1 us (18%)
  local copies, waits for them, and re-layouts  4.63 us (4%)
    ppermute x21, waiting for transfers between devices, swap(): lax.ppermute(value, 'ctx', [(i, i ^ bits) for i in range(lax.axis_size('c...  42.8 us
    pallas_call x3, Pallas kernels, attention(): pl.pallas_call(kernel, out_shape=[jax.ShapeDtypeStruct((rows, width), bf)...  23.3 us
    ppermute x8, waiting for transfers between devices, swap_levels(): return lax.ppermute(value, 'ctx', sorted(pairs.items()))  19.6 us
    ppermute x21, starting transfers between devices, swap(): lax.ppermute(value, 'ctx', [(i, i ^ bits) for i in range(lax.axis_size('c...  13.5 us
    ppermute x8, starting transfers between devices, swap_levels(): return lax.ppermute(value, 'ctx', sorted(pairs.items()))  8.55 us
    pallas_call x3, Pallas kernels, pack_columns(): pl.pallas_call(kernel, out_shape=[jax.ShapeDtypeStruct((rows, total), arr...  6.21 us
    unnamed x30, local copies, waits for them, and re-layouts  4.63 us
  transfers between devices with their start and end apart: 29, of which 13 were waited for; matrix products, arithmetic and copies ran while one was open for 0% of the time, Pallas kernels for 24%

profile of v3, /device:TPU:14, one launch (start us, length us, event | category | flops | bytes accessed | tf_op | source)
XLA Modules:
  0.0 123.1 jit_solution(5495202441293814460)
XLA Ops:
  0.0 2.3 %shard_map.56 = (bf16[256,512]{1,0:T(8,128)(2,1)}, bf16[256,512]{1,0:T(8,128)(2,1)}, bf16[256,512]{1,0:T(8,128)(2,1)}) custom-call(bf16[256,3072]{1,0:T(8,128)(2,1)} %refs_0_.5, bf16[256,3072]{1,0:T(8,128)(2,1)} %refs_1_.5), custom_call_target="tpu_custom_call" | custom-call | bytes 1572864 | tf_op jit(solution)/shard_map/pallas_call | solution.py:70
  2.4 1.4 %copy-done.4 = bf16[256,3072]{1,0:T(8,128)(2,1)S(1)} copy-done((bf16[256,3072]{1,0:T(8,128)(2,1)S(1)}, bf16[256,3072]{1,0:T(8,128)(2,1)}, u32[]{:S(2)}) %copy-start.4) | copy-done | bytes 1572888
  3.8 1.8 %shard_map.57 = (bf16[256,768]{1,0:T(8,128)(2,1)}, bf16[256,768]{1,0:T(8,128)(2,1)S(1)}, bf16[256,768]{1,0:T(8,128)(2,1)S(1)}, bf16[256,768]{1,0:T(8,128)(2,1)},...) custom-call(bf16[256,3072]{1,0:T(8,128)(2,1)S(1)} %copy-done.3, ...), custom_call_target="tpu_custom_call" | custom-call | bytes 5505024 | tf_op jit(solution)/shard_map/pallas_call | solution.py:70
  5.6 0.7 copy-done.9
  6.4 0.7 copy-done.12
  7.0 0.5 collective-permute-start.21
  7.5 0.5 collective-permute-start.22
  8.0 1.5 %collective-permute-start.1 = (bf16[256,512]{1,0:T(8,128)(2,1)S(1)}, bf16[256,512]{1,0:T(8,128)(2,1)S(1)}, u32[]{:S(2)}, u32[]{:S(2)}) collective-permute-start(bf16[256,512]{1,0:T(8,128)(2,1)S(1)} %copy-done.14), channel_id=1, source_target_pairs={{0,2},{1,3},{2,0},{3,1},{4,6},{5,7},{6,4},{7,5},{8,10},{9,11},{10,... | collective-permute-start | bytes 786440 | tf_op jit(solution)/shard_map/ppermute | solution.py:26
  9.5 0.6 collective-permute-start.13
  10.2 3.7 %collective-permute-done.22.rest_5_ = bf16[256,256]{1,0:T(8,128)(2,1)S(1)} collective-permute-done((bf16[256,256]{1,0:T(8,128)(2,1)S(1)}, bf16[256,256]{1,0:T(8,128)(2,1)S(1)}, u32[]{:S(2)}, u32[]{:S(2)}) %collective-permute-start.22) | collective-permute-done | bytes 131104 | tf_op jit(solution)/shard_map/ppermute | solution.py:26
  13.9 0.6 copy-done.5
  14.5 0.5 collective-permute-start.14
  15.0 4.5 %collective-permute-done.1.rest_1_.rest_2_ = bf16[256,512]{1,0:T(8,128)(2,1)S(1)} collective-permute-done((bf16[256,512]{1,0:T(8,128)(2,1)S(1)}, bf16[256,512]{1,0:T(8,128)(2,1)S(1)}, u32[]{:S(2)}, u32[]{:S(2)}) %collective-permute-start.1) | collective-permute-done | bytes 262176 | tf_op jit(solution)/shard_map/ppermute | solution.py:26
  19.5 2.1 %shard_map.55.o.rest_0_ = bf16[256,1536]{1,0:T(8,128)(2,1)} custom-call(bf16[256,3072]{1,0:T(8,128)(2,1)} %refs_0_.5, bf16[256,3072]{1,0:T(8,128)(2,1)} %refs_1_.5), custom_call_target="tpu_custom_call" | custom-call | bytes 1572864 | tf_op jit(solution)/shard_map/pallas_call | solution.py:70
  21.6 1.6 %collective-permute-done.2.rest_2_.rest_3_ = bf16[256,512]{1,0:T(8,128)(2,1)S(1)} collective-permute-done((bf16[256,512]{1,0:T(8,128)(2,1)}, bf16[256,512]{1,0:T(8,128)(2,1)S(1)}, u32[]{:S(2)}, u32[]{:S(2)}) %collective-permute-start.2) | collective-permute-done | bytes 262176 | tf_op jit(solution)/shard_map/ppermute | solution.py:26
  23.2 0.4 collective-permute-start.6
  23.7 1.5 %collective-permute-start.4 = (bf16[256,768]{1,0:T(8,128)(2,1)}, bf16[256,768]{1,0:T(8,128)(2,1)S(1)}, u32[]{:S(2)}, u32[]{:S(2)}) collective-permute-start(bf16[256,768]{1,0:T(8,128)(2,1)} %copy-done.11), channel_id=1, source_target_pairs={{0,2},{1,3},{2,0},{3,1},{4,6},{5,7},{6,4},{7,5},{8,10},{9,11},{10,... | collective-permute-start | bytes 1179656 | tf_op jit(solution)/shard_map/ppermute | solution.py:26
  25.2 1.1 copy-done
  26.5 7.0 %collective-permute-done.14.rest_5_.rest_1_.rest_2_ = bf16[256,768]{1,0:T(8,128)(2,1)S(1)} collective-permute-done((bf16[256,768]{1,0:T(8,128)(2,1)}, bf16[256,768]{1,0:T(8,128)(2,1)S(1)}, u32[]{:S(2)}, u32[]{:S(2)}) %collective-permute-start.14) | collective-permute-done | bytes 393248 | tf_op jit(solution)/shard_map/ppermute | solution.py:26
  33.5 1.6 %collective-permute-start.7 = (bf16[256,1536]{1,0:T(8,128)(2,1)S(1)}, bf16[256,1536]{1,0:T(8,128)(2,1)S(1)}, u32[]{:S(2)}, u32[]{:S(2)}) collective-permute-start(bf16[256,1536]{1,0:T(8,128)(2,1)S(1)} %copy-done), channel_id=1, source_target_pairs={{0,1},{1,0},{2,3},{3,2},{4,8},{5,9},{6,10},{7,11},{8,4},{9,5},{10,... | collective-permute-start | bytes 2359304 | tf_op jit(solution)/shard_map/ppermute | solution.py:35
  35.1 5.0 %collective-permute-done.15.rest_6_.rest_2_.rest_3_ = bf16[256,768]{1,0:T(8,128)(2,1)S(1)} collective-permute-done((bf16[256,768]{1,0:T(8,128)(2,1)}, bf16[256,768]{1,0:T(8,128)(2,1)S(1)}, u32[]{:S(2)}, u32[]{:S(2)}) %collective-permute-start.15) | collective-permute-done | bytes 393248 | tf_op jit(solution)/shard_map/ppermute | solution.py:26
  40.1 0.4 collective-permute-start.8
  40.5 1.8 %collective-permute-start.5 = (bf16[256,768]{1,0:T(8,128)(2,1)S(1)}, bf16[256,768]{1,0:T(8,128)(2,1)S(1)}, u32[]{:S(2)}, u32[]{:S(2)}) collective-permute-start(bf16[256,768]{1,0:T(8,128)(2,1)S(1)} %copy-done.10), channel_id=1, source_target_pairs={{0,3},{1,2},{2,1},{3,0},{4,7},{5,6},{6,5},{7,4},{8,11},{9,10},{10,... | collective-permute-start | bytes 1179656 | tf_op jit(solution)/shard_map/ppermute | solution.py:26
  42.4 8.0 %collective-permute-done.4.rest_5_.rest_1_.rest_2_ = bf16[256,768]{1,0:T(8,128)(2,1)S(1)} collective-permute-done((bf16[256,768]{1,0:T(8,128)(2,1)}, bf16[256,768]{1,0:T(8,128)(2,1)S(1)}, u32[]{:S(2)}, u32[]{:S(2)}) %collective-permute-start.4) | collective-permute-done | bytes 393248 | tf_op jit(solution)/shard_map/ppermute | solution.py:26
  50.4 1.6 %collective-permute-start.9 = (bf16[3,256,512]{2,1,0:T(8,128)(2,1)S(1)}, bf16[3,256,512]{2,1,0:T(8,128)(2,1)S(1)}, u32[]{:S(2)}, u32[]{:S(2)}) collective-permute-start(bf16[3,256,512]{2,1,0:T(8,128)(2,1)S(1)} %get-tuple-element.48), channel_id=1, source_target_pairs={{0,1},{1,0},{2,3},{3,2},{4,8},{5,9},{6,10},{7,11},{8,4},{9,5},{10,... | collective-permute-start | bytes 2359304 | tf_op jit(solution)/shard_map/ppermute | solution.py:35
  52.0 0.2 pack_z.5
  52.2 4.7 %collective-permute-done.5.rest_6_.rest_2_.rest_3_ = bf16[256,768]{1,0:T(8,128)(2,1)S(1)} collective-permute-done((bf16[256,768]{1,0:T(8,128)(2,1)S(1)}, bf16[256,768]{1,0:T(8,128)(2,1)S(1)}, u32[]{:S(2)}, u32[]{:S(2)}) %collective-permute-start.5) | collective-permute-done | bytes 393248 | tf_op jit(solution)/shard_map/ppermute | solution.py:26
  56.9 0.4 collective-permute-start.24
  57.4 2.7 %collective-permute-start.25 = (bf16[3,256,512]{2,1,0:T(8,128)(2,1)S(1)}, bf16[3,256,512]{2,1,0:T(8,128)(2,1)S(1)}, u32[]{:S(2)}, u32[]{:S(2)}) collective-permute-start(bf16[3,256,512]{2,1,0:T(8,128)(2,1)S(1)} %get-tuple-element.66), channel_id=1, source_target_pairs={{0,1},{1,0},{2,3},{3,2},{4,8},{5,9},{6,10},{7,11},{8,4},{9,5},{10,... | collective-permute-start | bytes 2359304 | tf_op jit(solution)/shard_map/ppermute | solution.py:35
  60.4 1.2 collective-permute-start.17
  61.6 2.1 %lookup_tables.1 = (bf16[2560,128]{1,0:T(8,128)(2,1)S(1)}, bf16[1024,128]{1,0:T(8,128)(2,1)S(1)}, s32[5,2]{1,0:T(8,128)S(1)}) custom-call(s32[16]{0:T(128)S(1)} %copy-done.8, s32[16,16]{1,0:T(8,128)S(1)} %copy-done.7), custom_call_target="tpu_custom_call" | custom-call | bytes 917504 | tf_op jit(solution)/shard_map/lookup_tables/pallas_call | solution.py:183
  63.7 7.2 %collective-permute-done.9.rest_10_ = bf16[3,256,512]{2,1,0:T(8,128)(2,1)S(1)} collective-permute-done((bf16[3,256,512]{2,1,0:T(8,128)(2,1)S(1)}, bf16[3,256,512]{2,1,0:T(8,128)(2,1)S(1)}, u32[]{:S(2)}, u32[]{:S(2)}) %collective-permute-start.9) | collective-permute-done | bytes 786464 | tf_op jit(solution)/shard_map/ppermute | solution.py:35
  70.9 7.5 %attention.3 = (bf16[256,256]{1,0:T(8,128)(2,1)S(1)}, bf16[256,256]{1,0:T(8,128)(2,1)S(1)}, bf16[256,256]{1,0:T(8,128)(2,1)S(1)}, bf16[256,256]{1,0:T(8,128)(2,1)S(1)}) custom-call(s32[5,2]{1,0:T(8,128)S(1)} %get-tuple-element.38.ranges, bf16[2560,128]{1,0:T(8,128)(2,1)S(1)} %get-tuple-element.39.bias_hbm, ...), custom_call_target="tpu_custom_call" | custom-call | flops 2147483648 | bytes 2621440 | tf_op jit(solution)/shard_map/attention/pallas_call | solution.py:327
  78.4 0.6 collective-permute-start.10
  79.0 1.5 %collective-permute-start.11 = (bf16[256,256]{1,0:T(8,128)(2,1)S(1)}, bf16[256,256]{1,0:T(8,128)(2,1)S(1)}, u32[]{:S(2)}, u32[]{:S(2)}) collective-permute-start(bf16[256,256]{1,0:T(8,128)(2,1)S(1)} %get-tuple-element.51), channel_id=1, source_target_pairs={{0,2},{1,3},{2,0},{3,1},{4,6},{5,7},{6,4},{7,5},{8,10},{9,11},{10,... | collective-permute-start | bytes 393224 | tf_op jit(solution)/shard_map/ppermute | solution.py:26
  80.6 7.2 %collective-permute-done.25.rest_10_ = bf16[3,256,512]{2,1,0:T(8,128)(2,1)S(1)} collective-permute-done((bf16[3,256,512]{2,1,0:T(8,128)(2,1)S(1)}, bf16[3,256,512]{2,1,0:T(8,128)(2,1)S(1)}, u32[]{:S(2)}, u32[]{:S(2)}) %collective-permute-start.25) | collective-permute-done | bytes 786464 | tf_op jit(solution)/shard_map/ppermute | solution.py:35
  87.7 8.2 %attention.5 = (bf16[256,256]{1,0:T(8,128)(2,1)S(1)}, bf16[256,256]{1,0:T(8,128)(2,1)S(1)}, bf16[256,256]{1,0:T(8,128)(2,1)S(1)}, bf16[256,256]{1,0:T(8,128)(2,1)S(1)}) custom-call(s32[5,2]{1,0:T(8,128)S(1)} %get-tuple-element.38.ranges, bf16[2560,128]{1,0:T(8,128)(2,1)S(1)} %get-tuple-element.39.bias_hbm, ...), custom_call_target="tpu_custom_call" | custom-call | flops 2147483648 | bytes 2621440 | tf_op jit(solution)/shard_map/attention/pallas_call | solution.py:327
  95.9 0.7 collective-permute-start.26
  96.6 5.2 %collective-permute-done.17.rest_10_ = bf16[3,256,512]{2,1,0:T(8,128)(2,1)S(1)} collective-permute-done((bf16[3,256,512]{2,1,0:T(8,128)(2,1)S(1)}, bf16[3,256,512]{2,1,0:T(8,128)(2,1)S(1)}, u32[]{:S(2)}, u32[]{:S(2)}) %collective-permute-start.17) | collective-permute-done | bytes 786464 | tf_op jit(solution)/shard_map/ppermute | solution.py:35
  101.8 0.5 collective-permute-start.27
  102.4 7.7 %attention.4 = (bf16[256,256]{1,0:T(8,128)(2,1)S(1)}, bf16[256,256]{1,0:T(8,128)(2,1)S(1)}, bf16[256,256]{1,0:T(8,128)(2,1)S(1)}, bf16[256,256]{1,0:T(8,128)(2,1)S(1)}) custom-call(s32[5,2]{1,0:T(8,128)S(1)} %get-tuple-element.38.ranges, bf16[2560,128]{1,0:T(8,128)(2,1)S(1)} %get-tuple-element.39.bias_hbm, ...), custom_call_target="tpu_custom_call" | custom-call | flops 2147483648 | bytes 2621440 | tf_op jit(solution)/shard_map/attention/pallas_call | solution.py:327
  110.1 1.6 %collective-permute-start.18 = (bf16[256,256]{1,0:T(8,128)(2,1)S(1)}, bf16[256,256]{1,0:T(8,128)(2,1)S(1)}, u32[]{:S(2)}, u32[]{:S(2)}) collective-permute-start(bf16[256,256]{1,0:T(8,128)(2,1)S(1)} %get-tuple-element.59), channel_id=1, source_target_pairs={{0,1},{1,0},{2,3},{3,2},{4,5},{5,4},{6,7},{7,6},{8,9},{9,8},{10,11... | collective-permute-start | bytes 393224 | tf_op jit(solution)/shard_map/ppermute | solution.py:26
  111.8 0.5 collective-permute-start.19
  112.3 0.9 collective-permute-start.20
  113.2 2.6 %collective-permute-done.28.refs_11_ = bf16[256,256]{1,0:T(8,128)(2,1)S(1)} collective-permute-done((bf16[256,256]{1,0:T(8,128)(2,1)S(1)}, bf16[256,256]{1,0:T(8,128)(2,1)S(1)}, u32[]{:S(2)}, u32[]{:S(2)}) %collective-permute-start.28) | collective-permute-done | bytes 131104 | tf_op jit(solution)/shard_map/ppermute | solution.py:26
  115.8 3.0 %collective-permute-done.19.refs_6_ = bf16[256,256]{1,0:T(8,128)(2,1)S(1)} collective-permute-done((bf16[256,256]{1,0:T(8,128)(2,1)S(1)}, bf16[256,256]{1,0:T(8,128)(2,1)S(1)}, u32[]{:S(2)}, u32[]{:S(2)}) %collective-permute-start.19) | collective-permute-done | bytes 131104 | tf_op jit(solution)/shard_map/ppermute | solution.py:26
  118.8 2.6 %collective-permute-done.20.refs_7_ = bf16[256,256]{1,0:T(8,128)(2,1)S(1)} collective-permute-done((bf16[256,256]{1,0:T(8,128)(2,1)S(1)}, bf16[256,256]{1,0:T(8,128)(2,1)S(1)}, u32[]{:S(2)}, u32[]{:S(2)}) %collective-permute-start.20) | collective-permute-done | bytes 131104 | tf_op jit(solution)/shard_map/ppermute | solution.py:26
  121.4 1.5 %gather_out.1 = bf16[256,3072]{1,0:T(8,128)(2,1)} custom-call(bf16[256,256]{1,0:T(8,128)(2,1)S(1)} %get-tuple-element.49.refs_0_, bf16[256,256]{1,0:T(8,128)(2,1)S(1)} %collective-permute-done.10.refs_1_, bf16[256,256]{1,0:T(8,128)(2,1)S(1)} %collective-permute-done.11.refs_2_, bf16[256,256]{1,0:T(8,128)(2,1)S(1)} %collective-permute-done.12.refs_3_, ...), custom_call_target="tpu_custom_call" | custom-call | bytes 3145728 | tf_op jit(solution)/shard_map/gather_out/pallas_call | solution.py:362
  (51 shorter events, 0.7 us)
Async XLA Ops:
  0.0 2.4 %copy-start.3 = (bf16[256,3072]{1,0:T(8,128)(2,1)S(1)}, bf16[256,3072]{1,0:T(8,128)(2,1)}, u32[]{:S(2)}) copy-start(bf16[256,3072]{1,0:T(8,128)(2,1)} %refs_0_.5) | copy-start | bytes 4718596
  0.0 2.4 %copy-start.2 = (bf16[256,3072]{1,0:T(8,128)(2,1)S(1)}, bf16[256,3072]{1,0:T(8,128)(2,1)}, u32[]{:S(2)}) copy-start(bf16[256,3072]{1,0:T(8,128)(2,1)} %q.5) | copy-start | bytes 4718596
  2.3 12.7 %collective-permute-start = (bf16[256,512]{1,0:T(8,128)(2,1)}, bf16[256,512]{1,0:T(8,128)(2,1)S(1)}, u32[]{:S(2)}, u32[]{:S(2)}) collective-permute-start(bf16[256,512]{1,0:T(8,128)(2,1)} %get-tuple-element.41), channel_id=1, source_target_pairs={{0,1},{1,0},{2,3},{3,2},{4,5},{5,4},{6,7},{7,6},{8,9},{9,8},{10,11... | collective-permute-start | bytes 786440 | tf_op jit(solution)/shard_map/ppermute | solution.py:26
  2.4 1.4 %copy-start.4 = (bf16[256,3072]{1,0:T(8,128)(2,1)S(1)}, bf16[256,3072]{1,0:T(8,128)(2,1)}, u32[]{:S(2)}) copy-start(bf16[256,3072]{1,0:T(8,128)(2,1)} %refs_1_.5) | copy-start | bytes 4718596
  3.8 4.2 %copy-start.14 = (bf16[256,512]{1,0:T(8,128)(2,1)S(1)}, bf16[256,512]{1,0:T(8,128)(2,1)}, u32[]{:S(2)}) copy-start(bf16[256,512]{1,0:T(8,128)(2,1)} %get-tuple-element.42) | copy-start | bytes 786436
  5.6 0.8 copy-start.9
  6.4 0.7 copy-start.12
  7.0 12.5 %copy-start.11 = (bf16[256,768]{1,0:T(8,128)(2,1)}, bf16[256,768]{1,0:T(8,128)(2,1)S(1)}, u32[]{:S(2)}) copy-start(bf16[256,768]{1,0:T(8,128)(2,1)S(1)} %get-tuple-element.45) | copy-start | bytes 1179652
  7.0 2.5 %collective-permute-start.21 = (bf16[256,256]{1,0:T(8,128)(2,1)S(1)}, bf16[256,256]{1,0:T(8,128)(2,1)S(1)}, u32[]{:S(2)}, u32[]{:S(2)}) collective-permute-start(bf16[256,256]{1,0:T(8,128)(2,1)S(1)} %get-tuple-element.62), channel_id=1, source_target_pairs={{0,1},{1,0},{2,3},{3,2},{4,5},{5,4},{6,7},{7,6},{8,9},{9,8},{10,11... | collective-permute-start | bytes 393224 | tf_op jit(solution)/shard_map/ppermute | solution.py:26
  7.5 6.4 %collective-permute-start.22 = (bf16[256,256]{1,0:T(8,128)(2,1)S(1)}, bf16[256,256]{1,0:T(8,128)(2,1)S(1)}, u32[]{:S(2)}, u32[]{:S(2)}) collective-permute-start(bf16[256,256]{1,0:T(8,128)(2,1)S(1)} %get-tuple-element.63), channel_id=1, source_target_pairs={{0,2},{1,3},{2,0},{3,1},{4,6},{5,7},{6,4},{7,5},{8,10},{9,11},{10,... | collective-permute-start | bytes 393224 | tf_op jit(solution)/shard_map/ppermute | solution.py:26
  8.0 11.5 %collective-permute-start.1 = (bf16[256,512]{1,0:T(8,128)(2,1)S(1)}, bf16[256,512]{1,0:T(8,128)(2,1)S(1)}, u32[]{:S(2)}, u32[]{:S(2)}) collective-permute-start(bf16[256,512]{1,0:T(8,128)(2,1)S(1)} %copy-done.14), channel_id=1, source_target_pairs={{0,2},{1,3},{2,0},{3,1},{4,6},{5,7},{6,4},{7,5},{8,10},{9,11},{10,... | collective-permute-start | bytes 786440 | tf_op jit(solution)/shard_map/ppermute | solution.py:26
  9.5 13.7 %collective-permute-start.2 = (bf16[256,512]{1,0:T(8,128)(2,1)}, bf16[256,512]{1,0:T(8,128)(2,1)S(1)}, u32[]{:S(2)}, u32[]{:S(2)}) collective-permute-start(bf16[256,512]{1,0:T(8,128)(2,1)} %get-tuple-element.43), channel_id=1, source_target_pairs={{0,3},{1,2},{2,1},{3,0},{4,7},{5,6},{6,5},{7,4},{8,11},{9,10},{10,... | collective-permute-start | bytes 786440 | tf_op jit(solution)/shard_map/ppermute | solution.py:26
  9.5 14.2 %collective-permute-start.13 = (bf16[256,768]{1,0:T(8,128)(2,1)}, bf16[256,768]{1,0:T(8,128)(2,1)S(1)}, u32[]{:S(2)}, u32[]{:S(2)}) collective-permute-start(bf16[256,768]{1,0:T(8,128)(2,1)} %get-tuple-element.53), channel_id=1, source_target_pairs={{0,1},{1,0},{2,3},{3,2},{4,5},{5,4},{6,7},{7,6},{8,9},{9,8},{10,11... | collective-permute-start | bytes 1179656 | tf_op jit(solution)/shard_map/ppermute | solution.py:26
  13.9 0.6 copy-start.5
  14.5 19.0 %collective-permute-start.14 = (bf16[256,768]{1,0:T(8,128)(2,1)}, bf16[256,768]{1,0:T(8,128)(2,1)S(1)}, u32[]{:S(2)}, u32[]{:S(2)}) collective-permute-start(bf16[256,768]{1,0:T(8,128)(2,1)} %get-tuple-element.54), channel_id=1, source_target_pairs={{0,2},{1,3},{2,0},{3,1},{4,6},{5,7},{6,4},{7,5},{8,10},{9,11},{10,... | collective-permute-start | bytes 1179656 | tf_op jit(solution)/shard_map/ppermute | solution.py:26
  15.0 25.1 %collective-permute-start.15 = (bf16[256,768]{1,0:T(8,128)(2,1)}, bf16[256,768]{1,0:T(8,128)(2,1)S(1)}, u32[]{:S(2)}, u32[]{:S(2)}) collective-permute-start(bf16[256,768]{1,0:T(8,128)(2,1)} %get-tuple-element.55), channel_id=1, source_target_pairs={{0,3},{1,2},{2,1},{3,0},{4,7},{5,6},{6,5},{7,4},{8,11},{9,10},{10,... | collective-permute-start | bytes 1179656 | tf_op jit(solution)/shard_map/ppermute | solution.py:26
  19.5 21.1 %collective-permute-start.3 = (bf16[256,768]{1,0:T(8,128)(2,1)}, bf16[256,768]{1,0:T(8,128)(2,1)S(1)}, u32[]{:S(2)}, u32[]{:S(2)}) collective-permute-start(bf16[256,768]{1,0:T(8,128)(2,1)} %get-tuple-element.44), channel_id=1, source_target_pairs={{0,1},{1,0},{2,3},{3,2},{4,5},{5,4},{6,7},{7,6},{8,9},{9,8},{10,11... | collective-permute-start | bytes 1179656 | tf_op jit(solution)/shard_map/ppermute | solution.py:26
  23.2 34.1 %collective-permute-start.6 = (bf16[256,1536]{1,0:T(8,128)(2,1)}, bf16[256,1536]{1,0:T(8,128)(2,1)S(1)}, u32[]{:S(2)}, u32[]{:S(2)}) collective-permute-start(bf16[256,1536]{1,0:T(8,128)(2,1)} %shard_map.55.o.rest_0_), channel_id=1, source_target_pairs={{0,4},{1,5},{2,6},{3,7},{4,0},{5,1},{6,2},{7,3},{8,12},{9,13},{10,... | collective-permute-start | bytes 2359304 | tf_op jit(solution)/shard_map/ppermute | solution.py:35
  23.7 26.7 %collective-permute-start.4 = (bf16[256,768]{1,0:T(8,128)(2,1)}, bf16[256,768]{1,0:T(8,128)(2,1)S(1)}, u32[]{:S(2)}, u32[]{:S(2)}) collective-permute-start(bf16[256,768]{1,0:T(8,128)(2,1)} %copy-done.11), channel_id=1, source_target_pairs={{0,2},{1,3},{2,0},{3,1},{4,6},{5,7},{6,4},{7,5},{8,10},{9,11},{10,... | collective-permute-start | bytes 1179656 | tf_op jit(solution)/shard_map/ppermute | solution.py:26
  25.2 1.1 copy-start
  26.3 14.2 %copy-start.10 = (bf16[256,768]{1,0:T(8,128)(2,1)S(1)}, bf16[256,768]{1,0:T(8,128)(2,1)}, u32[]{:S(2)}) copy-start(bf16[256,768]{1,0:T(8,128)(2,1)} %copy-done.9) | copy-start | bytes 1179652
  33.5 26.7 %collective-permute-start.7 = (bf16[256,1536]{1,0:T(8,128)(2,1)S(1)}, bf16[256,1536]{1,0:T(8,128)(2,1)S(1)}, u32[]{:S(2)}, u32[]{:S(2)}) collective-permute-start(bf16[256,1536]{1,0:T(8,128)(2,1)S(1)} %copy-done), channel_id=1, source_target_pairs={{0,1},{1,0},{2,3},{3,2},{4,8},{5,9},{6,10},{7,11},{8,4},{9,5},{10,... | collective-permute-start | bytes 2359304 | tf_op jit(solution)/shard_map/ppermute | solution.py:35
  40.1 20.3 %collective-permute-start.8 = (bf16[3,256,512]{2,1,0:T(8,128)(2,1)S(1)}, bf16[3,256,512]{2,1,0:T(8,128)(2,1)S(1)}, u32[]{:S(2)}, u32[]{:S(2)}) collective-permute-start(bf16[3,256,512]{2,1,0:T(8,128)(2,1)S(1)} %get-tuple-element.47), channel_id=1, source_target_pairs={{0,4},{1,5},{2,6},{3,7},{4,0},{5,1},{6,2},{7,3},{8,12},{9,13},{10,... | collective-permute-start | bytes 2359304 | tf_op jit(solution)/shard_map/ppermute | solution.py:35
  40.5 16.4 %collective-permute-start.5 = (bf16[256,768]{1,0:T(8,128)(2,1)S(1)}, bf16[256,768]{1,0:T(8,128)(2,1)S(1)}, u32[]{:S(2)}, u32[]{:S(2)}) collective-permute-start(bf16[256,768]{1,0:T(8,128)(2,1)S(1)} %copy-done.10), channel_id=1, source_target_pairs={{0,3},{1,2},{2,1},{3,0},{4,7},{5,6},{6,5},{7,4},{8,11},{9,10},{10,... | collective-permute-start | bytes 1179656 | tf_op jit(solution)/shard_map/ppermute | solution.py:26
  50.4 11.2 %copy-start.7 = (s32[16,16]{1,0:T(8,128)S(1)}, s32[16,16]{1,0:T(8,128)}, u32[]{:S(2)}) copy-start(s32[16,16]{1,0:T(8,128)} %mask_ref.1) | copy-start | bytes 3076
  50.4 11.2 %copy-start.8 = (s32[16]{0:T(128)S(1)}, s32[16]{0:T(128)}, u32[]{:S(2)}) copy-start(s32[16]{0:T(128)} %len_ref.1) | copy-start | bytes 196
  50.4 20.5 %copy-start.13 = (bf16[256,256]{1,0:T(8,128)(2,1)S(1)}, bf16[256,256]{1,0:T(8,128)(2,1)}, u32[]{:S(2)}) copy-start(bf16[256,256]{1,0:T(8,128)(2,1)} %copy-done.12) | copy-start | bytes 393220
  50.4 20.5 %copy-start.1 = (bf16[256,1536]{1,0:T(8,128)(2,1)S(1)}, bf16[256,1536]{1,0:T(8,128)(2,1)}, u32[]{:S(2)}) copy-start(bf16[256,1536]{1,0:T(8,128)(2,1)} %shard_map.55.o.rest_0_) | copy-start | bytes 2359300
  50.4 20.5 %collective-permute-start.9 = (bf16[3,256,512]{2,1,0:T(8,128)(2,1)S(1)}, bf16[3,256,512]{2,1,0:T(8,128)(2,1)S(1)}, u32[]{:S(2)}, u32[]{:S(2)}) collective-permute-start(bf16[3,256,512]{2,1,0:T(8,128)(2,1)S(1)} %get-tuple-element.48), channel_id=1, source_target_pairs={{0,1},{1,0},{2,3},{3,2},{4,8},{5,9},{6,10},{7,11},{8,4},{9,5},{10,... | collective-permute-start | bytes 2359304 | tf_op jit(solution)/shard_map/ppermute | solution.py:35
  56.9 22.1 %collective-permute-start.24 = (bf16[3,256,512]{2,1,0:T(8,128)(2,1)S(1)}, bf16[3,256,512]{2,1,0:T(8,128)(2,1)S(1)}, u32[]{:S(2)}, u32[]{:S(2)}) collective-permute-start(bf16[3,256,512]{2,1,0:T(8,128)(2,1)S(1)} %get-tuple-element.65), channel_id=1, source_target_pairs={{0,4},{1,5},{2,6},{3,7},{4,0},{5,1},{6,2},{7,3},{8,12},{9,13},{10,... | collective-permute-start | bytes 2359304 | tf_op jit(solution)/shard_map/ppermute | solution.py:35
  57.4 30.3 %collective-permute-start.25 = (bf16[3,256,512]{2,1,0:T(8,128)(2,1)S(1)}, bf16[3,256,512]{2,1,0:T(8,128)(2,1)S(1)}, u32[]{:S(2)}, u32[]{:S(2)}) collective-permute-start(bf16[3,256,512]{2,1,0:T(8,128)(2,1)S(1)} %get-tuple-element.66), channel_id=1, source_target_pairs={{0,1},{1,0},{2,3},{3,2},{4,8},{5,9},{6,10},{7,11},{8,4},{9,5},{10,... | collective-permute-start | bytes 2359304 | tf_op jit(solution)/shard_map/ppermute | solution.py:35
  60.3 35.7 %collective-permute-start.16 = (bf16[3,256,512]{2,1,0:T(8,128)(2,1)S(1)}, bf16[3,256,512]{2,1,0:T(8,128)(2,1)S(1)}, u32[]{:S(2)}, u32[]{:S(2)}) collective-permute-start(bf16[3,256,512]{2,1,0:T(8,128)(2,1)S(1)} %get-tuple-element.56), channel_id=1, source_target_pairs={{0,4},{1,5},{2,6},{3,7},{4,0},{5,1},{6,2},{7,3},{8,12},{9,13},{10,... | collective-permute-start | bytes 2359304 | tf_op jit(solution)/shard_map/ppermute | solution.py:35
  60.4 41.5 %collective-permute-start.17 = (bf16[3,256,512]{2,1,0:T(8,128)(2,1)S(1)}, bf16[3,256,512]{2,1,0:T(8,128)(2,1)S(1)}, u32[]{:S(2)}, u32[]{:S(2)}) collective-permute-start(bf16[3,256,512]{2,1,0:T(8,128)(2,1)S(1)} %get-tuple-element.57), channel_id=1, source_target_pairs={{0,1},{1,0},{2,3},{3,2},{4,8},{5,9},{6,10},{7,11},{8,4},{9,5},{10,... | collective-permute-start | bytes 2359304 | tf_op jit(solution)/shard_map/ppermute | solution.py:35
  70.9 7.5 %collective-permute-start.23 = (bf16[256,256]{1,0:T(8,128)(2,1)S(1)}, bf16[256,256]{1,0:T(8,128)(2,1)S(1)}, u32[]{:S(2)}, u32[]{:S(2)}) collective-permute-start(bf16[256,256]{1,0:T(8,128)(2,1)S(1)} %copy-done.13), channel_id=1, source_target_pairs={{0,3},{1,2},{2,1},{3,0},{4,7},{5,6},{6,5},{7,4},{8,11},{9,10},{10,... | collective-permute-start | bytes 393224 | tf_op jit(solution)/shard_map/ppermute | solution.py:26
  70.9 16.8 %copy-start.6 = (bf16[256,256]{1,0:T(8,128)(2,1)S(1)}, bf16[256,256]{1,0:T(8,128)(2,1)}, u32[]{:S(2)}) copy-start(bf16[256,256]{1,0:T(8,128)(2,1)} %copy-done.5) | copy-start | bytes 393220
  78.4 31.7 %collective-permute-start.10 = (bf16[256,256]{1,0:T(8,128)(2,1)S(1)}, bf16[256,256]{1,0:T(8,128)(2,1)S(1)}, u32[]{:S(2)}, u32[]{:S(2)}) collective-permute-start(bf16[256,256]{1,0:T(8,128)(2,1)S(1)} %get-tuple-element.50), channel_id=1, source_target_pairs={{0,1},{1,0},{2,3},{3,2},{4,5},{5,4},{6,7},{7,6},{8,9},{9,8},{10,11... | collective-permute-start | bytes 393224 | tf_op jit(solution)/shard_map/ppermute | solution.py:26
  79.0 31.1 %collective-permute-start.11 = (bf16[256,256]{1,0:T(8,128)(2,1)S(1)}, bf16[256,256]{1,0:T(8,128)(2,1)S(1)}, u32[]{:S(2)}, u32[]{:S(2)}) collective-permute-start(bf16[256,256]{1,0:T(8,128)(2,1)S(1)} %get-tuple-element.51), channel_id=1, source_target_pairs={{0,2},{1,3},{2,0},{3,1},{4,6},{5,7},{6,4},{7,5},{8,10},{9,11},{10,... | collective-permute-start | bytes 393224 | tf_op jit(solution)/shard_map/ppermute | solution.py:26
  87.7 24.0 %collective-permute-start.12 = (bf16[256,256]{1,0:T(8,128)(2,1)S(1)}, bf16[256,256]{1,0:T(8,128)(2,1)S(1)}, u32[]{:S(2)}, u32[]{:S(2)}) collective-permute-start(bf16[256,256]{1,0:T(8,128)(2,1)S(1)} %get-tuple-element.52), channel_id=1, source_target_pairs={{0,3},{1,2},{2,1},{3,0},{4,7},{5,6},{6,5},{7,4},{8,11},{9,10},{10,... | collective-permute-start | bytes 393224 | tf_op jit(solution)/shard_map/ppermute | solution.py:26
  95.9 16.3 %collective-permute-start.26 = (bf16[256,256]{1,0:T(8,128)(2,1)S(1)}, bf16[256,256]{1,0:T(8,128)(2,1)S(1)}, u32[]{:S(2)}, u32[]{:S(2)}) collective-permute-start(bf16[256,256]{1,0:T(8,128)(2,1)S(1)} %get-tuple-element.68), channel_id=1, source_target_pairs={{0,1},{1,0},{2,3},{3,2},{4,5},{5,4},{6,7},{7,6},{8,9},{9,8},{10,11... | collective-permute-start | bytes 393224 | tf_op jit(solution)/shard_map/ppermute | solution.py:26
  101.8 11.3 %collective-permute-start.27 = (bf16[256,256]{1,0:T(8,128)(2,1)S(1)}, bf16[256,256]{1,0:T(8,128)(2,1)S(1)}, u32[]{:S(2)}, u32[]{:S(2)}) collective-permute-start(bf16[256,256]{1,0:T(8,128)(2,1)S(1)} %get-tuple-element.69), channel_id=1, source_target_pairs={{0,2},{1,3},{2,0},{3,1},{4,6},{5,7},{6,4},{7,5},{8,10},{9,11},{10,... | collective-permute-start | bytes 393224 | tf_op jit(solution)/shard_map/ppermute | solution.py:26
  110.0 5.8 %collective-permute-start.28 = (bf16[256,256]{1,0:T(8,128)(2,1)S(1)}, bf16[256,256]{1,0:T(8,128)(2,1)S(1)}, u32[]{:S(2)}, u32[]{:S(2)}) collective-permute-start(bf16[256,256]{1,0:T(8,128)(2,1)S(1)} %get-tuple-element.70), channel_id=1, source_target_pairs={{0,3},{1,2},{2,1},{3,0},{4,7},{5,6},{6,5},{7,4},{8,11},{9,10},{10,... | collective-permute-start | bytes 393224 | tf_op jit(solution)/shard_map/ppermute | solution.py:26
  110.1 5.7 %collective-permute-start.18 = (bf16[256,256]{1,0:T(8,128)(2,1)S(1)}, bf16[256,256]{1,0:T(8,128)(2,1)S(1)}, u32[]{:S(2)}, u32[]{:S(2)}) collective-permute-start(bf16[256,256]{1,0:T(8,128)(2,1)S(1)} %get-tuple-element.59), channel_id=1, source_target_pairs={{0,1},{1,0},{2,3},{3,2},{4,5},{5,4},{6,7},{7,6},{8,9},{9,8},{10,11... | collective-permute-start | bytes 393224 | tf_op jit(solution)/shard_map/ppermute | solution.py:26
  111.8 7.0 %collective-permute-start.19 = (bf16[256,256]{1,0:T(8,128)(2,1)S(1)}, bf16[256,256]{1,0:T(8,128)(2,1)S(1)}, u32[]{:S(2)}, u32[]{:S(2)}) collective-permute-start(bf16[256,256]{1,0:T(8,128)(2,1)S(1)} %get-tuple-element.60), channel_id=1, source_target_pairs={{0,2},{1,3},{2,0},{3,1},{4,6},{5,7},{6,4},{7,5},{8,10},{9,11},{10,... | collective-permute-start | bytes 393224 | tf_op jit(solution)/shard_map/ppermute | solution.py:26
  112.3 9.2 %collective-permute-start.20 = (bf16[256,256]{1,0:T(8,128)(2,1)S(1)}, bf16[256,256]{1,0:T(8,128)(2,1)S(1)}, u32[]{:S(2)}, u32[]{:S(2)}) collective-permute-start(bf16[256,256]{1,0:T(8,128)(2,1)S(1)} %get-tuple-element.61), channel_id=1, source_target_pairs={{0,3},{1,2},{2,1},{3,0},{4,7},{5,6},{6,5},{7,4},{8,11},{9,10},{10,... | collective-permute-start | bytes 393224 | tf_op jit(solution)/shard_map/ppermute | solution.py:26
